TPU v7x, 32 devices: a whole 2x2x4 slice. The times are simulated.
32 devices in a mesh: energy: 8 (over y, x, core), space: 4 (over z).
Axes of the slice: x: 2, y: 2, z: 4, core: 2. Of those that a mesh axis runs over, the one named last changes fastest.
Arguments:
- screening: bfloat16 [8, 8, 3, 2, 128, 128], P('energy', 'space'), may hold values from -0.21875 to 0.21875
- polarization: bfloat16 [8, 8, 3, 2, 128, 128], P('energy', 'space'), may hold values from -6 to 6
- propagator: bfloat16 [8, 8, 3, 2, 128, 128], P('energy', 'space'), may hold values from -0.21875 to 0.21875
Outputs:
- dressed: bfloat16 [8, 8, 3, 2, 128, 128], P('energy', 'space')
All inputs are finite; a program needn't handle non-finite values.
Results may differ from a plain program's by a relative error of at most 0.015.
Values may be sent and summed in bfloat16 or wider, within the bound.
No kernel may reach another device: no remote copies, remote signals or barrier semaphores. Data moves between devices by JAX's collectives and lax.ppermute only.
A program may use at most 64 MiB of HBM per device.

v0:
```python
import math

import jax
import jax.numpy as jnp
from jax import lax
from jax.sharding import PartitionSpec as P


def with_halo(x, sides, width):
    for axis, dim in sides:
        peers, length = (lax.axis_size(axis), x.shape[dim])
        up = [(i, (i + 1) % peers) for i in range(peers - 1)]
        down = [(j, i) for i, j in up]
        last = lax.slice_in_dim(x, length - width, length, axis=dim)
        leading = lax.slice_in_dim(x, 0, width, axis=dim)
        before = lax.ppermute(last, axis, up)
        after = lax.ppermute(leading, axis, down)
        x = jnp.concatenate([before, x, after], axis=dim)
    return x


def clip_edges(banded, first_row, row_total):
    row_count = banded.shape[1]
    row_index = first_row + jnp.arange(row_count, dtype=jnp.int32)
    band_index = jnp.arange(3, dtype=jnp.int32)
    dropped = (band_index[None, :] == 0) & (row_index[:, None] == 0) | (
        band_index[None, :] == 2
    ) & (row_index[:, None] == row_total - 1)
    keep_mask = jnp.where(dropped, 0.0, 1.0).astype(banded.dtype)
    return banded * keep_mask[None, :, :, None, None, None]


def complex_product(first, second, adjoint):
    first_real = first[:, :, 0]
    first_imag = first[:, :, 1]
    second_real = second[:, :, 0]
    second_imag = second[:, :, 1]
    if adjoint:
        form = "erij,erkj->erik"
    else:
        form = "erij,erjk->erik"

    def product(lhs, rhs):
        return jnp.einsum(form, lhs, rhs, preferred_element_type=jnp.float32)

    if adjoint:
        real_part = product(first_real, second_real) + product(first_imag, second_imag)
        imag_part = product(first_imag, second_real) - product(first_real, second_imag)
    else:
        real_part = product(first_real, second_real) - product(first_imag, second_imag)
        imag_part = product(first_real, second_imag) + product(first_imag, second_real)
    return jnp.stack([real_part, imag_part], axis=2)


def pick_rows(banded, start, row_count, band):
    return lax.slice_in_dim(banded, start, start + row_count, axis=1)[:, :, band]


def sandwich(outside, between):
    row_count = outside.shape[1] - 2
    products = {}
    for offset in range(-2, 3):
        summed = None
        for inner in range(-1, 2):
            if abs(offset - inner) <= 1:
                term = complex_product(
                    pick_rows(outside, 1, row_count, inner + 1),
                    pick_rows(between, 1 + inner, row_count, offset - inner + 1),
                    False,
                )
                summed = term if summed is None else summed + term
        products[offset] = summed.astype(jnp.bfloat16)
    bands = []
    for target in range(-1, 2):
        summed = None
        for offset in range(target - 1, target + 2):
            term = complex_product(
                products[offset],
                pick_rows(outside, 1 + target, row_count, offset - target + 1),
                True,
            )
            summed = term if summed is None else summed + term
        bands.append(summed)
    return jnp.stack(bands, axis=2)


def split_table(table):
    upper = table.astype(jnp.bfloat16)
    lower = (table - upper.astype(jnp.float32)).astype(jnp.bfloat16)
    return (upper, lower)


def plain_dot(lhs, rhs):
    return jnp.dot(lhs, rhs, preferred_element_type=jnp.float32)


def table_times_data(table_pair, data):
    return plain_dot(table_pair[0], data) + plain_dot(table_pair[1], data)


def table_times_float(table_pair, values):
    value_upper, value_lower = split_table(values)
    return (
        plain_dot(table_pair[0], value_upper)
        + plain_dot(table_pair[0], value_lower)
        + plain_dot(table_pair[1], value_upper)
    )


def convolve(propa_owned, screen_owned, factor):
    energy_count = propa_owned.shape[0]
    owned_shape = propa_owned[:, :, :, 0].shape
    freq_index = jnp.arange(2 * energy_count, dtype=jnp.int32)
    time_index = jnp.arange(energy_count, dtype=jnp.int32)
    phase = freq_index[:, None] * time_index[None, :] % (2 * energy_count)
    angle = phase.astype(jnp.float32) * (math.pi / energy_count)
    cosine = jnp.cos(angle)
    sine = jnp.sin(angle)
    cos_fwd = split_table(cosine)
    sin_fwd = split_table(sine)
    cos_back = split_table(cosine.T)
    sin_back = split_table(sine.T)

    def forward(banded):
        real_part = banded[:, :, :, 0].reshape(energy_count, -1)
        imag_part = banded[:, :, :, 1].reshape(energy_count, -1)
        return (
            table_times_data(cos_fwd, real_part) + table_times_data(sin_fwd, imag_part),
            table_times_data(cos_fwd, imag_part) - table_times_data(sin_fwd, real_part),
        )

    propa_real, propa_imag = forward(propa_owned)
    screen_real, screen_imag = forward(screen_owned)
    spec_real = propa_real * screen_real - propa_imag * screen_imag
    spec_imag = propa_real * screen_imag + propa_imag * screen_real
    weight = factor / (2 * energy_count)
    out_real = (
        table_times_float(cos_back, spec_real) - table_times_float(sin_back, spec_imag)
    ) * weight
    out_imag = (
        table_times_float(cos_back, spec_imag) + table_times_float(sin_back, spec_real)
    ) * weight
    return jnp.stack([out_real.reshape(owned_shape), out_imag.reshape(owned_shape)], axis=3)


def local(screening, polarization, propagator):
    row_count = screening.shape[1]
    order = screening.shape[-1]
    first_row = lax.axis_index("space") * row_count
    row_total = lax.axis_size("space") * row_count
    screen_masked = clip_edges(screening, first_row, row_total)
    polar_masked = clip_edges(polarization, first_row, row_total)
    propa_masked = clip_edges(propagator, first_row, row_total)
    rimmed = with_halo(jnp.stack([screen_masked, polar_masked, propa_masked]), (("space", 2),), 1)
    screen_padded = rimmed[0]
    polar_padded = rimmed[1]
    propa_padded = rimmed[2]
    screened = sandwich(screen_padded, polar_padded).astype(jnp.bfloat16)
    screen_owned, propa_owned = (
        lax.all_to_all(screened, "energy", split_axis=4, concat_axis=0, tiled=True),
        lax.all_to_all(propa_masked, "energy", split_axis=4, concat_axis=0, tiled=True),
    )
    energy_count = screen_owned.shape[0]
    factor = (3.0 * order / energy_count) ** 0.5
    sigma_owned = convolve(propa_owned, screen_owned, factor).astype(jnp.bfloat16)
    sigma = lax.all_to_all(sigma_owned, "energy", split_axis=0, concat_axis=4, tiled=True)
    sigma_padded = with_halo(sigma, (("space", 1),), 1)
    return sandwich(propa_padded, sigma_padded).astype(jnp.bfloat16)


def solution(mesh):
    in_specs = (
        P("energy", "space", None, None, None, None),
        P("energy", "space", None, None, None, None),
        P("energy", "space", None, None, None, None),
    )
    out_specs = P("energy", "space", None, None, None, None)
    return jax.shard_map(local, mesh=mesh, in_specs=in_specs, out_specs=out_specs, check_vma=False)
```

profile of v0, /device:TPU:0, one launch (start us, length us, event | category | flops | bytes accessed | tf_op | source)
XLA Modules:
  0.0 100.8 jit_solution(13113473520460223739)
XLA Ops:
  0.1 1.4 %fusion.83 = (bf16[1,1,2,3,2,128,128]{6,5,2,4,3,1,0:T(8,128)(2,1)S(1)}, bf16[1,1,2,3,2,128,128]{6,5,2,4,3,1,0:T(8,128)(2,1)S(1)}, bf16[1,2,3,2,128,128]{5,4,1,3,2,0:T(8,128)(2,1)S(1)}) fusion(bf16[1,2,3,2,128,128]{5,4,3,2,1,0:T(8,128)(2,1)} %param.3, bf16[2,3]{0,1:T(4,128)(2,1)S(1)} %select_convert_fusion, bf16[1,2,3,2,128,128]{5,4,3,2,1,0:T(8,128)(2,1)} %param.4, ...), kind=kLoop, calls=%fused_computation.188 | loop fusion | flops 589824 | bytes 2359308 | tf_op jit(solution)/shard_map/stack | solution.py:154
  1.5 1.2 %copy.19 = bf16[1,2,3,2,128,128]{5,1,3,2,0,4:T(2,128)(2,1)} copy(bf16[1,2,3,2,128,128]{5,4,1,3,2,0:T(8,128)(2,1)S(1)} %get-tuple-element.59) | data formatting | bytes 786432 | tf_op jit(solution)/shard_map/mul | solution.py:30
  2.6 5.2 %all-to-all-start = ((bf16[1,2,3,2,128,128]{5,1,3,2,0,4:T(2,128)(2,1)}), bf16[1,2,3,2,128,128]{5,1,3,2,0,4:T(2,128)(2,1)S(1)}, u32[]{:S(2)}, u32[]{:S(2)}) async-start(bf16[1,2,3,2,128,128]{5,1,3,2,0,4:T(2,128)(2,1)} %copy.19), calls=%async_computation | async-start | bytes 786432 | tf_op jit(solution)/shard_map/all_to_all | solution.py:161
  8.0 1.2 %fusion.358 = (bf16[3,1,1,3,2,128,128]{6,5,2,4,3,1,0:T(8,128)(2,1)}, bf16[3,1,1,3,2,128,128]{6,5,2,4,3,1,0:T(8,128)(2,1)}) fusion(bf16[3,1,2,3,2,128,128]{6,5,2,4,3,1,0:T(8,128)(2,1)S(1)} %pad_maximum_fusion.1), kind=kLoop, calls=%fused_computation.593 | loop fusion | bytes 2359296 | tf_op jit(solution)/shard_map/slice | solution.py:14
  9.1 4.3 %collective-permute-start = (bf16[3,1,1,3,2,128,128]{6,5,2,4,3,1,0:T(8,128)(2,1)}, bf16[3,1,1,3,2,128,128]{6,5,2,4,3,1,0:T(8,128)(2,1)}, u32[]{:S(2)}, u32[]{:S(2)}) collective-permute-start(bf16[3,1,1,3,2,128,128]{6,5,2,4,3,1,0:T(8,128)(2,1)} %get-tuple-element.10), channel_id=1, source_target_pairs={{0,1},{1,2},{2,3},{4,5},{5,6},{6,7},{8,9},{9,10},{10,11},{12,13},{... | collective-permute-start | bytes 1769480 | tf_op jit(solution)/shard_map/ppermute | solution.py:16
  13.4 1.3 %collective-permute-start.1 = (bf16[3,1,1,3,2,128,128]{6,5,2,4,3,1,0:T(8,128)(2,1)}, bf16[3,1,1,3,2,128,128]{6,5,2,4,3,1,0:T(8,128)(2,1)}, u32[]{:S(2)}, u32[]{:S(2)}) collective-permute-start(bf16[3,1,1,3,2,128,128]{6,5,2,4,3,1,0:T(8,128)(2,1)} %get-tuple-element.11), channel_id=1, source_target_pairs={{1,0},{2,1},{3,2},{5,4},{6,5},{7,6},{9,8},{10,9},{11,10},{13,12},{... | collective-permute-start | bytes 1769480 | tf_op jit(solution)/shard_map/ppermute | solution.py:17
  14.7 1.4 %all-to-all-done = bf16[1,2,3,2,128,128]{5,1,3,2,0,4:T(2,128)(2,1)S(1)} async-done(((bf16[1,2,3,2,128,128]{5,1,3,2,0,4:T(2,128)(2,1)}), bf16[1,2,3,2,128,128]{5,1,3,2,0,4:T(2,128)(2,1)S(1)}, u32[]{:S(2)}, u32[]{:S(2)}) %all-to-all-start) | async-done | bytes 393248 | tf_op jit(solution)/shard_map/all_to_all | solution.py:161
  16.3 1.2 %fusion.203 = f32[16,12288]{1,0:T(8,128)} fusion(bf16[8,12288]{1,0:T(8,128)(2,1)S(1)} %reshape_squeeze.13), kind=kOutput, calls=%fused_computation.447 | convolution fusion | flops 3147648 | bytes 983040 | tf_op jit(solution)/shard_map/dot_general | solution.py:94
  17.9 0.3 fusion.211
  18.2 0.3 convolution_add_fusion.7
  18.5 1.2 %convolution_add_fusion.3 = f32[16,12288]{1,0:T(8,128)} fusion(f32[16,12288]{1,0:T(8,128)S(1)} %fusion.207, bf16[8,12288]{1,0:T(8,128)(2,1)S(1)} %reshape_squeeze.13), kind=kOutput, calls=%fused_computation.5 | convolution fusion | flops 3344640 | bytes 1769472 | tf_op jit(solution)/shard_map/dot_general | solution.py:94
  19.7 6.4 %collective-permute-done = bf16[3,1,1,3,2,128,128]{6,5,2,4,3,1,0:T(8,128)(2,1)} collective-permute-done((bf16[3,1,1,3,2,128,128]{6,5,2,4,3,1,0:T(8,128)(2,1)}, bf16[3,1,1,3,2,128,128]{6,5,2,4,3,1,0:T(8,128)(2,1)}, u32[]{:S(2)}, u32[]{:S(2)}) %collective-permute-start) | collective-permute-done | bytes 589856 | tf_op jit(solution)/shard_map/ppermute | solution.py:16
  26.2 4.9 %collective-permute-done.1 = bf16[3,1,1,3,2,128,128]{6,5,2,4,3,1,0:T(8,128)(2,1)} collective-permute-done((bf16[3,1,1,3,2,128,128]{6,5,2,4,3,1,0:T(8,128)(2,1)}, bf16[3,1,1,3,2,128,128]{6,5,2,4,3,1,0:T(8,128)(2,1)}, u32[]{:S(2)}, u32[]{:S(2)}) %collective-permute-start.1) | collective-permute-done | bytes 589856 | tf_op jit(solution)/shard_map/ppermute | solution.py:17
  31.1 1.4 %pad_maximum_fusion = bf16[3,1,4,3,2,128,128]{6,5,2,4,3,1,0:T(8,128)(2,1)S(1)} fusion(bf16[3,1,1,3,2,128,128]{6,5,2,4,3,1,0:T(8,128)(2,1)} %collective-permute-done.1, bf16[1,1,2,3,2,128,128]{6,5,2,4,3,1,0:T(8,128)(2,1)S(1)} %bitcast.730, bf16[1,1,2,3,2,128,128]{6,5,2,4,3,1,0:T(8,128)(2,1)S(1)} %get-tuple-element.58, ...), kind=kLoop, calls=%fused_computation.26 | loop fusion | flops 4718592 | bytes 4718592 | tf_op jit(solution)/shard_map/concatenate | solution.py:18
  45.6 1.2 %copy.21 = bf16[1,2,3,2,128,128]{5,1,3,2,0,4:T(2,128)(2,1)} copy(bf16[1,2,3,2,128,128]{5,4,1,3,2,0:T(8,128)(2,1)S(1)} %pad_maximum_fusion.2) | data formatting | bytes 786432 | tf_op jit(solution)/shard_map/stack | solution.py:84
  46.7 3.8 %all-to-all-start.1 = ((bf16[1,2,3,2,128,128]{5,1,3,2,0,4:T(2,128)(2,1)}), bf16[1,2,3,2,128,128]{5,1,3,2,0,4:T(2,128)(2,1)S(1)}, u32[]{:S(2)}, u32[]{:S(2)}) async-start(bf16[1,2,3,2,128,128]{5,1,3,2,0,4:T(2,128)(2,1)} %copy.21), calls=%async_computation.1 | async-start | bytes 786432 | tf_op jit(solution)/shard_map/all_to_all | solution.py:160
  50.6 1.2 %fusion.199 = f32[16,12288]{1,0:T(8,128)} fusion(bf16[8,12288]{1,0:T(8,128)(2,1)S(1)} %reshape_squeeze.12), kind=kOutput, calls=%fused_computation.445 | convolution fusion | flops 3147648 | bytes 983040 | tf_op jit(solution)/shard_map/dot_general | solution.py:94
  51.8 1.2 %fusion.3 = f32[16,12288]{1,0:T(8,128)} fusion(f32[16,12288]{1,0:T(8,128)S(1)} %convolution_add_fusion.7, f32[16,12288]{1,0:T(8,128)S(1)} %copy-done.1, bf16[8,12288]{1,0:T(8,128)(2,1)S(1)} %reshape_squeeze.13), kind=kOutput, calls=%fused_computation.10 | convolution fusion | flops 3541248 | bytes 2555904 | tf_op jit(solution)/shard_map/dot_general | solution.py:94
  53.0 5.9 %all-to-all-done.1 = bf16[1,2,3,2,128,128]{5,1,3,2,0,4:T(2,128)(2,1)S(1)} async-done(((bf16[1,2,3,2,128,128]{5,1,3,2,0,4:T(2,128)(2,1)}), bf16[1,2,3,2,128,128]{5,1,3,2,0,4:T(2,128)(2,1)S(1)}, u32[]{:S(2)}, u32[]{:S(2)}) %all-to-all-start.1) | async-done | bytes 393248 | tf_op jit(solution)/shard_map/all_to_all | solution.py:160
  59.1 0.3 fusion.201
  60.4 0.3 convolution_add_fusion.5
  60.7 0.3 convolution_add_fusion.1
  61.0 0.3 fusion.2
  61.3 0.3 fusion
  61.6 0.5 copy-done
  62.6 0.4 multiply_subtract_fusion
  66.1 10.7 %all_to_all.54 = bf16[8,2,3,2,16,128]{5,4,2,1,3,0:T(8,128)(2,1)S(1)} all-to-all(bf16[8,2,3,2,16,128]{5,4,2,1,3,0:T(8,128)(2,1)S(1)} %pad_maximum_fusion.3), channel_id=1, replica_groups=mesh['energy'=8,'space'=4] {'energy'}, dimensions={0} | all-to-all | bytes 786432 | tf_op jit(solution)/shard_map/all_to_all | solution.py:166
  76.8 2.7 %collective-permute-start.2 = (bf16[1,1,3,2,128,128]{5,4,1,3,2,0:T(8,128)(2,1)S(1)}, bf16[1,1,3,2,128,128]{5,4,1,3,2,0:T(8,128)(2,1)S(1)}, u32[]{:S(2)}, u32[]{:S(2)}) collective-permute-start(bf16[1,1,3,2,128,128]{5,4,1,3,2,0:T(8,128)(2,1)S(1)} %get-tuple-element.51), channel_id=1, source_target_pairs={{0,1},{1,2},{2,3},{4,5},{5,6},{6,7},{8,9},{9,10},{10,11},{12,13},{... | collective-permute-start | bytes 589832 | tf_op jit(solution)/shard_map/ppermute | solution.py:16
  79.6 1.3 %collective-permute-start.3 = (bf16[1,1,3,2,128,128]{5,4,1,3,2,0:T(8,128)(2,1)S(1)}, bf16[1,1,3,2,128,128]{5,4,1,3,2,0:T(8,128)(2,1)S(1)}, u32[]{:S(2)}, u32[]{:S(2)}) collective-permute-start(bf16[1,1,3,2,128,128]{5,4,1,3,2,0:T(8,128)(2,1)S(1)} %get-tuple-element.52), channel_id=1, source_target_pairs={{1,0},{2,1},{3,2},{5,4},{6,5},{7,6},{9,8},{10,9},{11,10},{13,12},{... | collective-permute-start | bytes 589832 | tf_op jit(solution)/shard_map/ppermute | solution.py:17
  81.1 2.3 %collective-permute-done.2 = bf16[1,1,3,2,128,128]{5,4,1,3,2,0:T(8,128)(2,1)S(1)} collective-permute-done((bf16[1,1,3,2,128,128]{5,4,1,3,2,0:T(8,128)(2,1)S(1)}, bf16[1,1,3,2,128,128]{5,4,1,3,2,0:T(8,128)(2,1)S(1)}, u32[]{:S(2)}, u32[]{:S(2)}) %collective-permute-start.2) | collective-permute-done | bytes 196640 | tf_op jit(solution)/shard_map/ppermute | solution.py:16
  83.4 4.1 %collective-permute-done.3 = bf16[1,1,3,2,128,128]{5,4,1,3,2,0:T(8,128)(2,1)S(1)} collective-permute-done((bf16[1,1,3,2,128,128]{5,4,1,3,2,0:T(8,128)(2,1)S(1)}, bf16[1,1,3,2,128,128]{5,4,1,3,2,0:T(8,128)(2,1)S(1)}, u32[]{:S(2)}, u32[]{:S(2)}) %collective-permute-start.3) | collective-permute-done | bytes 196640 | tf_op jit(solution)/shard_map/ppermute | solution.py:17
  100.0 0.8 copy.26
  (203 shorter events, 30.9 us)
Async XLA Ops:
  2.6 13.5 %all-to-all-start = ((bf16[1,2,3,2,128,128]{5,1,3,2,0,4:T(2,128)(2,1)}), bf16[1,2,3,2,128,128]{5,1,3,2,0,4:T(2,128)(2,1)S(1)}, u32[]{:S(2)}, u32[]{:S(2)}) async-start(bf16[1,2,3,2,128,128]{5,1,3,2,0,4:T(2,128)(2,1)} %copy.19), calls=%async_computation | async-start | bytes 786432 | tf_op jit(solution)/shard_map/all_to_all | solution.py:161
  9.1 17.0 %collective-permute-start = (bf16[3,1,1,3,2,128,128]{6,5,2,4,3,1,0:T(8,128)(2,1)}, bf16[3,1,1,3,2,128,128]{6,5,2,4,3,1,0:T(8,128)(2,1)}, u32[]{:S(2)}, u32[]{:S(2)}) collective-permute-start(bf16[3,1,1,3,2,128,128]{6,5,2,4,3,1,0:T(8,128)(2,1)} %get-tuple-element.10), channel_id=1, source_target_pairs={{0,1},{1,2},{2,3},{4,5},{5,6},{6,7},{8,9},{9,10},{10,11},{12,13},{... | collective-permute-start | bytes 1769480 | tf_op jit(solution)/shard_map/ppermute | solution.py:16
  13.4 17.7 %collective-permute-start.1 = (bf16[3,1,1,3,2,128,128]{6,5,2,4,3,1,0:T(8,128)(2,1)}, bf16[3,1,1,3,2,128,128]{6,5,2,4,3,1,0:T(8,128)(2,1)}, u32[]{:S(2)}, u32[]{:S(2)}) collective-permute-start(bf16[3,1,1,3,2,128,128]{6,5,2,4,3,1,0:T(8,128)(2,1)} %get-tuple-element.11), channel_id=1, source_target_pairs={{1,0},{2,1},{3,2},{5,4},{6,5},{7,6},{9,8},{10,9},{11,10},{13,12},{... | collective-permute-start | bytes 1769480 | tf_op jit(solution)/shard_map/ppermute | solution.py:17
  45.4 6.3 %copy-start.1 = (f32[16,12288]{1,0:T(8,128)S(1)}, f32[16,12288]{1,0:T(8,128)}, u32[]{:S(2)}) copy-start(f32[16,12288]{1,0:T(8,128)} %fusion.203) | copy-start | bytes 2359300
  46.7 12.1 %all-to-all-start.1 = ((bf16[1,2,3,2,128,128]{5,1,3,2,0,4:T(2,128)(2,1)}), bf16[1,2,3,2,128,128]{5,1,3,2,0,4:T(2,128)(2,1)S(1)}, u32[]{:S(2)}, u32[]{:S(2)}) async-start(bf16[1,2,3,2,128,128]{5,1,3,2,0,4:T(2,128)(2,1)} %copy.21), calls=%async_computation.1 | async-start | bytes 786432 | tf_op jit(solution)/shard_map/all_to_all | solution.py:160
  61.0 1.1 %copy-start = (f32[16,12288]{1,0:T(8,128)S(1)}, f32[16,12288]{1,0:T(8,128)}, u32[]{:S(2)}) copy-start(f32[16,12288]{1,0:T(8,128)} %convolution_add_fusion.3) | copy-start | bytes 2359300
  61.0 1.4 %copy-start.2 = (f32[16,12288]{1,0:T(8,128)S(1)}, f32[16,12288]{1,0:T(8,128)}, u32[]{:S(2)}) copy-start(f32[16,12288]{1,0:T(8,128)} %fusion.199) | copy-start | bytes 2359300
  61.0 1.6 %copy-start.3 = (f32[16,12288]{1,0:T(8,128)S(1)}, f32[16,12288]{1,0:T(8,128)}, u32[]{:S(2)}) copy-start(f32[16,12288]{1,0:T(8,128)} %fusion.3) | copy-start | bytes 2359300
  76.8 6.5 %collective-permute-start.2 = (bf16[1,1,3,2,128,128]{5,4,1,3,2,0:T(8,128)(2,1)S(1)}, bf16[1,1,3,2,128,128]{5,4,1,3,2,0:T(8,128)(2,1)S(1)}, u32[]{:S(2)}, u32[]{:S(2)}) collective-permute-start(bf16[1,1,3,2,128,128]{5,4,1,3,2,0:T(8,128)(2,1)S(1)} %get-tuple-element.51), channel_id=1, source_target_pairs={{0,1},{1,2},{2,3},{4,5},{5,6},{6,7},{8,9},{9,10},{10,11},{12,13},{... | collective-permute-start | bytes 589832 | tf_op jit(solution)/shard_map/ppermute | solution.py:16
  79.6 8.0 %collective-permute-start.3 = (bf16[1,1,3,2,128,128]{5,4,1,3,2,0:T(8,128)(2,1)S(1)}, bf16[1,1,3,2,128,128]{5,4,1,3,2,0:T(8,128)(2,1)S(1)}, u32[]{:S(2)}, u32[]{:S(2)}) collective-permute-start(bf16[1,1,3,2,128,128]{5,4,1,3,2,0:T(8,128)(2,1)S(1)} %get-tuple-element.52), channel_id=1, source_target_pairs={{1,0},{2,1},{3,2},{5,4},{6,5},{7,6},{9,8},{10,9},{11,10},{13,12},{... | collective-permute-start | bytes 589832 | tf_op jit(solution)/shard_map/ppermute | solution.py:17
where the time goes:
time: 101 us
  matrix products  35.2 us (35%)
  waiting for transfers between devices  25.1 us (25%)
  starting transfers between devices  18.6 us (18%)
  blocking collectives  10.7 us (11%)
  local copies, waits for them, and re-layouts  6.76 us (7%)
  other arithmetic  3.78 us (4%)
    dot_general x144, matrix products, product(): return jnp.einsum(form, lhs, rhs, preferred_element_type=jnp.float32)  23.9 us
    dot_general x28, matrix products, plain_dot(): return jnp.dot(lhs, rhs, preferred_element_type=jnp.float32)  11.4 us
    all_to_all x1, blocking collectives, local(): lax.all_to_all(sigma_owned, 'energy', split_axis=0, concat_axis=4, tiled=...  10.7 us
    ppermute x2, waiting for transfers between devices, with_halo(): after = lax.ppermute(leading, axis, down)  9.03 us
    ppermute x2, waiting for transfers between devices, with_halo(): before = lax.ppermute(last, axis, up)  8.72 us
    ppermute x2, starting transfers between devices, with_halo(): before = lax.ppermute(last, axis, up)  6.99 us
    all_to_all x1, waiting for transfers between devices, local(): lax.all_to_all(screened, 'energy', split_axis=4, concat_axis=0, tiled=True)  5.9 us
    all_to_all x1, starting transfers between devices, local(): lax.all_to_all(propa_masked, 'energy', split_axis=4, concat_axis=0, tiled...  5.2 us
  transfers between devices with their start and end apart: 6, of which 6 were waited for; matrix products, arithmetic and copies ran while one was open for 7% of the time, Pallas kernels for 0%

commit v1 on v0

v1 whole, which is shorter than its diff:
```python
import functools

import jax
import jax.numpy as jnp
from jax import lax
from jax.experimental import pallas as pl
from jax.experimental.pallas import tpu as pltpu
from jax.sharding import PartitionSpec as P

BF16 = jnp.bfloat16
F32 = jnp.float32
VMEM = pl.BlockSpec(memory_space=pltpu.VMEM)
PACK = 16


def row_form(real, imag):
    return jnp.concatenate([real, imag], axis=1)


def square_form(real, imag):
    return jnp.concatenate([row_form(real, imag), row_form(-imag, real)], axis=0)


def times(lhs, rhs):
    return jnp.dot(lhs, rhs, preferred_element_type=F32)


def times_adjoint(lhs, rhs):
    return lax.dot_general(lhs, rhs, (((1,), (1,)), ((), ())), preferred_element_type=F32)


def edge_mask(block, is_edge):
    return jnp.where(is_edge, jnp.zeros_like(block), block)


class Band:
    def __init__(self, load, rows, first, last):
        self.load, self.rows, self.first, self.last = load, rows, first, last
        self.cache = {}

    def pair(self, row, col):
        if (row, col) not in self.cache:
            real, imag = self.load(row, col - row + 1, 0), self.load(row, col - row + 1, 1)
            if self.first is not None and row == 0 and col == -1:
                real, imag = edge_mask(real, self.first), edge_mask(imag, self.first)
            if self.last is not None and row == self.rows - 1 and col == self.rows:
                real, imag = edge_mask(real, self.last), edge_mask(imag, self.last)
            self.cache[row, col] = (real, imag)
        return self.cache[row, col]

    def row(self, row, col):
        return row_form(*self.pair(row, col))

    def square(self, row, col):
        return square_form(*self.pair(row, col))


def plain_load(ref):
    return lambda i, t, c: ref[i, t, c]


def slot_load(ref):
    def load(i, t, c):
        value = ref[:, i, t, c]
        return value.reshape(value.shape[0] * value.shape[1], value.shape[2])

    return load


def own_adjoint(outer, inner, row):
    total = None
    for col in range(row - 1, row + 2):
        term = times_adjoint(inner.row(row, col), outer.square(row, col))
        total = term if total is None else total + term
    return total.astype(BF16)


def split_store(ref, index, value):
    half = value.shape[1] // 2
    ref[index, 0] = value[:, :half]
    ref[index, 1] = value[:, half:]


def copy_pair(ref, index, pair):
    ref[index, 0] = pair[0]
    ref[index, 1] = pair[1]


def sandwich(outer, inner, rows, left, right, store):
    def inner_pair(row, col):
        if row == -1:
            return left("inner", "same" if col == row else "cross")
        if row == rows:
            return right("inner", "same" if col == row else "cross")
        return inner.pair(row, col)

    full, local = {}, {}
    for mid in range(-1, rows + 1):
        users = [i for i in range(max(mid - 1, 0), min(mid + 2, rows))]
        lhs = jnp.concatenate([outer.row(i, mid) for i in users], axis=0)
        for col in range(mid - 1, mid + 2):
            if col < -1 or col > rows:
                continue
            result = times(lhs, square_form(*inner_pair(mid, col)))
            size = result.shape[0] // len(users)
            for place, i in enumerate(users):
                part = result[place * size : (place + 1) * size]
                full[i, col] = full[i, col] + part if (i, col) in full else part
                if 0 <= mid < rows:
                    local[i, col] = local[i, col] + part if (i, col) in local else part
    for target in range(rows):
        users = [i for i in range(max(target - 1, 0), min(target + 2, rows))]
        total = None
        for col in range(target - 1, target + 2):
            lhs = jnp.concatenate([full[i, col].astype(BF16) for i in users], axis=0)
            term = times_adjoint(lhs, outer.square(target, col))
            total = term if total is None else total + term
        size = total.shape[0] // len(users)
        for place, i in enumerate(users):
            store(i, target - i + 1, total[place * size : (place + 1) * size].astype(BF16))
    for row, edge, side, band in ((0, -1, left, 0), (rows - 1, rows, right, 2)):
        total = times(outer.row(row, edge), square_form(*side("adjoint", None)))
        total += times_adjoint(local[row, edge].astype(BF16), square_form(*side("outer", "same")))
        total += times_adjoint(local[row, row].astype(BF16), square_form(*side("outer", "cross")))
        store(row, band, total.astype(BF16))


def edges(space, rows):
    place = lax.axis_index(space)
    return place == 0, place == lax.axis_size(space) - 1


def send_kernel(space, w_ref, p_ref, up_ref, down_ref):
    rows = w_ref.shape[0]
    first, last = edges(space, rows)
    outer = Band(plain_load(w_ref), rows, None, None)
    inner = Band(plain_load(p_ref), rows, first, last)
    for ref, row, cross in ((up_ref, rows - 1, rows), (down_ref, 0, -1)):
        copy_pair(ref, 0, inner.pair(row, row))
        copy_pair(ref, 1, inner.pair(row, cross))
        copy_pair(ref, 2, outer.pair(row, row))
        copy_pair(ref, 3, outer.pair(row, cross))
        split_store(ref, 4, own_adjoint(outer, inner, row))


def halo_side(ref):
    where = {("inner", "same"): 0, ("inner", "cross"): 1, ("outer", "same"): 2, ("outer", "cross"): 3, ("adjoint", None): 4}

    def side(kind, which):
        index = where[kind, which]
        return ref[index, 0], ref[index, 1]

    return side


def screened_kernel(space, w_ref, p_ref, left_ref, right_ref, out_ref):
    rows = w_ref.shape[0]
    first, last = edges(space, rows)
    outer = Band(plain_load(w_ref), rows, None, None)
    inner = Band(plain_load(p_ref), rows, first, last)
    slots, piece = out_ref.shape[0], out_ref.shape[4]

    def store(i, t, value):
        half = value.shape[1] // 2
        out_ref[:, i, t, 0] = value[:, :half].reshape(slots, piece, half)
        out_ref[:, i, t, 1] = value[:, half:].reshape(slots, piece, half)

    sandwich(outer, inner, rows, halo_side(left_ref), halo_side(right_ref), store)


def middle_kernel(g_ref, s_ref, up_ref, down_ref):
    rows = g_ref.shape[0]
    outer = Band(plain_load(g_ref), rows, None, None)
    inner = Band(slot_load(s_ref), rows, None, None)
    for ref, row, cross in ((up_ref, rows - 1, rows), (down_ref, 0, -1)):
        copy_pair(ref, 0, inner.pair(row, row))
        copy_pair(ref, 1, inner.pair(row, cross))
        split_store(ref, 2, own_adjoint(outer, inner, row))


def dressed_kernel(g_ref, s_ref, gl_ref, gr_ref, sl_ref, sr_ref, out_ref):
    rows = g_ref.shape[0]
    outer = Band(plain_load(g_ref), rows, None, None)
    inner = Band(slot_load(s_ref), rows, None, None)

    def side_of(outer_ref, inner_ref):
        where = {
            ("inner", "same"): (inner_ref, 0),
            ("inner", "cross"): (inner_ref, 1),
            ("adjoint", None): (inner_ref, 2),
            ("outer", "same"): (outer_ref, 0),
            ("outer", "cross"): (outer_ref, 1),
        }

        def side(kind, which):
            ref, index = where[kind, which]
            return ref[index, 0], ref[index, 1]

        return side

    def store(i, t, value):
        half = value.shape[1] // 2
        out_ref[i, t, 0] = value[:, :half]
        out_ref[i, t, 1] = value[:, half:]

    sandwich(outer, inner, rows, side_of(gl_ref, sl_ref), side_of(gr_ref, sr_ref), store)


def convolve_kernel(factor, g_ref, s_ref, out_ref):
    count, groups = out_ref.shape[0], out_ref.shape[1]

    def load(ref, e, a, c):
        return ref[e, a, c].astype(F32)

    if count <= PACK:
        for a in range(groups):
            g_real = [load(g_ref, e, a, 0) for e in range(count)]
            g_imag = [load(g_ref, e, a, 1) for e in range(count)]
            s_real = [load(s_ref, e, a, 0) for e in range(count)]
            s_imag = [load(s_ref, e, a, 1) for e in range(count)]
            for e in range(count):
                real = imag = None
                for k in range(e + 1):
                    r = g_real[e - k] * s_real[k] - g_imag[e - k] * s_imag[k]
                    m = g_real[e - k] * s_imag[k] + g_imag[e - k] * s_real[k]
                    real, imag = (r, m) if real is None else (real + r, imag + m)
                out_ref[e, a, 0] = (real * factor).astype(BF16)
                out_ref[e, a, 1] = (imag * factor).astype(BF16)
        return
    for a in range(groups):

        def energy(e, carry):
            def term(k, totals):
                g_real, g_imag = load(g_ref, e - k, a, 0), load(g_ref, e - k, a, 1)
                s_real, s_imag = load(s_ref, k, a, 0), load(s_ref, k, a, 1)
                return (
                    totals[0] + g_real * s_real - g_imag * s_imag,
                    totals[1] + g_real * s_imag + g_imag * s_real,
                )

            zero = jnp.zeros(out_ref.shape[3:], F32)
            real, imag = lax.fori_loop(0, e + 1, term, (zero, zero))
            out_ref[e, a, 0] = (real * factor).astype(BF16)
            out_ref[e, a, 1] = (imag * factor).astype(BF16)
            return carry

        lax.fori_loop(0, count, energy, 0)


def call(kernel, shapes, *args, flops=0, name=None):
    outs = tuple(jax.ShapeDtypeStruct(shape, BF16) for shape in shapes)
    moved = sum(2 * a.size for a in args) + sum(2 * o.size for o in outs)
    single = len(outs) == 1
    return pl.pallas_call(
        kernel,
        out_shape=outs[0] if single else outs,
        in_specs=[VMEM] * len(args),
        out_specs=VMEM if single else tuple([VMEM] * len(outs)),
        cost_estimate=pl.CostEstimate(flops=flops, bytes_accessed=moved, transcendentals=0),
        compiler_params=pltpu.CompilerParams(vmem_limit_bytes=32 * 1024 * 1024),
        name=name,
    )(*args)


def local(screening, polarization, propagator):
    w, p, g = screening[0], polarization[0], propagator[0]
    rows, bands, parts, order = w.shape[0], w.shape[1], w.shape[2], w.shape[3]
    peers, count = lax.axis_size("space"), lax.axis_size("energy")
    up = [(i, i + 1) for i in range(peers - 1)]
    down = [(j, i) for i, j in up]
    piece = order // count
    slots = count if piece % PACK == 0 else 1
    block = 8 * order**3

    def spread(x):
        if slots == count:
            return x
        x = x.reshape(rows, bands, parts, count, piece, order)
        return jnp.moveaxis(x, 3, 0)

    def exchange(x):
        return lax.all_to_all(x, "energy", 0, 0, tiled=True)

    def flat(x):
        if slots == count:
            return x.reshape(count, rows * bands, parts, piece, order)
        x = jnp.moveaxis(x, 3, 1)
        return x.reshape(count, 1, parts, rows * bands * piece, order)

    def unflat(x):
        if slots == count:
            return x.reshape(count, rows, bands, parts, piece, order)
        return jnp.moveaxis(x.reshape(count, parts, rows, bands, piece, order), 1, 3)

    def gather(x):
        if slots == count:
            return x
        return jnp.moveaxis(x, 0, 3).reshape(1, rows, bands, parts, order, order)

    up_buf, down_buf = call(
        functools.partial(send_kernel, "space"), [(5, parts, order, order)] * 2, w, p, flops=6 * block, name="send"
    )
    left = lax.ppermute(up_buf, "space", up)
    right = lax.ppermute(down_buf, "space", down)

    g_slots = jnp.moveaxis(g.reshape(rows, bands, parts, count, piece, order), 3, 0)
    g_owned = exchange(g_slots)

    g_left = lax.ppermute(g[rows - 1, 1:3], "space", up)
    g_right = lax.ppermute(jnp.stack([g[0, 1], g[0, 0]]), "space", down)

    screened = call(
        functools.partial(screened_kernel, "space"),
        [(slots, rows, bands, parts, order // slots, order)],
        w, p, left, right, flops=34 * block, name="screened",
    )
    s_owned = exchange(spread(screened))
    factor = (3.0 * order / count) ** 0.5
    g_flat, s_flat = flat(g_owned), flat(s_owned)
    sigma_owned = call(functools.partial(convolve_kernel, factor), [s_flat.shape], g_flat, s_flat, name="convolve")
    sigma = gather(exchange(unflat(sigma_owned)))

    up_buf, down_buf = call(middle_kernel, [(3, parts, order, order)] * 2, g, sigma, flops=6 * block, name="middle")
    s_left = lax.ppermute(up_buf, "space", up)
    s_right = lax.ppermute(down_buf, "space", down)
    out = call(
        dressed_kernel, [w.shape], g, sigma, g_left, g_right, s_left, s_right, flops=34 * block, name="dressed"
    )
    return out[None]


def solution(mesh):
    spec = P("energy", "space", None, None, None, None)
    return jax.shard_map(local, mesh=mesh, in_specs=(spec, spec, spec), out_specs=spec, check_vma=False)
```

time: 101 us -> 60.8 us (0.60)
  matrix products: 35.2 us -> 0 us
  waiting for transfers between devices: 25.1 us -> 16.8 us
  starting transfers between devices: 18.6 us -> 25.3 us
  Pallas kernels: 0 us -> 4.57 us
  local copies, waits for them, and re-layouts: 6.76 us -> 2.8 us
  other arithmetic: 3.78 us -> 0.02 us
    dot_general x172 -> x0, matrix products: 35.2 us -> none  [the longest x144 23.9 us: product(): return jnp.einsum(form, lhs, rhs, preferred_element_type=jnp.float32)]
    ppermute x4 -> x6, waiting for transfers between devices: 17.8 us -> 7.6 us  [the longest x1 4.13 us: local(): right = lax.ppermute(down_buf, 'space', down)]
    ppermute x4 -> x6, starting transfers between devices: 9.56 us -> 18 us  [the longest x1 4.98 us: local(): left = lax.ppermute(up_buf, 'space', up)]
    pallas_call x0 -> x5, Pallas kernels: none -> 4.57 us  [call(): pl.pallas_call(kernel, out_shape=outs[0] if single else outs, in_specs=[V...]
    another operation x11 -> x1, other arithmetic: 1.95 us -> 0.02 us  [local(): g_right = lax.ppermute(jnp.stack([g[0, 1], g[0, 0]]), 'space', down)]
    all_to_all x2, waiting for transfers between devices: 7.33 us -> 9.22 us  [exchange(): return lax.all_to_all(x, 'energy', 0, 0, tiled=True)]
    all_to_all x2, starting transfers between devices: 9.01 us -> 7.31 us  [exchange(): return lax.all_to_all(x, 'energy', 0, 0, tiled=True)]
    another operation x8 -> x2, local copies, waits for them, and re-layouts: 2.33 us -> 0.79 us  [the longest x1 0.78 us: local(): g.reshape(rows, bands, parts, count, piece, order)]
  transfers between devices with their start and end apart: 6 -> 8, of which waited for: 6 -> 5; matrix products, arithmetic and copies ran while one was open for 7% -> 1% of each run, Pallas kernels for 0% -> 2%
where the time goes in v1:
time: 60.8 us; the launch traced here: 60.3 us
  starting transfers between devices  25.3 us (42%)
  waiting for transfers between devices  16.8 us (28%)
  blocking collectives  10.7 us (18%)
  Pallas kernels  4.57 us (8%)
  local copies, waits for them, and re-layouts  2.8 us (5%)
    all_to_all x1, blocking collectives, exchange(): return lax.all_to_all(x, 'energy', 0, 0, tiled=True)  10.7 us
    all_to_all x2, waiting for transfers between devices, exchange(): return lax.all_to_all(x, 'energy', 0, 0, tiled=True)  9.22 us
    all_to_all x2, starting transfers between devices, exchange(): return lax.all_to_all(x, 'energy', 0, 0, tiled=True)  7.31 us
    ppermute x1, starting transfers between devices, local(): left = lax.ppermute(up_buf, 'space', up)  4.98 us
    pallas_call x5, Pallas kernels, call(): pl.pallas_call(kernel, out_shape=outs[0] if single else outs, in_specs=[V...  4.57 us
    ppermute x1, starting transfers between devices, local(): g_left = lax.ppermute(g[rows - 1, 1:3], 'space', up)  4.55 us
    ppermute x1, starting transfers between devices, local(): s_left = lax.ppermute(up_buf, 'space', up)  4.55 us
    ppermute x1, waiting for transfers between devices, local(): right = lax.ppermute(down_buf, 'space', down)  4.13 us
  transfers between devices with their start and end apart: 8, of which 5 were waited for; matrix products, arithmetic and copies ran while one was open for 1% of the time, Pallas kernels for 2%

profile of v1, /device:TPU:0, one launch (start us, length us, event | category | flops | bytes accessed | tf_op | source)
XLA Modules:
  0.0 60.3 jit_solution(1240726320944094251)
XLA Ops:
  0.0 0.0 copy-start.1
  0.0 1.0 %copy-done.1 = bf16[1,2,3,2,128,128]{5,4,3,2,1,0:T(8,128)(2,1)S(1)} copy-done((bf16[1,2,3,2,128,128]{5,4,3,2,1,0:T(8,128)(2,1)S(1)}, bf16[1,2,3,2,128,128]{5,4,3,2,1,0:T(8,128)(2,1)}, u32[]{:S(2)}) %copy-start.1) | copy-done | bytes 393240
  1.0 0.0 copy-start.3
  1.0 1.0 %copy-done.3 = bf16[1,2,3,2,128,128]{5,4,3,2,1,0:T(8,128)(2,1)S(1)} copy-done((bf16[1,2,3,2,128,128]{5,4,3,2,1,0:T(8,128)(2,1)S(1)}, bf16[1,2,3,2,128,128]{5,4,3,2,1,0:T(8,128)(2,1)}, u32[]{:S(2)}) %copy-start.3) | copy-done | bytes 393240
  2.0 0.0 copy-start
  2.0 0.4 send.1
  2.4 5.0 %collective-permute-start = (bf16[5,2,128,128]{3,2,1,0:T(8,128)(2,1)S(1)}, bf16[5,2,128,128]{3,2,1,0:T(8,128)(2,1)S(1)}, u32[]{:S(2)}, u32[]{:S(2)}) collective-permute-start(bf16[5,2,128,128]{3,2,1,0:T(8,128)(2,1)S(1)} %get-tuple-element.9), channel_id=1, source_target_pairs={{0,1},{1,2},{2,3},{4,5},{5,6},{6,7},{8,9},{9,10},{10,11},{12,13},{... | collective-permute-start | bytes 983048 | tf_op jit(solution)/shard_map/ppermute | solution.py:303
  7.4 1.3 %collective-permute-start.1 = (bf16[5,2,128,128]{3,2,1,0:T(8,128)(2,1)S(1)}, bf16[5,2,128,128]{3,2,1,0:T(8,128)(2,1)S(1)}, u32[]{:S(2)}, u32[]{:S(2)}) collective-permute-start(bf16[5,2,128,128]{3,2,1,0:T(8,128)(2,1)S(1)} %get-tuple-element.10), channel_id=1, source_target_pairs={{1,0},{2,1},{3,2},{5,4},{6,5},{7,6},{9,8},{10,9},{11,10},{13,12},{... | collective-permute-start | bytes 983048 | tf_op jit(solution)/shard_map/ppermute | solution.py:304
  8.7 0.0 copy-done
  8.7 0.8 %copy.6 = bf16[2,3,2,8,16,128]{5,4,2,1,0,3:T(8,128)(2,1)} copy(bf16[2,3,2,8,16,128]{5,4,3,2,1,0:T(8,128)(2,1)S(1)} %bitcast.17) | data formatting | bytes 786432 | tf_op jit(solution)/shard_map/reshape;squeeze | solution.py:306
  9.5 0.0 copy-start.2
  9.5 3.9 %all-to-all-start = ((bf16[8,2,3,2,16,128]{5,4,3,2,1,0:T(8,128)(2,1)}), bf16[8,2,3,2,16,128]{5,4,3,2,1,0:T(8,128)(2,1)S(1)}, u32[]{:S(2)}, u32[]{:S(2)}) async-start(bf16[8,2,3,2,16,128]{5,4,3,2,1,0:T(8,128)(2,1)} %bitcast.16), calls=%async_computation | async-start | bytes 786432 | tf_op jit(solution)/shard_map/all_to_all | solution.py:282
  13.3 1.0 %collective-permute-done.left_ref = bf16[5,2,128,128]{3,2,1,0:T(8,128)(2,1)S(1)} collective-permute-done((bf16[5,2,128,128]{3,2,1,0:T(8,128)(2,1)S(1)}, bf16[5,2,128,128]{3,2,1,0:T(8,128)(2,1)S(1)}, u32[]{:S(2)}, u32[]{:S(2)}) %collective-permute-start) | collective-permute-done | bytes 327712 | tf_op jit(solution)/shard_map/ppermute | solution.py:303
  14.3 4.1 %collective-permute-done.1.right_ref = bf16[5,2,128,128]{3,2,1,0:T(8,128)(2,1)S(1)} collective-permute-done((bf16[5,2,128,128]{3,2,1,0:T(8,128)(2,1)S(1)}, bf16[5,2,128,128]{3,2,1,0:T(8,128)(2,1)S(1)}, u32[]{:S(2)}, u32[]{:S(2)}) %collective-permute-start.1) | collective-permute-done | bytes 327712 | tf_op jit(solution)/shard_map/ppermute | solution.py:304
  18.5 0.0 copy-done.2
  18.5 0.0 copy-done.4
  18.5 0.9 %screened.1 = bf16[8,2,3,2,16,128]{5,4,3,2,1,0:T(8,128)(2,1)S(1)} custom-call(bf16[2,3,2,128,128]{4,3,2,1,0:T(8,128)(2,1)S(1)} %bitcast.25, bf16[2,3,2,128,128]{4,3,2,1,0:T(8,128)(2,1)S(1)} %bitcast.27, bf16[5,2,128,128]{3,2,1,0:T(8,128)(2,1)S(1)} %collective-permute-done.left_ref, bf16[5,2,128,128]{3,2,1,0:T(8,128)(2,1)S(1)} %collective-permute-done.1.right_ref), custom_call_target="tpu_custom_call" | custom-call | flops 570425344 | bytes 1835008 | tf_op jit(solution)/shard_map/screened/pallas_call | solution.py:254
  19.3 2.3 %all-to-all-done = bf16[8,2,3,2,16,128]{5,4,3,2,1,0:T(8,128)(2,1)S(1)} async-done(((bf16[8,2,3,2,16,128]{5,4,3,2,1,0:T(8,128)(2,1)}), bf16[8,2,3,2,16,128]{5,4,3,2,1,0:T(8,128)(2,1)S(1)}, u32[]{:S(2)}, u32[]{:S(2)}) %all-to-all-start) | async-done | bytes 393248 | tf_op jit(solution)/shard_map/all_to_all | solution.py:282
  21.6 10.7 %all_to_all.15 = bf16[8,2,3,2,16,128]{5,4,3,2,1,0:T(8,128)(2,1)S(1)} all-to-all(bf16[8,2,3,2,16,128]{5,4,3,2,1,0:T(8,128)(2,1)S(1)} %screened.1), channel_id=1, replica_groups=mesh['energy'=8,'space'=4] {'energy'}, dimensions={0} | all-to-all | bytes 786432 | tf_op jit(solution)/shard_map/all_to_all | solution.py:282
  32.3 1.3 %convolve.1 = bf16[8,6,2,16,128]{4,3,2,1,0:T(8,128)(2,1)} custom-call(bf16[8,6,2,16,128]{4,3,2,1,0:T(8,128)(2,1)S(1)} %bitcast.22, bf16[8,6,2,16,128]{4,3,2,1,0:T(8,128)(2,1)S(1)} %bitcast.23), custom_call_target="tpu_custom_call" | custom-call | bytes 1179648 | tf_op jit(solution)/shard_map/convolve/pallas_call | solution.py:254
  33.6 3.5 %all-to-all-start.2 = ((bf16[8,2,3,2,16,128]{5,4,3,2,1,0:T(8,128)(2,1)}), bf16[8,2,3,2,16,128]{5,4,3,2,1,0:T(8,128)(2,1)S(1)}, u32[]{:S(2)}, u32[]{:S(2)}) async-start(bf16[8,2,3,2,16,128]{5,4,3,2,1,0:T(8,128)(2,1)} %bitcast.7), calls=%async_computation.2 | async-start | bytes 786432 | tf_op jit(solution)/shard_map/all_to_all | solution.py:282
  37.1 1.3 %collective-permute-start.3 = (bf16[2,2,128,128]{3,2,1,0:T(8,128)(2,1)S(1)}, bf16[2,2,128,128]{3,2,1,0:T(8,128)(2,1)S(1)}, u32[]{:S(2)}, u32[]{:S(2)}) collective-permute-start(bf16[2,2,128,128]{3,2,1,0:T(8,128)(2,1)S(1)} %pad_maximum_fusion), channel_id=1, source_target_pairs={{1,0},{2,1},{3,2},{5,4},{6,5},{7,6},{9,8},{10,9},{11,10},{13,12},{... | collective-permute-start | bytes 393224 | tf_op jit(solution)/shard_map/ppermute | solution.py:310
  38.4 6.9 %all-to-all-done.2.s_ref = bf16[8,2,3,2,16,128]{5,4,3,2,1,0:T(8,128)(2,1)S(1)} async-done(((bf16[8,2,3,2,16,128]{5,4,3,2,1,0:T(8,128)(2,1)}), bf16[8,2,3,2,16,128]{5,4,3,2,1,0:T(8,128)(2,1)S(1)}, u32[]{:S(2)}, u32[]{:S(2)}) %all-to-all-start.2) | async-done | bytes 393248 | tf_op jit(solution)/shard_map/all_to_all | solution.py:282
  45.3 0.4 middle.1
  45.7 4.6 %collective-permute-start.4 = (bf16[3,2,128,128]{3,2,1,0:T(8,128)(2,1)S(1)}, bf16[3,2,128,128]{3,2,1,0:T(8,128)(2,1)S(1)}, u32[]{:S(2)}, u32[]{:S(2)}) collective-permute-start(bf16[3,2,128,128]{3,2,1,0:T(8,128)(2,1)S(1)} %get-tuple-element.11), channel_id=1, source_target_pairs={{0,1},{1,2},{2,3},{4,5},{5,6},{6,7},{8,9},{9,10},{10,11},{12,13},{... | collective-permute-start | bytes 589832 | tf_op jit(solution)/shard_map/ppermute | solution.py:324
  50.3 1.3 %collective-permute-start.5 = (bf16[3,2,128,128]{3,2,1,0:T(8,128)(2,1)S(1)}, bf16[3,2,128,128]{3,2,1,0:T(8,128)(2,1)S(1)}, u32[]{:S(2)}, u32[]{:S(2)}) collective-permute-start(bf16[3,2,128,128]{3,2,1,0:T(8,128)(2,1)S(1)} %get-tuple-element.12), channel_id=1, source_target_pairs={{1,0},{2,1},{3,2},{5,4},{6,5},{7,6},{9,8},{10,9},{11,10},{13,12},{... | collective-permute-start | bytes 589832 | tf_op jit(solution)/shard_map/ppermute | solution.py:325
  51.6 4.6 %collective-permute-start.2 = (bf16[2,2,128,128]{3,2,1,0:T(8,128)(2,1)S(1)}, bf16[2,2,128,128]{3,2,1,0:T(8,128)(2,1)S(1)}, u32[]{:S(2)}, u32[]{:S(2)}) collective-permute-start(bf16[2,2,128,128]{3,2,1,0:T(8,128)(2,1)S(1)} %slice_bitcast_fusion), channel_id=1, source_target_pairs={{0,1},{1,2},{2,3},{4,5},{5,6},{6,7},{8,9},{9,10},{10,11},{12,13},{... | collective-permute-start | bytes 393224 | tf_op jit(solution)/shard_map/ppermute | solution.py:309
  56.2 0.0 collective-permute-done.3.gr_ref
  56.2 2.5 %collective-permute-done.2.gl_ref = bf16[2,2,128,128]{3,2,1,0:T(8,128)(2,1)S(1)} collective-permute-done((bf16[2,2,128,128]{3,2,1,0:T(8,128)(2,1)S(1)}, bf16[2,2,128,128]{3,2,1,0:T(8,128)(2,1)S(1)}, u32[]{:S(2)}, u32[]{:S(2)}) %collective-permute-start.2) | collective-permute-done | bytes 131104 | tf_op jit(solution)/shard_map/ppermute | solution.py:309
  58.7 0.0 collective-permute-done.4.sl_ref
  58.7 0.0 collective-permute-done.5.sr_ref
  58.7 1.6 %dressed.1 = bf16[2,3,2,128,128]{4,3,2,1,0:T(8,128)(2,1)} custom-call(bf16[2,3,2,128,128]{4,3,2,1,0:T(8,128)(2,1)S(1)} %bitcast.21, bf16[8,2,3,2,16,128]{5,4,3,2,1,0:T(8,128)(2,1)S(1)} %all-to-all-done.2.s_ref, bf16[2,2,128,128]{3,2,1,0:T(8,128)(2,1)S(1)} %collective-permute-done.2.gl_ref, bf16[2,2,128,128]{3,2,1,0:T(8,128)(2,1)S(1)} %collective-permute-done.3.gr_ref, ...), custom_call_target="tpu_custom_call" | custom-call | flops 570425344 | bytes 1835008 | tf_op jit(solution)/shard_map/dressed/pallas_call | solution.py:254
  (4 shorter events, 0.0 us)
Async XLA Ops:
  0.0 1.0 %copy-start.1 = (bf16[1,2,3,2,128,128]{5,4,3,2,1,0:T(8,128)(2,1)S(1)}, bf16[1,2,3,2,128,128]{5,4,3,2,1,0:T(8,128)(2,1)}, u32[]{:S(2)}) copy-start(bf16[1,2,3,2,128,128]{5,4,3,2,1,0:T(8,128)(2,1)} %param.3) | copy-start | bytes 1179652
  1.0 1.0 %copy-start.3 = (bf16[1,2,3,2,128,128]{5,4,3,2,1,0:T(8,128)(2,1)S(1)}, bf16[1,2,3,2,128,128]{5,4,3,2,1,0:T(8,128)(2,1)}, u32[]{:S(2)}) copy-start(bf16[1,2,3,2,128,128]{5,4,3,2,1,0:T(8,128)(2,1)} %param.4) | copy-start | bytes 1179652
  2.0 6.7 %copy-start = (bf16[1,2,3,2,128,128]{5,4,3,2,1,0:T(8,128)(2,1)S(1)}, bf16[1,2,3,2,128,128]{5,4,3,2,1,0:T(8,128)(2,1)}, u32[]{:S(2)}) copy-start(bf16[1,2,3,2,128,128]{5,4,3,2,1,0:T(8,128)(2,1)} %param.5) | copy-start | bytes 1179652
  2.4 11.9 %collective-permute-start = (bf16[5,2,128,128]{3,2,1,0:T(8,128)(2,1)S(1)}, bf16[5,2,128,128]{3,2,1,0:T(8,128)(2,1)S(1)}, u32[]{:S(2)}, u32[]{:S(2)}) collective-permute-start(bf16[5,2,128,128]{3,2,1,0:T(8,128)(2,1)S(1)} %get-tuple-element.9), channel_id=1, source_target_pairs={{0,1},{1,2},{2,3},{4,5},{5,6},{6,7},{8,9},{9,10},{10,11},{12,13},{... | collective-permute-start | bytes 983048 | tf_op jit(solution)/shard_map/ppermute | solution.py:303
  7.4 11.1 %collective-permute-start.1 = (bf16[5,2,128,128]{3,2,1,0:T(8,128)(2,1)S(1)}, bf16[5,2,128,128]{3,2,1,0:T(8,128)(2,1)S(1)}, u32[]{:S(2)}, u32[]{:S(2)}) collective-permute-start(bf16[5,2,128,128]{3,2,1,0:T(8,128)(2,1)S(1)} %get-tuple-element.10), channel_id=1, source_target_pairs={{1,0},{2,1},{3,2},{5,4},{6,5},{7,6},{9,8},{10,9},{11,10},{13,12},{... | collective-permute-start | bytes 983048 | tf_op jit(solution)/shard_map/ppermute | solution.py:304
  9.5 9.0 %copy-start.2 = (bf16[1,2,3,2,128,128]{5,4,3,2,1,0:T(8,128)(2,1)S(1)}, bf16[1,2,3,2,128,128]{5,4,3,2,1,0:T(8,128)(2,1)}, u32[]{:S(2)}) copy-start(bf16[1,2,3,2,128,128]{5,4,3,2,1,0:T(8,128)(2,1)} %param.3) | copy-start | bytes 1179652
  9.5 9.0 %copy-start.4 = (bf16[1,2,3,2,128,128]{5,4,3,2,1,0:T(8,128)(2,1)S(1)}, bf16[1,2,3,2,128,128]{5,4,3,2,1,0:T(8,128)(2,1)}, u32[]{:S(2)}) copy-start(bf16[1,2,3,2,128,128]{5,4,3,2,1,0:T(8,128)(2,1)} %param.4) | copy-start | bytes 1179652
  9.5 12.2 %all-to-all-start = ((bf16[8,2,3,2,16,128]{5,4,3,2,1,0:T(8,128)(2,1)}), bf16[8,2,3,2,16,128]{5,4,3,2,1,0:T(8,128)(2,1)S(1)}, u32[]{:S(2)}, u32[]{:S(2)}) async-start(bf16[8,2,3,2,16,128]{5,4,3,2,1,0:T(8,128)(2,1)} %bitcast.16), calls=%async_computation | async-start | bytes 786432 | tf_op jit(solution)/shard_map/all_to_all | solution.py:282
  33.6 11.7 %all-to-all-start.2 = ((bf16[8,2,3,2,16,128]{5,4,3,2,1,0:T(8,128)(2,1)}), bf16[8,2,3,2,16,128]{5,4,3,2,1,0:T(8,128)(2,1)S(1)}, u32[]{:S(2)}, u32[]{:S(2)}) async-start(bf16[8,2,3,2,16,128]{5,4,3,2,1,0:T(8,128)(2,1)} %bitcast.7), calls=%async_computation.2 | async-start | bytes 786432 | tf_op jit(solution)/shard_map/all_to_all | solution.py:282
  37.1 19.0 %collective-permute-start.3 = (bf16[2,2,128,128]{3,2,1,0:T(8,128)(2,1)S(1)}, bf16[2,2,128,128]{3,2,1,0:T(8,128)(2,1)S(1)}, u32[]{:S(2)}, u32[]{:S(2)}) collective-permute-start(bf16[2,2,128,128]{3,2,1,0:T(8,128)(2,1)S(1)} %pad_maximum_fusion), channel_id=1, source_target_pairs={{1,0},{2,1},{3,2},{5,4},{6,5},{7,6},{9,8},{10,9},{11,10},{13,12},{... | collective-permute-start | bytes 393224 | tf_op jit(solution)/shard_map/ppermute | solution.py:310
  45.7 12.9 %collective-permute-start.4 = (bf16[3,2,128,128]{3,2,1,0:T(8,128)(2,1)S(1)}, bf16[3,2,128,128]{3,2,1,0:T(8,128)(2,1)S(1)}, u32[]{:S(2)}, u32[]{:S(2)}) collective-permute-start(bf16[3,2,128,128]{3,2,1,0:T(8,128)(2,1)S(1)} %get-tuple-element.11), channel_id=1, source_target_pairs={{0,1},{1,2},{2,3},{4,5},{5,6},{6,7},{8,9},{9,10},{10,11},{12,13},{... | collective-permute-start | bytes 589832 | tf_op jit(solution)/shard_map/ppermute | solution.py:324
  50.3 8.4 %collective-permute-start.5 = (bf16[3,2,128,128]{3,2,1,0:T(8,128)(2,1)S(1)}, bf16[3,2,128,128]{3,2,1,0:T(8,128)(2,1)S(1)}, u32[]{:S(2)}, u32[]{:S(2)}) collective-permute-start(bf16[3,2,128,128]{3,2,1,0:T(8,128)(2,1)S(1)} %get-tuple-element.12), channel_id=1, source_target_pairs={{1,0},{2,1},{3,2},{5,4},{6,5},{7,6},{9,8},{10,9},{11,10},{13,12},{... | collective-permute-start | bytes 589832 | tf_op jit(solution)/shard_map/ppermute | solution.py:325
  51.6 7.1 %collective-permute-start.2 = (bf16[2,2,128,128]{3,2,1,0:T(8,128)(2,1)S(1)}, bf16[2,2,128,128]{3,2,1,0:T(8,128)(2,1)S(1)}, u32[]{:S(2)}, u32[]{:S(2)}) collective-permute-start(bf16[2,2,128,128]{3,2,1,0:T(8,128)(2,1)S(1)} %slice_bitcast_fusion), channel_id=1, source_target_pairs={{0,1},{1,2},{2,3},{4,5},{5,6},{6,7},{8,9},{9,10},{10,11},{12,13},{... | collective-permute-start | bytes 393224 | tf_op jit(solution)/shard_map/ppermute | solution.py:309

commit v2 on v1

v2 whole, which is shorter than its diff:
```python
import functools

import jax
import jax.numpy as jnp
from jax import lax
from jax.experimental import pallas as pl
from jax.experimental.pallas import tpu as pltpu
from jax.sharding import PartitionSpec as P


BF16 = jnp.bfloat16
F32 = jnp.float32
VMEM = pl.BlockSpec(memory_space=pltpu.VMEM)
PACK = 16


def row_form(real, imag):
    return jnp.concatenate([real, imag], axis=1)


def square_form(real, imag):
    return jnp.concatenate([row_form(real, imag), row_form(-imag, real)], axis=0)


def times(lhs, rhs):
    return jnp.dot(lhs, rhs, preferred_element_type=F32)


def times_adjoint(lhs, rhs):
    return lax.dot_general(lhs, rhs, (((1,), (1,)), ((), ())), preferred_element_type=F32)


def edge_mask(block, is_edge):
    return jnp.where(is_edge, jnp.zeros_like(block), block)


class Band:
    def __init__(self, load):
        self.load = load

    def pair(self, row, col):
        return self.load(row, col - row + 1, 0), self.load(row, col - row + 1, 1)

    def row(self, row, col):
        return row_form(*self.pair(row, col))

    def square(self, row, col):
        return square_form(*self.pair(row, col))


def plain_load(ref):
    return lambda i, t, c: ref[i, t, c]


def own_adjoint(outer, inner, row):
    total = None
    for col in range(row - 1, row + 2):
        term = times_adjoint(inner.row(row, col), outer.square(row, col))
        total = term if total is None else total + term
    return total.astype(BF16)


def split_store(ref, index, value):
    half = value.shape[1] // 2
    ref[index, 0] = value[:, :half]
    ref[index, 1] = value[:, half:]


def copy_pair(ref, index, pair):
    ref[index, 0] = pair[0]
    ref[index, 1] = pair[1]


def neighbours(place, rows):
    return [i for i in range(max(place - 1, 0), min(place + 2, rows))]


def chunks(value, count):
    size = value.shape[0] // count
    return [value[place * size : (place + 1) * size] for place in range(count)]


def sandwich_local(outer, inner, rows, store, store_edge):
    partial = {}
    for mid in range(rows):
        users = neighbours(mid, rows)
        lhs = jnp.concatenate([outer.row(i, mid) for i in users], axis=0)
        for col in range(mid - 1, mid + 2):
            for i, part in zip(users, chunks(times(lhs, inner.square(mid, col)), len(users))):
                partial[i, col] = partial[i, col] + part if (i, col) in partial else part
    partial = {key: value.astype(BF16) for key, value in partial.items()}
    for target in range(rows):
        users = neighbours(target, rows)
        total = None
        for col in range(target - 1, target + 2):
            wanted = [i for i in users if (i, col) in partial]
            if wanted != users:
                zero = jnp.zeros_like(partial[target, target])
                lhs = jnp.concatenate([partial.get((i, col), zero) for i in users], axis=0)
            else:
                lhs = jnp.concatenate([partial[i, col] for i in users], axis=0)
            term = times_adjoint(lhs, outer.square(target, col))
            total = term if total is None else total + term
        for i, part in zip(users, chunks(total, len(users))):
            store(i, target - i + 1, part)
    for side, row, edge in ((0, 0, -1), (1, rows - 1, rows)):
        store_edge(side, 0, partial[row, edge])
        store_edge(side, 1, partial[row, row])


def sandwich_cross(outer, rows, sides, missing, load, load_edge, store):
    added = {}
    for side, row, edge in ((0, 0, -1), (1, rows - 1, rows)):
        get = sides[side]
        link = edge_mask(outer.row(row, edge), missing[side])
        through = times(link, square_form(*get("inner", 0))).astype(BF16)
        direct = times(link, square_form(*get("inner", 1))).astype(BF16)
        beyond = times(link, square_form(*get("adjoint", 0)))
        beyond += times_adjoint(load_edge(side, 0), square_form(*get("outer", 0)))
        beyond += times_adjoint(load_edge(side, 1), square_form(*get("outer", 1)))
        store(row, edge - row + 1, edge_mask(beyond.astype(BF16), missing[side]))
        for target in neighbours(row, rows):
            term = times_adjoint(direct, outer.square(target, row))
            if target == row:
                term += times_adjoint(through, outer.square(row, edge))
            key = (row, target)
            added[key] = added[key] + term if key in added else term
    for i in range(rows):
        for target in neighbours(i, rows):
            value = load(i, target - i + 1)
            if (i, target) in added:
                value = value + added[i, target]
            store(i, target - i + 1, value.astype(BF16))


def pairs_of(start, peers, count):
    mate = {i: i + 1 for i in range(start, peers - 1, 2)}
    mate.update({j: i for i, j in mate.items()})
    return [
        (e * peers + z, e * peers + mate[z] if z in mate else (e ^ 1) * peers + z)
        for e in range(count)
        for z in range(peers)
    ]


def edges(space):
    place = lax.axis_index(space)
    return place == 0, place == lax.axis_size(space) - 1


def owner():
    index = lax.axis_index("energy")
    return lax.shift_right_logical(index, 1), lax.bitwise_and(index, 1)


def outer_band(ref):
    return Band(plain_load(ref))


def by_turn(even_case, odd_case):
    even = lax.rem(lax.axis_index("space"), 2) == 0
    pl.when(even)(even_case)
    pl.when(jnp.logical_not(even))(odd_case)


def ends(ref):
    rows = ref.shape[0]
    return (rows - 1, rows), (0, -1)


def fill_near(outer_ref, inner_ref, first_ref, second_ref):
    def fill(*refs):
        outer, inner = outer_band(outer_ref), outer_band(inner_ref) if inner_ref is not None else None
        for ref, (row, cross) in zip(refs, ends(outer_ref)):
            if inner is None:
                copy_pair(ref, 0, outer.pair(row, row))
                copy_pair(ref, 1, outer.pair(row, cross))
                continue
            copy_pair(ref, 0, inner.pair(row, row))
            copy_pair(ref, 1, inner.pair(row, cross))
            split_store(ref, 2, own_adjoint(outer, inner, row))
            if ref.shape[0] > 3:
                copy_pair(ref, 3, outer.pair(row, row))
                copy_pair(ref, 4, outer.pair(row, cross))

    by_turn(lambda: fill(first_ref, second_ref), lambda: fill(second_ref, first_ref))


def send_kernel(w_hbm, p_hbm, first_ref, second_ref, w_ref, p_ref, sems):
    copies = [pltpu.make_async_copy(a, b, sems.at[n]) for n, (a, b) in enumerate(((w_hbm, w_ref), (p_hbm, p_ref)))]
    for copy in copies:
        copy.start()
    for copy in copies:
        copy.wait()
    start, end = edges("space")

    @pl.when(start)
    def _():
        p_ref[0, 0] = jnp.zeros(p_ref.shape[2:], BF16)

    @pl.when(end)
    def _():
        p_ref[p_ref.shape[0] - 1, 2] = jnp.zeros(p_ref.shape[2:], BF16)

    fill_near(w_ref, p_ref, first_ref, second_ref)


def side_of(inner_ref, adjoint_at, outer_ref, outer_at):
    def side(kind, which):
        ref, at = {"inner": (inner_ref, 0), "adjoint": (inner_ref, adjoint_at), "outer": (outer_ref, outer_at)}[kind]
        return ref[at + which, 0], ref[at + which, 1]

    return side


def local_kernel(w_ref, p_ref, sum_ref, edge_ref):
    def store(i, t, value):
        sum_ref[i, t] = value

    def store_edge(side, n, value):
        edge_ref[side, n] = value

    sandwich_local(outer_band(w_ref), outer_band(p_ref), w_ref.shape[0], store, store_edge)


def cross_terms(outer_ref, sum_ref, edge_ref, near, out_ref):
    def run(below, above):
        sandwich_cross(
            outer_band(outer_ref),
            outer_ref.shape[0],
            [side_of(below[0], 2, *below[1:]), side_of(above[0], 2, *above[1:])],
            edges("space"),
            lambda i, t: sum_ref[i, t],
            lambda side, n: edge_ref[side, n],
            lambda i, t, value: split_store(out_ref.at[i], t, value),
        )

    by_turn(lambda: run(near[1], near[0]), lambda: run(near[0], near[1]))


def piece_rows(slot, size):
    return pl.ds(pl.multiple_of(slot * size, size), size)


def screened_kernel(w_ref, sum_ref, edge_ref, first_ref, second_ref, *rest):
    *out_refs, whole_ref = rest
    chip, _ = owner()
    cross_terms(w_ref, sum_ref, edge_ref, [(ref, ref, 3) for ref in (first_ref, second_ref)], whole_ref)
    size = out_refs[0].shape[3]
    if len(out_refs) == 1:
        out_refs[0][...] = whole_ref[...]
    else:
        for s, ref in enumerate(out_refs):
            ref[...] = whole_ref[:, :, :, piece_rows(chip ^ s, size), :]


def split_kernel(g_ref, first_ref, second_ref, *out_refs):
    chip, _ = owner()
    fill_near(g_ref, None, first_ref, second_ref)
    if len(out_refs) > 1:
        size = out_refs[0].shape[3]
        for s, ref in enumerate(out_refs):
            ref[...] = g_ref[:, :, :, piece_rows(chip ^ s, size), :]


def order_kernel(chips, *refs):
    chip, place = owner()
    out_ref = refs[-1]
    out_ref[0] = jnp.zeros(out_ref.shape[1:], BF16)
    for s in range(chips):
        out_ref[2 * (chip ^ s) + place + 1] = refs[s][...]
        out_ref[2 * (chip ^ s) + (1 - place) + 1] = refs[chips + s][...]


def convolve_kernel(chips, factor, g_ref, *refs):
    chip, place = owner()
    own, other = refs[:chips], refs[chips : 2 * chips]
    outs, s_ref, o_ref = refs[2 * chips : 3 * chips], refs[-2], refs[-1]
    groups = s_ref.shape[1]
    for s in range(chips):
        s_ref[2 * (chip ^ s) + place] = own[s][...]
        s_ref[2 * (chip ^ s) + (1 - place)] = other[s][...]

    def load(ref, e, a, c, span):
        return ref[e, a, c, span].astype(F32)

    def result(x, a, span, sums):
        o_ref[x, a, 0, span] = ((sums[0] - sums[1]) * factor).astype(BF16)
        o_ref[x, a, 1, span] = ((sums[2] + sums[3]) * factor).astype(BF16)

    def add(sums, g_real, g_imag, s_real, s_imag):
        terms = (g_real * s_real, g_imag * s_imag, g_real * s_imag, g_imag * s_real)
        return terms if sums is None else tuple(a + b for a, b in zip(sums, terms))

    height = s_ref.shape[3]
    step = PACK if height % PACK == 0 else height
    if chips <= PACK:
        for a in range(groups):
            for start in range(0, height, step):
                span = slice(start, start + step)
                g = [[(load(g_ref, 2 * j + place + 1 - d, a, 0, span), load(g_ref, 2 * j + place + 1 - d, a, 1, span)) for j in range(chips)] for d in range(2)]
                for x in range(chips):
                    sums = None
                    for k in range(x + 1):
                        for d in range(2):
                            sums = add(sums, *g[d][x - k], load(s_ref, 2 * k + d, a, 0, span), load(s_ref, 2 * k + d, a, 1, span))
                    result(x, a, span, sums)
    else:
        for a in range(groups):
            span = slice(0, height)

            def energy(x, carry):
                def term(k, sums):
                    for d in range(2):
                        e = 2 * (x - k) + place + 1 - d
                        sums = add(sums, load(g_ref, e, a, 0, span), load(g_ref, e, a, 1, span), load(s_ref, 2 * k + d, a, 0, span), load(s_ref, 2 * k + d, a, 1, span))
                    return sums

                zero = jnp.zeros(s_ref.shape[3:], F32)
                result(x, a, span, lax.fori_loop(0, x + 1, term, (zero,) * 4))
                return carry

            lax.fori_loop(0, chips, energy, 0)
    for s in range(chips):
        outs[s][...] = o_ref[chip ^ s]


def middle_kernel(pieces, g_ref, *refs):
    first_ref, second_ref, sigma_ref = refs[pieces:]
    if pieces == 1:
        sigma_ref[...] = refs[0][...]
    else:
        chip, _ = owner()
        for s in range(pieces):
            sigma_ref[:, :, :, piece_rows(chip ^ s, refs[s].shape[3]), :] = refs[s][...]
    fill_near(g_ref, sigma_ref, first_ref, second_ref)


def dressed_kernel(g_ref, sum_ref, edge_ref, g_first_ref, g_second_ref, s_first_ref, s_second_ref, out_ref):
    near = [(s_first_ref, g_first_ref, 0), (s_second_ref, g_second_ref, 0)]
    cross_terms(g_ref, sum_ref, edge_ref, near, out_ref)


HBM = pl.BlockSpec(memory_space=pltpu.HBM)


def call(kernel, shapes, *args, flops=0, scratch=(), in_hbm=False):
    outs = tuple(jax.ShapeDtypeStruct(s[0], s[1]) if isinstance(s[0], tuple) else jax.ShapeDtypeStruct(s, BF16) for s in shapes)
    moved = sum(2 * a.size for a in args) + sum(2 * o.size for o in outs)
    single = len(outs) == 1
    return pl.pallas_call(
        kernel,
        out_shape=outs[0] if single else outs,
        in_specs=[HBM if in_hbm else VMEM] * len(args),
        out_specs=VMEM if single else tuple([VMEM] * len(outs)),
        scratch_shapes=list(scratch),
        cost_estimate=pl.CostEstimate(flops=flops, bytes_accessed=moved, transcendentals=0),
        compiler_params=pltpu.CompilerParams(vmem_limit_bytes=32 * 1024 * 1024),
    )(*args)


def local(screening, polarization, propagator):
    w, p, g = screening[0], polarization[0], propagator[0]
    rows, bands, parts, order = w.shape[0], w.shape[1], w.shape[2], w.shape[3]
    peers, count = lax.axis_size("space"), lax.axis_size("energy")
    turns = [pairs_of(start, peers, count) for start in range(2)]
    chips = count // 2
    piece = order // chips
    inside = piece % PACK == 0
    block = 8 * order**3
    chip, _ = owner()
    whole, part = (rows, bands, parts, order, order), (rows, bands, parts, piece, order)
    sums = [((rows, bands, order, 2 * order), F32), ((2, 2, order, 2 * order), BF16)]

    def pieces_of(x):
        cut = x.reshape(rows, bands, parts, chips, piece, order)
        return [lax.dynamic_index_in_dim(cut, chip ^ s, 3, keepdims=False) for s in range(chips)]

    def joined(pieces):
        order_of = jnp.arange(chips, dtype=jnp.int32) ^ chip
        return jnp.moveaxis(jnp.stack(pieces)[order_of], 0, 3).reshape(whole)

    def flat(x):
        if inside:
            return x.reshape(rows * bands, parts, piece, order)
        return jnp.moveaxis(x, 2, 0).reshape(1, parts, rows * bands * piece, order)

    def unflat(x):
        if inside:
            return x.reshape(part)
        return jnp.moveaxis(x.reshape(parts, rows, bands, piece, order), 0, 2)

    def trade(first, second):
        return [lax.ppermute(x, ("energy", "space"), pairs) for x, pairs in zip((first, second), turns)]

    def to_chip(x, s):
        return lax.ppermute(x, "energy", [(i, i ^ (2 * s)) for i in range(count)]) if s else x

    def to_partner(x):
        return lax.ppermute(x, "energy", [(i, i ^ 1) for i in range(count)])

    def to_owners(pieces):
        own = [flat(to_chip(x, s)) for s, x in enumerate(pieces)]
        return own, [to_partner(x) for x in own]

    cut = [part] * chips if inside else [whole]
    first_buf, second_buf, w_in, p_in = call(
        send_kernel, [(5, parts, order, order)] * 2 + [whole] * 2, w, p, flops=6 * block,
        scratch=[pltpu.SemaphoreType.DMA((2,))], in_hbm=True,
    )
    near_w = trade(first_buf, second_buf)

    near = [(2, parts, order, order)] * 2
    g_first, g_second, *g_pieces = call(split_kernel, near + (cut if inside else []), g)
    g_own, g_other = to_owners(g_pieces if inside else pieces_of(g))
    flat_shape = g_own[0].shape
    g_all = call(functools.partial(order_kernel, chips), [(count + 1,) + flat_shape], *g_own, *g_other)
    near_g = trade(g_first, g_second)

    w_sums, w_edge = call(local_kernel, sums, w_in, p_in, flops=24 * block)
    screened = call(
        screened_kernel, cut, w_in, w_sums, w_edge, *near_w, flops=16 * block,
        scratch=[pltpu.VMEM(whole, BF16)],
    )
    s_own, s_other = to_owners(screened if inside else pieces_of(screened))
    factor = (3.0 * order / count) ** 0.5
    owned = [pltpu.VMEM((size,) + flat_shape, BF16) for size in (count, chips)]
    sigma = call(
        functools.partial(convolve_kernel, chips, factor), [flat_shape] * chips, g_all, *s_own, *s_other,
        scratch=owned,
    )
    sigma = [to_chip(unflat(x), s) for s, x in enumerate(sigma)]
    sigma = sigma if inside else [joined(sigma)]

    first_buf, second_buf, sigma = call(
        functools.partial(middle_kernel, len(sigma)), [(3, parts, order, order)] * 2 + [whole], g, *sigma,
        flops=6 * block,
    )
    near_s = trade(first_buf, second_buf)
    g_sums, g_edge = call(local_kernel, sums, g, sigma, flops=24 * block)
    out = call(dressed_kernel, [whole], g, g_sums, g_edge, *near_g, *near_s, flops=16 * block)
    return out[None]


def solution(mesh):
    spec = P("energy", "space", None, None, None, None)

    return jax.shard_map(local, mesh=mesh, in_specs=(spec, spec, spec), out_specs=spec, check_vma=False)
```

time: 60.8 us -> 45.1 us (0.74)
  blocking collectives: 10.7 us -> 0 us
  starting transfers between devices: 25.3 us -> 21.5 us
  local copies, waits for them, and re-layouts: 2.8 us -> 1.99 us
  waiting for transfers between devices: 16.8 us -> 16 us
  Pallas kernels: 4.57 us -> 5.2 us
    all_to_all x1 -> x0, blocking collectives: 10.7 us -> none  [exchange(): return lax.all_to_all(x, 'energy', 0, 0, tiled=True)]
    all_to_all x2 -> x0, waiting for transfers between devices: 9.22 us -> none  [exchange(): return lax.all_to_all(x, 'energy', 0, 0, tiled=True)]
    ppermute x6 -> x23, waiting for transfers between devices: 7.6 us -> 16 us  [the longest x9 10.5 us: to_chip(): lax.ppermute(x, 'energy', [(i, i ^ 2 * s) for i in range(count)])]
    all_to_all x2 -> x0, starting transfers between devices: 7.31 us -> none  [exchange(): return lax.all_to_all(x, 'energy', 0, 0, tiled=True)]
    ppermute x6 -> x23, starting transfers between devices: 18 us -> 21.5 us  [the longest x9 12.7 us: to_chip(): lax.ppermute(x, 'energy', [(i, i ^ 2 * s) for i in range(count)])]
    another operation x2 -> x0, local copies, waits for them, and re-layouts: 0.79 us -> none  [the longest x1 0.78 us: local(): g.reshape(rows, bands, parts, count, piece, order)]
    pallas_call x5 -> x9, Pallas kernels: 4.57 us -> 5.2 us  [call(): pl.pallas_call(kernel, out_shape=outs[0] if single else outs, in_specs=[H...]
    unnamed x10 -> x6, local copies, waits for them, and re-layouts: 2 us -> 1.99 us
  transfers between devices with their start and end apart: 8 -> 23, of which waited for: 5 -> 9; matrix products, arithmetic and copies ran while one was open for 1% -> 0% of each run, Pallas kernels for 2% -> 5%
where the time goes in v2:
time: 45.1 us; the launch traced here: 44.9 us
  starting transfers between devices  21.5 us (48%)
  waiting for transfers between devices  16 us (35%)
  Pallas kernels  5.2 us (12%)
  local copies, waits for them, and re-layouts  1.99 us (4%)
    ppermute x9, starting transfers between devices, to_chip(): lax.ppermute(x, 'energy', [(i, i ^ 2 * s) for i in range(count)])  12.7 us
    ppermute x9, waiting for transfers between devices, to_chip(): lax.ppermute(x, 'energy', [(i, i ^ 2 * s) for i in range(count)])  10.5 us
    ppermute x6, starting transfers between devices, trade(): lax.ppermute(x, ('energy', 'space'), pairs)  7.8 us
    pallas_call x9, Pallas kernels, call(): pl.pallas_call(kernel, out_shape=outs[0] if single else outs, in_specs=[H...  5.2 us
    ppermute x6, waiting for transfers between devices, trade(): lax.ppermute(x, ('energy', 'space'), pairs)  4.36 us
    unnamed x6, local copies, waits for them, and re-layouts  1.99 us
    ppermute x8, waiting for transfers between devices, to_partner(): return lax.ppermute(x, 'energy', [(i, i ^ 1) for i in range(count)])  1.22 us
    ppermute x8, starting transfers between devices, to_partner(): return lax.ppermute(x, 'energy', [(i, i ^ 1) for i in range(count)])  1.08 us
  transfers between devices with their start and end apart: 23, of which 9 were waited for; matrix products, arithmetic and copies ran while one was open for 0% of the time, Pallas kernels for 5%

profile of v2, /device:TPU:0, one launch (start us, length us, event | category | flops | bytes accessed | tf_op | source)
XLA Modules:
  0.0 44.9 jit_solution(5756168060632586944)
XLA Ops:
  0.0 1.0 %copy-done.1 = bf16[1,2,3,2,128,128]{5,4,3,2,1,0:T(8,128)(2,1)S(1)} copy-done((bf16[1,2,3,2,128,128]{5,4,3,2,1,0:T(8,128)(2,1)S(1)}, bf16[1,2,3,2,128,128]{5,4,3,2,1,0:T(8,128)(2,1)}, u32[]{:S(2)}) %copy-start.1) | copy-done | bytes 393240
  1.0 1.0 %copy-done.2 = bf16[1,2,3,2,128,128]{5,4,3,2,1,0:T(8,128)(2,1)S(1)} copy-done((bf16[1,2,3,2,128,128]{5,4,3,2,1,0:T(8,128)(2,1)S(1)}, bf16[1,2,3,2,128,128]{5,4,3,2,1,0:T(8,128)(2,1)}, u32[]{:S(2)}) %copy-start.2) | copy-done | bytes 393240
  2.0 0.8 %shard_map.39 = (bf16[5,2,128,128]{3,2,1,0:T(8,128)(2,1)S(1)}, bf16[5,2,128,128]{3,2,1,0:T(8,128)(2,1)S(1)}, bf16[2,3,2,128,128]{4,3,2,1,0:T(8,128)(2,1)S(1)}, bf16[2,3,2,128,128]{4,3,2,1,0:T(8,128)(2,1)S(1)}) custom-call(bf16[2,3,2,128,128]{4,3,2,1,0:T(8,128)(2,1)S(1)} %bitcast.20, bf16[2,3,2,128,128]{4,3,2,1,0:T(8,128)(2,1)S(1)} %bitcast.21), custom_call_target="tpu_custom_call" | custom-call | flops 100663296 | bytes 2228224 | tf_op jit(solution)/shard_map/pallas_call | solution.py:351
  2.8 3.1 %collective-permute-start.7 = (bf16[5,2,128,128]{3,2,1,0:T(8,128)(2,1)S(1)}, bf16[5,2,128,128]{3,2,1,0:T(8,128)(2,1)S(1)}, u32[]{:S(2)}, u32[]{:S(2)}) collective-permute-start(bf16[5,2,128,128]{3,2,1,0:T(8,128)(2,1)S(1)} %get-tuple-element.38), channel_id=1, source_target_pairs={{0,1},{1,0},{2,3},{3,2},{4,5},{5,4},{6,7},{7,6},{8,9},{9,8},{10,11... | collective-permute-start | bytes 983048 | tf_op jit(solution)/shard_map/ppermute | solution.py:394
  6.0 1.6 %collective-permute-start = (bf16[2,3,2,32,128]{4,3,2,1,0:T(8,128)(2,1)S(1)}, bf16[2,3,2,32,128]{4,3,2,1,0:T(8,128)(2,1)S(1)}, u32[]{:S(2)}, u32[]{:S(2)}) collective-permute-start(bf16[2,3,2,32,128]{4,3,2,1,0:T(8,128)(2,1)S(1)} %get-tuple-element.31), channel_id=1, source_target_pairs={{0,8},{4,12},{8,0},{12,4},{16,24},{20,28},{24,16},{28,20},{1,9},{5... | collective-permute-start | bytes 294920 | tf_op jit(solution)/shard_map/ppermute | solution.py:397
  7.5 1.5 %collective-permute-start.1 = (bf16[2,3,2,32,128]{4,3,2,1,0:T(8,128)(2,1)S(1)}, bf16[2,3,2,32,128]{4,3,2,1,0:T(8,128)(2,1)S(1)}, u32[]{:S(2)}, u32[]{:S(2)}) collective-permute-start(bf16[2,3,2,32,128]{4,3,2,1,0:T(8,128)(2,1)S(1)} %get-tuple-element.32), channel_id=1, source_target_pairs={{0,16},{4,20},{8,24},{12,28},{16,0},{20,4},{24,8},{28,12},{1,17},{... | collective-permute-start | bytes 294920 | tf_op jit(solution)/shard_map/ppermute | solution.py:397
  9.1 2.2 %collective-permute-done = bf16[2,3,2,32,128]{4,3,2,1,0:T(8,128)(2,1)S(1)} collective-permute-done((bf16[2,3,2,32,128]{4,3,2,1,0:T(8,128)(2,1)S(1)}, bf16[2,3,2,32,128]{4,3,2,1,0:T(8,128)(2,1)S(1)}, u32[]{:S(2)}, u32[]{:S(2)}) %collective-permute-start) | collective-permute-done | bytes 98336 | tf_op jit(solution)/shard_map/ppermute | solution.py:397
  11.3 2.4 %collective-permute-start.2 = (bf16[2,3,2,32,128]{4,3,2,1,0:T(8,128)(2,1)S(1)}, bf16[2,3,2,32,128]{4,3,2,1,0:T(8,128)(2,1)S(1)}, u32[]{:S(2)}, u32[]{:S(2)}) collective-permute-start(bf16[2,3,2,32,128]{4,3,2,1,0:T(8,128)(2,1)S(1)} %get-tuple-element.33), channel_id=1, source_target_pairs={{0,24},{4,28},{8,16},{12,20},{16,8},{20,12},{24,0},{28,4},{1,25},{... | collective-permute-start | bytes 294920 | tf_op jit(solution)/shard_map/ppermute | solution.py:397
  13.7 0.6 %shard_map.40 = (f32[2,3,128,256]{3,2,1,0:T(8,128)S(1)}, bf16[2,2,128,256]{3,2,1,0:T(8,128)(2,1)S(1)}) custom-call(bf16[2,3,2,128,128]{4,3,2,1,0:T(8,128)(2,1)S(1)} %get-tuple-element.34.w_ref, bf16[2,3,2,128,128]{4,3,2,1,0:T(8,128)(2,1)S(1)} %get-tuple-element.35.p_ref), custom_call_target="tpu_custom_call" | custom-call | flops 402653184 | bytes 1441792 | tf_op jit(solution)/shard_map/pallas_call | solution.py:351
  14.4 0.5 %collective-permute-start.5 = (bf16[6,2,32,128]{3,2,1,0:T(8,128)(2,1)S(1)}, bf16[6,2,32,128]{3,2,1,0:T(8,128)(2,1)S(1)}, u32[]{:S(2)}, u32[]{:S(2)}) collective-permute-start(bf16[6,2,32,128]{3,2,1,0:T(8,128)(2,1)S(1)} %bitcast.26), channel_id=1, source_target_pairs={{0,4},{4,0},{8,12},{12,8},{16,20},{20,16},{24,28},{28,24},{1,5},{5... | collective-permute-start | bytes 294920 | tf_op jit(solution)/shard_map/ppermute | solution.py:400
  14.9 0.7 %shard_map.41 = (bf16[2,3,2,32,128]{4,3,2,1,0:T(8,128)(2,1)S(1)}, bf16[2,3,2,32,128]{4,3,2,1,0:T(8,128)(2,1)S(1)}, bf16[2,3,2,32,128]{4,3,2,1,0:T(8,128)(2,1)S(1)}, bf16[2,3,2,32,128]{4,3,2,1,0:T(8,128)(2,1)S(1)}) custom-call(bf16[2,3,2,128,128]{4,3,2,1,0:T(8,128)(2,1)S(1)} %get-tuple-element.34.w_ref, f32[2,3,128,256]{3,2,1,0:T(8,128)S(1)} %get-tuple-element.36.sum_ref, ...), custom_call_target="tpu_custom_call" | custom-call | flops 268435456 | bytes 2097152 | tf_op jit(solution)/shard_map/pallas_call | solution.py:351
  15.6 0.6 %collective-permute-start.9 = (bf16[2,3,2,32,128]{4,3,2,1,0:T(8,128)(2,1)S(1)}, bf16[2,3,2,32,128]{4,3,2,1,0:T(8,128)(2,1)S(1)}, u32[]{:S(2)}, u32[]{:S(2)}) collective-permute-start(bf16[2,3,2,32,128]{4,3,2,1,0:T(8,128)(2,1)S(1)} %get-tuple-element.41), channel_id=1, source_target_pairs={{0,8},{4,12},{8,0},{12,4},{16,24},{20,28},{24,16},{28,20},{1,9},{5... | collective-permute-start | bytes 294920 | tf_op jit(solution)/shard_map/ppermute | solution.py:397
  16.2 1.4 %collective-permute-start.10 = (bf16[2,3,2,32,128]{4,3,2,1,0:T(8,128)(2,1)S(1)}, bf16[2,3,2,32,128]{4,3,2,1,0:T(8,128)(2,1)S(1)}, u32[]{:S(2)}, u32[]{:S(2)}) collective-permute-start(bf16[2,3,2,32,128]{4,3,2,1,0:T(8,128)(2,1)S(1)} %get-tuple-element.42), channel_id=1, source_target_pairs={{0,16},{4,20},{8,24},{12,28},{16,0},{20,4},{24,8},{28,12},{1,17},{... | collective-permute-start | bytes 294920 | tf_op jit(solution)/shard_map/ppermute | solution.py:397
  17.6 1.6 %collective-permute-start.11 = (bf16[2,3,2,32,128]{4,3,2,1,0:T(8,128)(2,1)S(1)}, bf16[2,3,2,32,128]{4,3,2,1,0:T(8,128)(2,1)S(1)}, u32[]{:S(2)}, u32[]{:S(2)}) collective-permute-start(bf16[2,3,2,32,128]{4,3,2,1,0:T(8,128)(2,1)S(1)} %get-tuple-element.43), channel_id=1, source_target_pairs={{0,24},{4,28},{8,16},{12,20},{16,8},{20,12},{24,0},{28,4},{1,25},{... | collective-permute-start | bytes 294920 | tf_op jit(solution)/shard_map/ppermute | solution.py:397
  19.2 0.5 %collective-permute-start.12 = (bf16[6,2,32,128]{3,2,1,0:T(8,128)(2,1)S(1)}, bf16[6,2,32,128]{3,2,1,0:T(8,128)(2,1)S(1)}, u32[]{:S(2)}, u32[]{:S(2)}) collective-permute-start(bf16[6,2,32,128]{3,2,1,0:T(8,128)(2,1)S(1)} %bitcast.30), channel_id=1, source_target_pairs={{0,4},{4,0},{8,12},{12,8},{16,20},{20,16},{24,28},{28,24},{1,5},{5... | collective-permute-start | bytes 294920 | tf_op jit(solution)/shard_map/ppermute | solution.py:400
  19.7 1.1 %collective-permute-done.9 = bf16[2,3,2,32,128]{4,3,2,1,0:T(8,128)(2,1)S(1)} collective-permute-done((bf16[2,3,2,32,128]{4,3,2,1,0:T(8,128)(2,1)S(1)}, bf16[2,3,2,32,128]{4,3,2,1,0:T(8,128)(2,1)S(1)}, u32[]{:S(2)}, u32[]{:S(2)}) %collective-permute-start.9) | collective-permute-done | bytes 98336 | tf_op jit(solution)/shard_map/ppermute | solution.py:397
  20.9 1.3 %collective-permute-done.10 = bf16[2,3,2,32,128]{4,3,2,1,0:T(8,128)(2,1)S(1)} collective-permute-done((bf16[2,3,2,32,128]{4,3,2,1,0:T(8,128)(2,1)S(1)}, bf16[2,3,2,32,128]{4,3,2,1,0:T(8,128)(2,1)S(1)}, u32[]{:S(2)}, u32[]{:S(2)}) %collective-permute-start.10) | collective-permute-done | bytes 98336 | tf_op jit(solution)/shard_map/ppermute | solution.py:397
  22.2 1.0 %collective-permute-done.11 = bf16[2,3,2,32,128]{4,3,2,1,0:T(8,128)(2,1)S(1)} collective-permute-done((bf16[2,3,2,32,128]{4,3,2,1,0:T(8,128)(2,1)S(1)}, bf16[2,3,2,32,128]{4,3,2,1,0:T(8,128)(2,1)S(1)}, u32[]{:S(2)}, u32[]{:S(2)}) %collective-permute-start.11) | collective-permute-done | bytes 98336 | tf_op jit(solution)/shard_map/ppermute | solution.py:397
  23.2 0.2 collective-permute-done.14.refs_6_
  23.5 1.0 %collective-permute-done.15.refs_7_ = bf16[6,2,32,128]{3,2,1,0:T(8,128)(2,1)S(1)} collective-permute-done((bf16[6,2,32,128]{3,2,1,0:T(8,128)(2,1)S(1)}, bf16[6,2,32,128]{3,2,1,0:T(8,128)(2,1)S(1)}, u32[]{:S(2)}, u32[]{:S(2)}) %collective-permute-start.15) | collective-permute-done | bytes 98336 | tf_op jit(solution)/shard_map/ppermute | solution.py:400
  24.5 0.4 shard_map.42
  24.9 1.5 %collective-permute-start.16 = (bf16[2,3,2,32,128]{4,3,2,1,0:T(8,128)(2,1)S(1)}, bf16[2,3,2,32,128]{4,3,2,1,0:T(8,128)(2,1)S(1)}, u32[]{:S(2)}, u32[]{:S(2)}) collective-permute-start(bf16[2,3,2,32,128]{4,3,2,1,0:T(8,128)(2,1)S(1)} %bitcast.41), channel_id=1, source_target_pairs={{0,8},{4,12},{8,0},{12,4},{16,24},{20,28},{24,16},{28,20},{1,9},{5... | collective-permute-start | bytes 294920 | tf_op jit(solution)/shard_map/ppermute | solution.py:397
  26.4 0.7 %collective-permute-start.17 = (bf16[2,3,2,32,128]{4,3,2,1,0:T(8,128)(2,1)S(1)}, bf16[2,3,2,32,128]{4,3,2,1,0:T(8,128)(2,1)S(1)}, u32[]{:S(2)}, u32[]{:S(2)}) collective-permute-start(bf16[2,3,2,32,128]{4,3,2,1,0:T(8,128)(2,1)S(1)} %bitcast.40), channel_id=1, source_target_pairs={{0,16},{4,20},{8,24},{12,28},{16,0},{20,4},{24,8},{28,12},{1,17},{... | collective-permute-start | bytes 294920 | tf_op jit(solution)/shard_map/ppermute | solution.py:397
  27.1 1.3 %collective-permute-start.18 = (bf16[2,3,2,32,128]{4,3,2,1,0:T(8,128)(2,1)S(1)}, bf16[2,3,2,32,128]{4,3,2,1,0:T(8,128)(2,1)S(1)}, u32[]{:S(2)}, u32[]{:S(2)}) collective-permute-start(bf16[2,3,2,32,128]{4,3,2,1,0:T(8,128)(2,1)S(1)} %bitcast.39), channel_id=1, source_target_pairs={{0,24},{4,28},{8,16},{12,20},{16,8},{20,12},{24,0},{28,4},{1,25},{... | collective-permute-start | bytes 294920 | tf_op jit(solution)/shard_map/ppermute | solution.py:397
  28.5 1.4 %collective-permute-done.16.refs_1_ = bf16[2,3,2,32,128]{4,3,2,1,0:T(8,128)(2,1)S(1)} collective-permute-done((bf16[2,3,2,32,128]{4,3,2,1,0:T(8,128)(2,1)S(1)}, bf16[2,3,2,32,128]{4,3,2,1,0:T(8,128)(2,1)S(1)}, u32[]{:S(2)}, u32[]{:S(2)}) %collective-permute-start.16) | collective-permute-done | bytes 98336 | tf_op jit(solution)/shard_map/ppermute | solution.py:397
  29.8 3.5 %collective-permute-done.17.refs_2_ = bf16[2,3,2,32,128]{4,3,2,1,0:T(8,128)(2,1)S(1)} collective-permute-done((bf16[2,3,2,32,128]{4,3,2,1,0:T(8,128)(2,1)S(1)}, bf16[2,3,2,32,128]{4,3,2,1,0:T(8,128)(2,1)S(1)}, u32[]{:S(2)}, u32[]{:S(2)}) %collective-permute-start.17) | collective-permute-done | bytes 98336 | tf_op jit(solution)/shard_map/ppermute | solution.py:397
  33.3 0.5 %shard_map.43 = (bf16[3,2,128,128]{3,2,1,0:T(8,128)(2,1)S(1)}, bf16[3,2,128,128]{3,2,1,0:T(8,128)(2,1)S(1)}, bf16[2,3,2,128,128]{4,3,2,1,0:T(8,128)(2,1)S(1)}) custom-call(bf16[2,3,2,128,128]{4,3,2,1,0:T(8,128)(2,1)S(1)} %bitcast.17, bf16[2,3,2,32,128]{4,3,2,1,0:T(8,128)(2,1)S(1)} %bitcast.38, ...), custom_call_target="tpu_custom_call" | custom-call | flops 100663296 | bytes 1572864 | tf_op jit(solution)/shard_map/pallas_call | solution.py:351
  33.8 2.6 %collective-permute-start.21 = (bf16[3,2,128,128]{3,2,1,0:T(8,128)(2,1)S(1)}, bf16[3,2,128,128]{3,2,1,0:T(8,128)(2,1)S(1)}, u32[]{:S(2)}, u32[]{:S(2)}) collective-permute-start(bf16[3,2,128,128]{3,2,1,0:T(8,128)(2,1)S(1)} %get-tuple-element.53), channel_id=1, source_target_pairs={{0,1},{1,0},{2,3},{3,2},{4,5},{5,4},{6,7},{7,6},{8,9},{9,8},{10,11... | collective-permute-start | bytes 589832 | tf_op jit(solution)/shard_map/ppermute | solution.py:394
  36.4 2.1 %collective-permute-start.19 = (bf16[2,2,128,128]{3,2,1,0:T(8,128)(2,1)S(1)}, bf16[2,2,128,128]{3,2,1,0:T(8,128)(2,1)S(1)}, u32[]{:S(2)}, u32[]{:S(2)}) collective-permute-start(bf16[2,2,128,128]{3,2,1,0:T(8,128)(2,1)S(1)} %get-tuple-element.51), channel_id=1, source_target_pairs={{0,1},{1,0},{2,3},{3,2},{4,5},{5,4},{6,7},{7,6},{8,9},{9,8},{10,11... | collective-permute-start | bytes 393224 | tf_op jit(solution)/shard_map/ppermute | solution.py:394
  38.5 0.6 %shard_map.44 = (f32[2,3,128,256]{3,2,1,0:T(8,128)S(1)}, bf16[2,2,128,256]{3,2,1,0:T(8,128)(2,1)S(1)}) custom-call(bf16[2,3,2,128,128]{4,3,2,1,0:T(8,128)(2,1)S(1)} %bitcast.18, bf16[2,3,2,128,128]{4,3,2,1,0:T(8,128)(2,1)S(1)} %get-tuple-element.48.p_ref), custom_call_target="tpu_custom_call" | custom-call | flops 402653184 | bytes 1441792 | tf_op jit(solution)/shard_map/pallas_call | solution.py:351
  39.1 4.3 %collective-permute-done.19.g_first_ref = bf16[2,2,128,128]{3,2,1,0:T(8,128)(2,1)S(1)} collective-permute-done((bf16[2,2,128,128]{3,2,1,0:T(8,128)(2,1)S(1)}, bf16[2,2,128,128]{3,2,1,0:T(8,128)(2,1)S(1)}, u32[]{:S(2)}, u32[]{:S(2)}) %collective-permute-start.19) | collective-permute-done | bytes 131104 | tf_op jit(solution)/shard_map/ppermute | solution.py:394
  43.4 1.4 %shard_map.45 = bf16[2,3,2,128,128]{4,3,2,1,0:T(8,128)(2,1)} custom-call(bf16[2,3,2,128,128]{4,3,2,1,0:T(8,128)(2,1)S(1)} %bitcast.19, f32[2,3,128,256]{3,2,1,0:T(8,128)S(1)} %get-tuple-element.49.sum_ref, bf16[2,2,128,256]{3,2,1,0:T(8,128)(2,1)S(1)} %get-tuple-element.50.edge_ref, bf16[2,2,128,128]{3,2,1,0:T(8,128)(2,1)S(1)} %collective-permute-done.19.g_first_ref, ...), custom_call_target="tpu_custom_call" | custom-call | flops 268435456 | bytes 2097152 | tf_op jit(solution)/shard_map/pallas_call | solution.py:351
  (29 shorter events, 0.2 us)
Async XLA Ops:
  0.0 1.0 %copy-start.1 = (bf16[1,2,3,2,128,128]{5,4,3,2,1,0:T(8,128)(2,1)S(1)}, bf16[1,2,3,2,128,128]{5,4,3,2,1,0:T(8,128)(2,1)}, u32[]{:S(2)}) copy-start(bf16[1,2,3,2,128,128]{5,4,3,2,1,0:T(8,128)(2,1)} %param.3) | copy-start | bytes 1179652
  1.0 1.0 %copy-start.2 = (bf16[1,2,3,2,128,128]{5,4,3,2,1,0:T(8,128)(2,1)S(1)}, bf16[1,2,3,2,128,128]{5,4,3,2,1,0:T(8,128)(2,1)}, u32[]{:S(2)}) copy-start(bf16[1,2,3,2,128,128]{5,4,3,2,1,0:T(8,128)(2,1)} %param.4) | copy-start | bytes 1179652
  2.0 3.9 %copy-start = (bf16[1,2,3,2,128,128]{5,4,3,2,1,0:T(8,128)(2,1)S(1)}, bf16[1,2,3,2,128,128]{5,4,3,2,1,0:T(8,128)(2,1)}, u32[]{:S(2)}) copy-start(bf16[1,2,3,2,128,128]{5,4,3,2,1,0:T(8,128)(2,1)} %param.5) | copy-start | bytes 1179652
  2.8 11.6 %collective-permute-start.7 = (bf16[5,2,128,128]{3,2,1,0:T(8,128)(2,1)S(1)}, bf16[5,2,128,128]{3,2,1,0:T(8,128)(2,1)S(1)}, u32[]{:S(2)}, u32[]{:S(2)}) collective-permute-start(bf16[5,2,128,128]{3,2,1,0:T(8,128)(2,1)S(1)} %get-tuple-element.38), channel_id=1, source_target_pairs={{0,1},{1,0},{2,3},{3,2},{4,5},{5,4},{6,7},{7,6},{8,9},{9,8},{10,11... | collective-permute-start | bytes 983048 | tf_op jit(solution)/shard_map/ppermute | solution.py:394
  5.9 9.0 %collective-permute-start.8 = (bf16[5,2,128,128]{3,2,1,0:T(8,128)(2,1)S(1)}, bf16[5,2,128,128]{3,2,1,0:T(8,128)(2,1)S(1)}, u32[]{:S(2)}, u32[]{:S(2)}) collective-permute-start(bf16[5,2,128,128]{3,2,1,0:T(8,128)(2,1)S(1)} %get-tuple-element.39), channel_id=1, source_target_pairs={{0,4},{1,2},{2,1},{3,7},{4,0},{5,6},{6,5},{7,3},{8,12},{9,10},{10,... | collective-permute-start | bytes 983048 | tf_op jit(solution)/shard_map/ppermute | solution.py:394
  6.0 5.3 %collective-permute-start = (bf16[2,3,2,32,128]{4,3,2,1,0:T(8,128)(2,1)S(1)}, bf16[2,3,2,32,128]{4,3,2,1,0:T(8,128)(2,1)S(1)}, u32[]{:S(2)}, u32[]{:S(2)}) collective-permute-start(bf16[2,3,2,32,128]{4,3,2,1,0:T(8,128)(2,1)S(1)} %get-tuple-element.31), channel_id=1, source_target_pairs={{0,8},{4,12},{8,0},{12,4},{16,24},{20,28},{24,16},{28,20},{1,9},{5... | collective-permute-start | bytes 294920 | tf_op jit(solution)/shard_map/ppermute | solution.py:397
  7.5 6.8 %collective-permute-start.1 = (bf16[2,3,2,32,128]{4,3,2,1,0:T(8,128)(2,1)S(1)}, bf16[2,3,2,32,128]{4,3,2,1,0:T(8,128)(2,1)S(1)}, u32[]{:S(2)}, u32[]{:S(2)}) collective-permute-start(bf16[2,3,2,32,128]{4,3,2,1,0:T(8,128)(2,1)S(1)} %get-tuple-element.32), channel_id=1, source_target_pairs={{0,16},{4,20},{8,24},{12,28},{16,0},{20,4},{24,8},{28,12},{1,17},{... | collective-permute-start | bytes 294920 | tf_op jit(solution)/shard_map/ppermute | solution.py:397
  9.1 7.2 %collective-permute-start.3 = (bf16[6,2,32,128]{3,2,1,0:T(8,128)(2,1)S(1)}, bf16[6,2,32,128]{3,2,1,0:T(8,128)(2,1)S(1)}, u32[]{:S(2)}, u32[]{:S(2)}) collective-permute-start(bf16[6,2,32,128]{3,2,1,0:T(8,128)(2,1)S(1)} %bitcast.22), channel_id=1, source_target_pairs={{0,4},{4,0},{8,12},{12,8},{16,20},{20,16},{24,28},{28,24},{1,5},{5... | collective-permute-start | bytes 294920 | tf_op jit(solution)/shard_map/ppermute | solution.py:400
  11.3 6.3 %collective-permute-start.2 = (bf16[2,3,2,32,128]{4,3,2,1,0:T(8,128)(2,1)S(1)}, bf16[2,3,2,32,128]{4,3,2,1,0:T(8,128)(2,1)S(1)}, u32[]{:S(2)}, u32[]{:S(2)}) collective-permute-start(bf16[2,3,2,32,128]{4,3,2,1,0:T(8,128)(2,1)S(1)} %get-tuple-element.33), channel_id=1, source_target_pairs={{0,24},{4,28},{8,16},{12,20},{16,8},{20,12},{24,0},{28,4},{1,25},{... | collective-permute-start | bytes 294920 | tf_op jit(solution)/shard_map/ppermute | solution.py:397
  14.3 4.9 %collective-permute-start.4 = (bf16[6,2,32,128]{3,2,1,0:T(8,128)(2,1)S(1)}, bf16[6,2,32,128]{3,2,1,0:T(8,128)(2,1)S(1)}, u32[]{:S(2)}, u32[]{:S(2)}) collective-permute-start(bf16[6,2,32,128]{3,2,1,0:T(8,128)(2,1)S(1)} %bitcast.24), channel_id=1, source_target_pairs={{0,4},{4,0},{8,12},{12,8},{16,20},{20,16},{24,28},{28,24},{1,5},{5... | collective-permute-start | bytes 294920 | tf_op jit(solution)/shard_map/ppermute | solution.py:400
  14.4 4.8 %collective-permute-start.5 = (bf16[6,2,32,128]{3,2,1,0:T(8,128)(2,1)S(1)}, bf16[6,2,32,128]{3,2,1,0:T(8,128)(2,1)S(1)}, u32[]{:S(2)}, u32[]{:S(2)}) collective-permute-start(bf16[6,2,32,128]{3,2,1,0:T(8,128)(2,1)S(1)} %bitcast.26), channel_id=1, source_target_pairs={{0,4},{4,0},{8,12},{12,8},{16,20},{20,16},{24,28},{28,24},{1,5},{5... | collective-permute-start | bytes 294920 | tf_op jit(solution)/shard_map/ppermute | solution.py:400
  15.6 5.2 %collective-permute-start.9 = (bf16[2,3,2,32,128]{4,3,2,1,0:T(8,128)(2,1)S(1)}, bf16[2,3,2,32,128]{4,3,2,1,0:T(8,128)(2,1)S(1)}, u32[]{:S(2)}, u32[]{:S(2)}) collective-permute-start(bf16[2,3,2,32,128]{4,3,2,1,0:T(8,128)(2,1)S(1)} %get-tuple-element.41), channel_id=1, source_target_pairs={{0,8},{4,12},{8,0},{12,4},{16,24},{20,28},{24,16},{28,20},{1,9},{5... | collective-permute-start | bytes 294920 | tf_op jit(solution)/shard_map/ppermute | solution.py:397
  16.2 5.9 %collective-permute-start.10 = (bf16[2,3,2,32,128]{4,3,2,1,0:T(8,128)(2,1)S(1)}, bf16[2,3,2,32,128]{4,3,2,1,0:T(8,128)(2,1)S(1)}, u32[]{:S(2)}, u32[]{:S(2)}) collective-permute-start(bf16[2,3,2,32,128]{4,3,2,1,0:T(8,128)(2,1)S(1)} %get-tuple-element.42), channel_id=1, source_target_pairs={{0,16},{4,20},{8,24},{12,28},{16,0},{20,4},{24,8},{28,12},{1,17},{... | collective-permute-start | bytes 294920 | tf_op jit(solution)/shard_map/ppermute | solution.py:397
  17.6 5.5 %collective-permute-start.11 = (bf16[2,3,2,32,128]{4,3,2,1,0:T(8,128)(2,1)S(1)}, bf16[2,3,2,32,128]{4,3,2,1,0:T(8,128)(2,1)S(1)}, u32[]{:S(2)}, u32[]{:S(2)}) collective-permute-start(bf16[2,3,2,32,128]{4,3,2,1,0:T(8,128)(2,1)S(1)} %get-tuple-element.43), channel_id=1, source_target_pairs={{0,24},{4,28},{8,16},{12,20},{16,8},{20,12},{24,0},{28,4},{1,25},{... | collective-permute-start | bytes 294920 | tf_op jit(solution)/shard_map/ppermute | solution.py:397
  19.2 3.9 %collective-permute-start.6 = (bf16[6,2,32,128]{3,2,1,0:T(8,128)(2,1)S(1)}, bf16[6,2,32,128]{3,2,1,0:T(8,128)(2,1)S(1)}, u32[]{:S(2)}, u32[]{:S(2)}) collective-permute-start(bf16[6,2,32,128]{3,2,1,0:T(8,128)(2,1)S(1)} %bitcast.28), channel_id=1, source_target_pairs={{0,4},{4,0},{8,12},{12,8},{16,20},{20,16},{24,28},{28,24},{1,5},{5... | collective-permute-start | bytes 294920 | tf_op jit(solution)/shard_map/ppermute | solution.py:400
  19.2 4.0 %collective-permute-start.12 = (bf16[6,2,32,128]{3,2,1,0:T(8,128)(2,1)S(1)}, bf16[6,2,32,128]{3,2,1,0:T(8,128)(2,1)S(1)}, u32[]{:S(2)}, u32[]{:S(2)}) collective-permute-start(bf16[6,2,32,128]{3,2,1,0:T(8,128)(2,1)S(1)} %bitcast.30), channel_id=1, source_target_pairs={{0,4},{4,0},{8,12},{12,8},{16,20},{20,16},{24,28},{28,24},{1,5},{5... | collective-permute-start | bytes 294920 | tf_op jit(solution)/shard_map/ppermute | solution.py:400
  20.9 2.4 %collective-permute-start.13 = (bf16[6,2,32,128]{3,2,1,0:T(8,128)(2,1)S(1)}, bf16[6,2,32,128]{3,2,1,0:T(8,128)(2,1)S(1)}, u32[]{:S(2)}, u32[]{:S(2)}) collective-permute-start(bf16[6,2,32,128]{3,2,1,0:T(8,128)(2,1)S(1)} %bitcast.32), channel_id=1, source_target_pairs={{0,4},{4,0},{8,12},{12,8},{16,20},{20,16},{24,28},{28,24},{1,5},{5... | collective-permute-start | bytes 294920 | tf_op jit(solution)/shard_map/ppermute | solution.py:400
  22.2 1.3 %collective-permute-start.14 = (bf16[6,2,32,128]{3,2,1,0:T(8,128)(2,1)S(1)}, bf16[6,2,32,128]{3,2,1,0:T(8,128)(2,1)S(1)}, u32[]{:S(2)}, u32[]{:S(2)}) collective-permute-start(bf16[6,2,32,128]{3,2,1,0:T(8,128)(2,1)S(1)} %bitcast.34), channel_id=1, source_target_pairs={{0,4},{4,0},{8,12},{12,8},{16,20},{20,16},{24,28},{28,24},{1,5},{5... | collective-permute-start | bytes 294920 | tf_op jit(solution)/shard_map/ppermute | solution.py:400
  23.2 1.3 %collective-permute-start.15 = (bf16[6,2,32,128]{3,2,1,0:T(8,128)(2,1)S(1)}, bf16[6,2,32,128]{3,2,1,0:T(8,128)(2,1)S(1)}, u32[]{:S(2)}, u32[]{:S(2)}) collective-permute-start(bf16[6,2,32,128]{3,2,1,0:T(8,128)(2,1)S(1)} %bitcast.36), channel_id=1, source_target_pairs={{0,4},{4,0},{8,12},{12,8},{16,20},{20,16},{24,28},{28,24},{1,5},{5... | collective-permute-start | bytes 294920 | tf_op jit(solution)/shard_map/ppermute | solution.py:400
  24.9 4.9 %collective-permute-start.16 = (bf16[2,3,2,32,128]{4,3,2,1,0:T(8,128)(2,1)S(1)}, bf16[2,3,2,32,128]{4,3,2,1,0:T(8,128)(2,1)S(1)}, u32[]{:S(2)}, u32[]{:S(2)}) collective-permute-start(bf16[2,3,2,32,128]{4,3,2,1,0:T(8,128)(2,1)S(1)} %bitcast.41), channel_id=1, source_target_pairs={{0,8},{4,12},{8,0},{12,4},{16,24},{20,28},{24,16},{28,20},{1,9},{5... | collective-permute-start | bytes 294920 | tf_op jit(solution)/shard_map/ppermute | solution.py:397
  26.4 6.9 %collective-permute-start.17 = (bf16[2,3,2,32,128]{4,3,2,1,0:T(8,128)(2,1)S(1)}, bf16[2,3,2,32,128]{4,3,2,1,0:T(8,128)(2,1)S(1)}, u32[]{:S(2)}, u32[]{:S(2)}) collective-permute-start(bf16[2,3,2,32,128]{4,3,2,1,0:T(8,128)(2,1)S(1)} %bitcast.40), channel_id=1, source_target_pairs={{0,16},{4,20},{8,24},{12,28},{16,0},{20,4},{24,8},{28,12},{1,17},{... | collective-permute-start | bytes 294920 | tf_op jit(solution)/shard_map/ppermute | solution.py:397
  27.1 6.2 %collective-permute-start.18 = (bf16[2,3,2,32,128]{4,3,2,1,0:T(8,128)(2,1)S(1)}, bf16[2,3,2,32,128]{4,3,2,1,0:T(8,128)(2,1)S(1)}, u32[]{:S(2)}, u32[]{:S(2)}) collective-permute-start(bf16[2,3,2,32,128]{4,3,2,1,0:T(8,128)(2,1)S(1)} %bitcast.39), channel_id=1, source_target_pairs={{0,24},{4,28},{8,16},{12,20},{16,8},{20,12},{24,0},{28,4},{1,25},{... | collective-permute-start | bytes 294920 | tf_op jit(solution)/shard_map/ppermute | solution.py:397
  33.8 9.7 %collective-permute-start.21 = (bf16[3,2,128,128]{3,2,1,0:T(8,128)(2,1)S(1)}, bf16[3,2,128,128]{3,2,1,0:T(8,128)(2,1)S(1)}, u32[]{:S(2)}, u32[]{:S(2)}) collective-permute-start(bf16[3,2,128,128]{3,2,1,0:T(8,128)(2,1)S(1)} %get-tuple-element.53), channel_id=1, source_target_pairs={{0,1},{1,0},{2,3},{3,2},{4,5},{5,4},{6,7},{7,6},{8,9},{9,8},{10,11... | collective-permute-start | bytes 589832 | tf_op jit(solution)/shard_map/ppermute | solution.py:394
  36.4 7.1 %collective-permute-start.22 = (bf16[3,2,128,128]{3,2,1,0:T(8,128)(2,1)S(1)}, bf16[3,2,128,128]{3,2,1,0:T(8,128)(2,1)S(1)}, u32[]{:S(2)}, u32[]{:S(2)}) collective-permute-start(bf16[3,2,128,128]{3,2,1,0:T(8,128)(2,1)S(1)} %get-tuple-element.54), channel_id=1, source_target_pairs={{0,4},{1,2},{2,1},{3,7},{4,0},{5,6},{6,5},{7,3},{8,12},{9,10},{10,... | collective-permute-start | bytes 589832 | tf_op jit(solution)/shard_map/ppermute | solution.py:394
  36.4 7.1 %collective-permute-start.19 = (bf16[2,2,128,128]{3,2,1,0:T(8,128)(2,1)S(1)}, bf16[2,2,128,128]{3,2,1,0:T(8,128)(2,1)S(1)}, u32[]{:S(2)}, u32[]{:S(2)}) collective-permute-start(bf16[2,2,128,128]{3,2,1,0:T(8,128)(2,1)S(1)} %get-tuple-element.51), channel_id=1, source_target_pairs={{0,1},{1,0},{2,3},{3,2},{4,5},{5,4},{6,7},{7,6},{8,9},{9,8},{10,11... | collective-permute-start | bytes 393224 | tf_op jit(solution)/shard_map/ppermute | solution.py:394
  38.5 5.0 %collective-permute-start.20 = (bf16[2,2,128,128]{3,2,1,0:T(8,128)(2,1)S(1)}, bf16[2,2,128,128]{3,2,1,0:T(8,128)(2,1)S(1)}, u32[]{:S(2)}, u32[]{:S(2)}) collective-permute-start(bf16[2,2,128,128]{3,2,1,0:T(8,128)(2,1)S(1)} %get-tuple-element.52), channel_id=1, source_target_pairs={{0,4},{1,2},{2,1},{3,7},{4,0},{5,6},{6,5},{7,3},{8,12},{9,10},{10,... | collective-permute-start | bytes 393224 | tf_op jit(solution)/shard_map/ppermute | solution.py:394

commit v3 on v0

v3 whole, which is shorter than its diff:
```python
import functools

import jax
import jax.numpy as jnp
from jax import lax
from jax.experimental import pallas as pl
from jax.experimental.pallas import tpu as pltpu
from jax.sharding import PartitionSpec as P


BF16 = jnp.bfloat16
F32 = jnp.float32
VMEM = pl.BlockSpec(memory_space=pltpu.VMEM)
HBM = pl.BlockSpec(memory_space=pltpu.HBM)
PACK = 16


def row_form(real, imag):
    return jnp.concatenate([real, imag], axis=1)


def square_form(real, imag):
    return jnp.concatenate([row_form(real, imag), row_form(-imag, real)], axis=0)


def times(lhs, rhs):
    return jnp.dot(lhs, rhs, preferred_element_type=F32)


def times_adjoint(lhs, rhs):
    return lax.dot_general(lhs, rhs, (((1,), (1,)), ((), ())), preferred_element_type=F32)


def zero_where(condition, value):
    return jnp.where(condition, jnp.zeros_like(value), value)


class Band:
    def __init__(self, ref):
        self.ref, self.rows = ref, ref.shape[0]

    def pair(self, row, col):
        return self.ref[row, col - row + 1, 0], self.ref[row, col - row + 1, 1]

    def row(self, row, col):
        return row_form(*self.pair(row, col))

    def square(self, row, col):
        return square_form(*self.pair(row, col))

    def ends(self):
        return (0, -1), (self.rows - 1, self.rows)


def store_pair(ref, index, pair):
    ref[index, 0] = pair[0]
    ref[index, 1] = pair[1]


def store_row(ref, index, value):
    half = value.shape[1] // 2
    store_pair(ref, index, (value[:, :half], value[:, half:]))


def load_square(ref, index):
    return square_form(ref[index, 0], ref[index, 1])


def own_adjoint(outer, inner, row):
    total = None
    for col in range(row - 1, row + 2):
        term = times_adjoint(inner.row(row, col), outer.square(row, col))
        total = term if total is None else total + term
    return total.astype(BF16)


def near_rows(place, rows):
    return [i for i in range(max(place - 1, 0), min(place + 2, rows))]


def chunks(value, count):
    size = value.shape[0] // count
    return [value[place * size : (place + 1) * size] for place in range(count)]


def by_turn(even_case, odd_case):
    even = lax.rem(lax.axis_index("space"), 2) == 0
    pl.when(even)(even_case)
    pl.when(jnp.logical_not(even))(odd_case)


def missing_sides():
    place = lax.axis_index("space")
    return place == 0, place == lax.axis_size("space") - 1


def owner():
    index = lax.axis_index("energy")
    return lax.shift_right_logical(index, 1), lax.bitwise_and(index, 1)


def fill(first_ref, second_ref, band, write):
    below, above = band.ends()

    def case(below_ref, above_ref):
        write(below_ref, *below)
        write(above_ref, *above)

    by_turn(lambda: case(second_ref, first_ref), lambda: case(first_ref, second_ref))


def send_kernel(w_ref, p_ref, first_ref, second_ref):
    outer, inner = Band(w_ref), Band(p_ref)

    def write(ref, row, past):
        for at, band in ((0, inner), (2, outer)):
            store_pair(ref, at, band.pair(row, row))
            store_pair(ref, at + 1, band.pair(row, past))
        store_row(ref, 4, own_adjoint(outer, inner, row))

    fill(first_ref, second_ref, outer, write)


def own_weights(outer, weight_ref):
    for side, (row, past) in enumerate(outer.ends()):
        for n, pair in enumerate([(row, past)] + [(target, row) for target in near_rows(row, outer.rows)]):
            weight_ref[side, n] = outer.square(*pair).T


def screened_local_kernel(w_ref, p_ref, sum_ref, edge_ref, weight_ref):
    local_kernel(w_ref, p_ref, sum_ref, edge_ref)
    own_weights(Band(w_ref), weight_ref)


def weights_kernel(g_ref, first_ref, second_ref, own_ref, near_ref):
    own_weights(Band(g_ref), own_ref)
    for turn, ref in enumerate((first_ref, second_ref)):
        for t in range(ref.shape[0]):
            near_ref[turn, t] = load_square(ref, t).T


def local_kernel(w_ref, p_ref, sum_ref, edge_ref):
    outer, inner = Band(w_ref), Band(p_ref)
    rows, partial = outer.rows, {}
    for mid in range(rows):
        users = near_rows(mid, rows)
        lhs = jnp.concatenate([outer.row(i, mid) for i in users], axis=0)
        for col in range(mid - 1, mid + 2):
            for i, part in zip(users, chunks(times(lhs, inner.square(mid, col)), len(users))):
                partial[i, col] = partial[i, col] + part if (i, col) in partial else part
    partial = {key: value.astype(BF16) for key, value in partial.items()}
    zero = jnp.zeros_like(partial[0, 0])
    for target in range(rows):
        users = near_rows(target, rows)
        total = None
        for col in range(target - 1, target + 2):
            lhs = jnp.concatenate([partial.get((i, col), zero) for i in users], axis=0)
            term = times_adjoint(lhs, outer.square(target, col))
            total = term if total is None else total + term
        for i, part in zip(users, chunks(total, len(users))):
            sum_ref[i, target - i + 1] = part
    for side, (row, past) in enumerate(outer.ends()):
        edge_ref[side, 0] = partial[row, past]
        edge_ref[side, 1] = partial[row, row]


def inside_terms(outer, sum_ref, weight_ref, passed, store):
    rows, added = outer.rows, {}
    for side, (row, past) in enumerate(outer.ends()):
        through, direct = passed[side]
        for n, target in enumerate(near_rows(row, rows)):
            term = times(direct, weight_ref[side, 1 + n])
            if target == row:
                term += times(through, weight_ref[side, 0])
            key = (row, target - row + 1)
            added[key] = added[key] + term if key in added else term
    for i in range(rows):
        for t in range(3):
            if 0 <= i + t - 1 < rows:
                value = sum_ref[i, t]
                store(i, t, (value + added[i, t] if (i, t) in added else value).astype(BF16))


def links(outer):
    return [zero_where(gone, outer.row(*end)) for gone, end in zip(missing_sides(), outer.ends())]


def piece_rows(slot, size):
    return pl.ds(pl.multiple_of(slot * size, size), size)


def cut(whole_ref, out_refs):
    if len(out_refs) == 1:
        out_refs[0][...] = whole_ref[...]
        return
    chip, _ = owner()
    size = out_refs[0].shape[-2]
    for s, ref in enumerate(out_refs):
        ref[...] = whole_ref[:, :, piece_rows(chip ^ s, size), :]


def screened_kernel(w_ref, sum_ref, edge_ref, weight_ref, first_ref, second_ref, *rest):
    *out_refs, whole_ref = rest
    outer = Band(w_ref)

    def store(i, t, value):
        store_row(whole_ref, 3 * i + t, value)

    def run(*refs):
        lhs = links(outer)
        passed = [[times(link, load_square(ref, n)).astype(BF16) for n in range(2)] for link, ref in zip(lhs, refs)]
        inside_terms(outer, sum_ref, weight_ref, passed, store)
        for side, (gone, (row, past)) in enumerate(zip(missing_sides(), outer.ends())):
            total = times(lhs[side], load_square(refs[side], 4))
            for n in range(2):
                total += times_adjoint(edge_ref[side, n], load_square(refs[side], 2 + n))
            store(row, past - row + 1, zero_where(gone, total).astype(BF16))

    by_turn(lambda: run(second_ref, first_ref), lambda: run(first_ref, second_ref))
    cut(whole_ref, out_refs)


def join(refs, out_ref):
    chip, _ = owner()
    slots = [(ref, n) for ref in refs for n in range(ref.shape[0])]
    for s, (ref, n) in enumerate(slots):
        size = ref.shape[-2]
        span = piece_rows(chip ^ s, size) if len(slots) > 1 else slice(0, size)
        out_ref[:, :, span, :] = ref[n]


def dressed_kernel(halves, g_ref, sum_ref, edge_ref, own_ref, near_ref, *rest):
    *sigma_refs, out_hbm, first_ref, second_ref, out_ref, sems = rest
    outer = Band(g_ref)
    rows = outer.rows
    join(sigma_refs[:halves], first_ref)
    join(sigma_refs[halves:], second_ref)

    def copy(i, t):
        return pltpu.make_async_copy(out_ref.at[i, t], out_hbm.at[i, t], sems.at[i, t])

    def run(below, above):
        stored = []

        def store(i, t, value):
            store_row(out_ref.at[i], t, value)
            stored.append((i, t))
            if len(stored) > 1:
                copy(*stored[-2]).start()

        order = ((1, 2, 0), (1, 0, 2))
        passed = [
            [times(link, load_square(ref, t)) for t in places]
            for link, (ref, _), places in zip(links(outer), (below, above), order)
        ]
        for side, (gone, (row, past)) in enumerate(zip(missing_sides(), outer.ends())):
            total = None
            for n, t in enumerate(order[side]):
                lhs = passed[side][n] + (edge_ref[side, n].astype(F32) if n < 2 else 0.0)
                term = times(lhs.astype(BF16), near_ref[(below, above)[side][1], t])
                total = term if total is None else total + term
            store(row, past - row + 1, zero_where(gone, total).astype(BF16))
        passed = [[value.astype(BF16) for value in values[:2]] for values in passed]
        inside_terms(outer, sum_ref, own_ref, passed, store)
        copy(*stored[-1]).start()

    first, second = (first_ref, 0), (second_ref, 1)
    by_turn(lambda: run(second, first), lambda: run(first, second))
    for i in range(rows):
        for t in range(3):
            copy(i, t).wait()


def split_kernel(g_ref, first_ref, second_ref, *out_refs):
    def write(ref, row, past):
        ref[...] = g_ref[row]

    fill(first_ref, second_ref, Band(g_ref), write)
    if out_refs:
        chip, _ = owner()
        size = out_refs[0].shape[-2]
        for s, ref in enumerate(out_refs):
            ref[...] = g_ref[:, :, :, piece_rows(chip ^ s, size), :].reshape(ref.shape)


def pack_kernel(*refs):
    chip, _ = owner()
    for s, ref in enumerate(refs[:-1]):
        refs[-1][chip ^ s] = ref[...]


def order_kernel(own_ref, other_ref, out_ref):
    _, place = owner()
    out_ref[0] = jnp.zeros(out_ref.shape[1:], BF16)
    for x in range(own_ref.shape[0]):
        out_ref[2 * x + place + 1] = own_ref[x]
        out_ref[2 * x + (1 - place) + 1] = other_ref[x]


def convolve_kernel(factor, early, g_ref, own_ref, other_ref, *refs):
    *outs, s_ref, o_ref = refs
    chip, place = owner()
    chips, groups = own_ref.shape[0], own_ref.shape[1]
    for x in range(chips):
        s_ref[2 * x + place] = own_ref[x]
        s_ref[2 * x + (1 - place)] = other_ref[x]

    def load(ref, e, a, c, span):
        return ref[e, a, c, span].astype(F32)

    def result(x, a, span, sums):
        o_ref[x, a, 0, span] = ((sums[0] - sums[1]) * factor).astype(BF16)
        o_ref[x, a, 1, span] = ((sums[2] + sums[3]) * factor).astype(BF16)

    def add(sums, g, s):
        terms = (g[0] * s[0], g[1] * s[1], g[0] * s[1], g[1] * s[0])
        return terms if sums is None else tuple(a + b for a, b in zip(sums, terms))

    def both(ref, e, a, span):
        return load(ref, e, a, 0, span), load(ref, e, a, 1, span)

    height = s_ref.shape[3]
    step = PACK if height % PACK == 0 else height
    for a in range(groups):
        for start in range(0, height, step):
            span = slice(start, start + step)
            if chips <= PACK:
                g = [[both(g_ref, 2 * j + place + 1 - d, a, span) for j in range(chips)] for d in range(2)]
                for x in range(chips):
                    sums = None
                    for k in range(x + 1):
                        for d in range(2):
                            sums = add(sums, g[d][x - k], both(s_ref, 2 * k + d, a, span))
                    result(x, a, span, sums)
                continue

            def energy(x, carry):
                def term(k, sums):
                    for d in range(2):
                        sums = add(sums, both(g_ref, 2 * (x - k) + place + 1 - d, a, span), both(s_ref, 2 * k + d, a, span))
                    return sums

                zero = jnp.zeros((step, s_ref.shape[4]), F32)
                result(x, a, span, lax.fori_loop(0, x + 1, term, (zero,) * 4))
                return carry

            lax.fori_loop(0, chips, energy, 0)
    if not early:
        outs[0][...] = o_ref[...]
        return
    *outs, first_ref, second_ref = outs
    for s, ref in enumerate(outs):
        ref[...] = o_ref[chip ^ s]
    end_rows([outs[0]], first_ref, second_ref)


def end_rows(pieces, first_ref, second_ref):
    last = pieces[0].shape[0] - 3

    def case(below_ref, above_ref):
        for n, ref in enumerate(pieces):
            below_ref[n] = ref[0:3]
            above_ref[n] = ref[last : last + 3]

    by_turn(lambda: case(second_ref, first_ref), lambda: case(first_ref, second_ref))


def late_kernel(*refs):
    *pieces, first_ref, second_ref = refs
    end_rows(pieces, first_ref, second_ref)


def join_kernel(*refs):
    g_ref, *pieces, sum_ref, edge_ref, sigma_ref = refs
    chip, _ = owner()
    for s, ref in enumerate(pieces):
        size = ref.shape[-2]
        span = piece_rows(chip ^ s, size) if len(pieces) > 1 else slice(0, size)
        for i in range(g_ref.shape[0]):
            sigma_ref[i, :, :, span, :] = ref[3 * i : 3 * i + 3]
    local_kernel(g_ref, sigma_ref, sum_ref, edge_ref)


def call(kernel, shapes, *args, flops=0, scratch=(), out_spec=VMEM):
    outs = tuple(jax.ShapeDtypeStruct(*s) if isinstance(s[0], tuple) else jax.ShapeDtypeStruct(s, BF16) for s in shapes)
    moved = sum(2 * a.size for a in args) + sum(2 * o.size for o in outs)
    single = len(outs) == 1
    return pl.pallas_call(
        kernel,
        out_shape=outs[0] if single else outs,
        in_specs=[VMEM] * len(args),
        out_specs=out_spec if single else tuple([out_spec] * len(outs)),
        scratch_shapes=list(scratch),
        cost_estimate=pl.CostEstimate(flops=flops, bytes_accessed=moved, transcendentals=0),
        compiler_params=pltpu.CompilerParams(vmem_limit_bytes=32 * 1024 * 1024),
    )(*args)


def trades(start, peers, count):
    mate = {i: i + 1 for i in range(start, peers - 1, 2)}
    mate.update({j: i for i, j in mate.items()})
    return [
        (e * peers + z, e * peers + mate[z] if z in mate else (e ^ 1) * peers + z)
        for e in range(count)
        for z in range(peers)
    ]


def local(screening, polarization, propagator):
    w, p, g = screening[0], polarization[0], propagator[0]
    rows, bands, parts, order = w.shape[0], w.shape[1], w.shape[2], w.shape[3]
    peers, count = lax.axis_size("space"), lax.axis_size("energy")
    turns = [trades(start, peers, count) for start in range(2)]
    chips = count // 2
    piece = order // chips
    inside = piece % PACK == 0
    product = 8 * order**3
    chip, place = owner()
    whole, square = (rows, bands, parts, order, order), (parts, order, order)
    blocks = rows * bands

    def trade(buffers):
        return [lax.ppermute(x, ("energy", "space"), pairs) for x, pairs in zip(buffers, turns)]

    def to_partner(x):
        return lax.ppermute(x, "energy", [(i, i ^ 1) for i in range(count)])

    def to_chips(pieces):
        return [
            lax.ppermute(x, "energy", [(i, i ^ (2 * s)) for i in range(count)]) if s else x
            for s, x in enumerate(pieces)
        ]

    cut_up = [(blocks, parts, piece, order)] * chips if inside else [(blocks, parts, order, order)]

    def same_place(x):
        groups = [[2 * c + k for c in range(chips)] for k in range(2)]
        return lax.all_to_all(x, "energy", 0, 0, tiled=True, axis_index_groups=groups)

    def to_owners(pieces):
        if inside:
            got = to_chips(pieces)
            return call(pack_kernel, [(chips,) + got[0].shape], *got)
        return same_place(jnp.moveaxis(pieces[0].reshape(blocks, parts, chips, piece, order), 2, 0))

    def from_owners(pieces):
        if inside:
            return to_chips(pieces)
        got = same_place(pieces[0])
        return [jnp.moveaxis(got, 0, 2).reshape((blocks,) + square)]

    row = lax.axis_index("space") * rows + jnp.arange(rows, dtype=jnp.int32)
    band = jnp.arange(bands, dtype=jnp.int32)
    past = (row[:, None] + band[None, :] == 0) | (row[:, None] + band[None, :] == peers * rows + 1)
    w, p = (zero_where(past[:, :, None, None, None], x) for x in (w, p))

    near_w = trade(call(send_kernel, [(5,) + square] * 2, w, p, flops=6 * product))
    near_g = [(bands,) + square] * 2
    g_first, g_second, *g_pieces = call(split_kernel, near_g + (cut_up if inside else []), g)
    g_own = to_owners(g_pieces or [g.reshape((blocks,) + square)])
    g_all = call(order_kernel, [(count + 1,) + g_own.shape[1:]], g_own, to_partner(g_own))
    g_weights = call(weights_kernel, [(2, 3, 2 * order, 2 * order)] * 2, g, *trade((g_first, g_second)))

    sums = [((rows, bands, order, 2 * order), F32), ((2, 2, order, 2 * order), BF16)]
    weights = (2, 3, 2 * order, 2 * order)
    w_sums, w_edge, w_weights = call(screened_local_kernel, sums + [weights], w, p, flops=24 * product)

    screened = call(
        screened_kernel, cut_up, w, w_sums, w_edge, w_weights, *near_w, flops=16 * product,
        scratch=[pltpu.VMEM((blocks,) + square, BF16)],
    )
    s_own = to_owners(screened if inside else [screened])
    factor = (3.0 * order / count) ** 0.5
    part, ends = (blocks, parts, piece, order), (bands, parts, piece, order)
    sigma = call(
        functools.partial(convolve_kernel, factor, inside),
        [part] * chips + [(1,) + ends] * 2 if inside else [(chips,) + part],
        g_all, s_own, to_partner(s_own),
        scratch=[pltpu.VMEM((size,) + part, BF16) for size in (count, chips)],
    )
    early = []
    if inside:
        *sigma, first, second = sigma
        early = trade((first, second))
    sigma = from_owners(sigma if inside else [sigma])
    rest = sigma[len(early) // 2 :]
    late = trade(call(late_kernel, [(len(rest), bands) + rest[0].shape[1:]] * 2, *rest))
    near_s = [x for turn in zip(*(pair for pair in (early, late) if pair)) for x in turn]
    g_sums, g_edge = call(join_kernel, sums, g, *sigma, flops=24 * product, scratch=[pltpu.VMEM(whole, BF16)])
    out = call(
        functools.partial(dressed_kernel, len(near_s) // 2), [whole],
        g, g_sums, g_edge, *g_weights, *near_s, flops=18 * product, out_spec=HBM,
        scratch=[pltpu.VMEM((bands,) + square, BF16)] * 2 + [pltpu.VMEM(whole, BF16), pltpu.SemaphoreType.DMA((rows, bands))],
    )
    return out[None]


def solution(mesh):
    spec = P("energy", "space", None, None, None, None)

    return jax.shard_map(local, mesh=mesh, in_specs=(spec, spec, spec), out_specs=spec, check_vma=False)
```

time: 101 us -> 40.7 us (0.40)
  matrix products: 35.2 us -> 0 us
  waiting for transfers between devices: 25.1 us -> 12.9 us
  blocking collectives: 10.7 us -> 0 us
  local copies, waits for them, and re-layouts: 6.76 us -> 0.01 us
  Pallas kernels: 0 us -> 4.78 us
  starting transfers between devices: 18.6 us -> 21.4 us
  other arithmetic: 3.78 us -> 1.32 us
    dot_general x172 -> x0, matrix products: 35.2 us -> none  [the longest x144 23.9 us: product(): return jnp.einsum(form, lhs, rhs, preferred_element_type=jnp.float32)]
    ppermute x4 -> x19, starting transfers between devices: 9.56 us -> 21.4 us  [the longest x9 10.7 us: to_chips(): lax.ppermute(x, 'energy', [(i, i ^ 2 * s) for i in range(count)])]
    all_to_all x1 -> x0, blocking collectives: 10.7 us -> none  [local(): lax.all_to_all(sigma_owned, 'energy', split_axis=0, concat_axis=4, tiled=...]
    all_to_all x2 -> x0, starting transfers between devices: 9.01 us -> none  [the longest x1 5.2 us: local(): lax.all_to_all(propa_masked, 'energy', split_axis=4, concat_axis=0, tiled...]
    all_to_all x2 -> x0, waiting for transfers between devices: 7.33 us -> none  [the longest x1 5.9 us: local(): lax.all_to_all(screened, 'energy', split_axis=4, concat_axis=0, tiled=True)]
    ppermute x4 -> x19, waiting for transfers between devices: 17.8 us -> 12.9 us  [the longest x9 6.14 us: to_chips(): lax.ppermute(x, 'energy', [(i, i ^ 2 * s) for i in range(count)])]
    pallas_call x0 -> x12, Pallas kernels: none -> 4.78 us  [call(): pl.pallas_call(kernel, out_shape=outs[0] if single else outs, in_specs=[V...]
    another operation x8 -> x0, local copies, waits for them, and re-layouts: 2.33 us -> none  [the longest x2 1.93 us: sandwich(): return jnp.stack(bands, axis=2)]
  transfers between devices with their start and end apart: 6 -> 19, of which waited for: 6 -> 7; matrix products, arithmetic and copies ran while one was open for 7% -> 0% of each run, Pallas kernels for 0% -> 6%
where the time goes in v3:
time: 40.7 us; the launch traced here: 40.5 us
  starting transfers between devices  21.4 us (53%)
  waiting for transfers between devices  12.9 us (32%)
  Pallas kernels  4.78 us (12%)
  other arithmetic  1.32 us (3%)
    ppermute x9, starting transfers between devices, to_chips(): lax.ppermute(x, 'energy', [(i, i ^ 2 * s) for i in range(count)])  10.7 us
    ppermute x8, starting transfers between devices, trade(): lax.ppermute(x, ('energy', 'space'), pairs)  10.6 us
    ppermute x9, waiting for transfers between devices, to_chips(): lax.ppermute(x, 'energy', [(i, i ^ 2 * s) for i in range(count)])  6.14 us
    ppermute x8, waiting for transfers between devices, trade(): lax.ppermute(x, ('energy', 'space'), pairs)  5.12 us
    pallas_call x12, Pallas kernels, call(): pl.pallas_call(kernel, out_shape=outs[0] if single else outs, in_specs=[V...  4.78 us
    ppermute x2, waiting for transfers between devices, to_partner(): return lax.ppermute(x, 'energy', [(i, i ^ 1) for i in range(count)])  1.62 us
    select_n x1, other arithmetic, zero_where(): return jnp.where(condition, jnp.zeros_like(value), value)  1.24 us
  transfers between devices with their start and end apart: 19, of which 7 were waited for; matrix products, arithmetic and copies ran while one was open for 0% of the time, Pallas kernels for 6%

profile of v3, /device:TPU:0, one launch (start us, length us, event | category | flops | bytes accessed | tf_op | source)
XLA Modules:
  0.0 40.5 jit_solution(2742431100225492242)
XLA Ops:
  0.0 0.1 compare_or_fusion
  0.1 1.2 %bitcast_select_fusion = (bf16[2,3,2,128,128]{4,3,2,1,0:T(8,128)(2,1)S(1)}, bf16[2,3,2,128,128]{4,3,2,1,0:T(8,128)(2,1)S(1)}) fusion(bf16[1,2,3,2,128,128]{5,4,3,2,1,0:T(8,128)(2,1)} %param.4, pred[2,3]{1,0:T(4,128)(4,1)S(1)} %compare_or_fusion, bf16[1,2,3,2,128,128]{5,4,3,2,1,0:T(8,128)(2,1)} %param.3), kind=kLoop, calls=%fused_computation | loop fusion | flops 393216 | bytes 1572870 | tf_op jit(solution)/shard_map/jit(_where)/select_n | solution.py:35
  1.3 0.4 %shard_map.41 = (bf16[5,2,128,128]{3,2,1,0:T(8,128)(2,1)S(1)}, bf16[5,2,128,128]{3,2,1,0:T(8,128)(2,1)S(1)}) custom-call(bf16[2,3,2,128,128]{4,3,2,1,0:T(8,128)(2,1)S(1)} %get-tuple-element.60.w_ref, bf16[2,3,2,128,128]{4,3,2,1,0:T(8,128)(2,1)S(1)} %get-tuple-element.59.p_ref), custom_call_target="tpu_custom_call" | custom-call | flops 100663296 | bytes 1441792 | tf_op jit(solution)/shard_map/pallas_call | solution.py:388
  1.8 3.1 %collective-permute-start.4 = (bf16[5,2,128,128]{3,2,1,0:T(8,128)(2,1)S(1)}, bf16[5,2,128,128]{3,2,1,0:T(8,128)(2,1)S(1)}, u32[]{:S(2)}, u32[]{:S(2)}) collective-permute-start(bf16[5,2,128,128]{3,2,1,0:T(8,128)(2,1)S(1)} %get-tuple-element.39), channel_id=1, source_target_pairs={{0,1},{1,0},{2,3},{3,2},{4,5},{5,4},{6,7},{7,6},{8,9},{9,8},{10,11... | collective-permute-start | bytes 983048 | tf_op jit(solution)/shard_map/ppermute | solution.py:423
  5.0 1.6 %collective-permute-start = (bf16[6,2,32,128]{3,2,1,0:T(8,128)(2,1)S(1)}, bf16[6,2,32,128]{3,2,1,0:T(8,128)(2,1)S(1)}, u32[]{:S(2)}, u32[]{:S(2)}) collective-permute-start(bf16[6,2,32,128]{3,2,1,0:T(8,128)(2,1)S(1)} %get-tuple-element.33), channel_id=1, source_target_pairs={{0,8},{4,12},{8,0},{12,4},{16,24},{20,28},{24,16},{28,20},{1,9},{5... | collective-permute-start | bytes 294920 | tf_op jit(solution)/shard_map/ppermute | solution.py:430
  6.5 1.5 %collective-permute-start.1 = (bf16[6,2,32,128]{3,2,1,0:T(8,128)(2,1)S(1)}, bf16[6,2,32,128]{3,2,1,0:T(8,128)(2,1)S(1)}, u32[]{:S(2)}, u32[]{:S(2)}) collective-permute-start(bf16[6,2,32,128]{3,2,1,0:T(8,128)(2,1)S(1)} %get-tuple-element.34), channel_id=1, source_target_pairs={{0,16},{4,20},{8,24},{12,28},{16,0},{20,4},{24,8},{28,12},{1,17},{... | collective-permute-start | bytes 294920 | tf_op jit(solution)/shard_map/ppermute | solution.py:430
  8.0 0.5 %collective-permute-start.2 = (bf16[6,2,32,128]{3,2,1,0:T(8,128)(2,1)S(1)}, bf16[6,2,32,128]{3,2,1,0:T(8,128)(2,1)S(1)}, u32[]{:S(2)}, u32[]{:S(2)}) collective-permute-start(bf16[6,2,32,128]{3,2,1,0:T(8,128)(2,1)S(1)} %get-tuple-element.35), channel_id=1, source_target_pairs={{0,24},{4,28},{8,16},{12,20},{16,8},{20,12},{24,0},{28,4},{1,25},{... | collective-permute-start | bytes 294920 | tf_op jit(solution)/shard_map/ppermute | solution.py:430
  8.5 0.6 %shard_map.40 = (f32[2,3,128,256]{3,2,1,0:T(8,128)S(1)}, bf16[2,2,128,256]{3,2,1,0:T(8,128)(2,1)S(1)}, bf16[2,3,256,256]{3,2,1,0:T(8,128)(2,1)S(1)}) custom-call(bf16[2,3,2,128,128]{4,3,2,1,0:T(8,128)(2,1)S(1)} %get-tuple-element.60.w_ref, bf16[2,3,2,128,128]{4,3,2,1,0:T(8,128)(2,1)S(1)} %get-tuple-element.59.p_ref), custom_call_target="tpu_custom_call" | custom-call | flops 402653184 | bytes 2228224 | tf_op jit(solution)/shard_map/pallas_call | solution.py:388
  9.1 3.5 %collective-permute-done.4.first_ref = bf16[5,2,128,128]{3,2,1,0:T(8,128)(2,1)S(1)} collective-permute-done((bf16[5,2,128,128]{3,2,1,0:T(8,128)(2,1)S(1)}, bf16[5,2,128,128]{3,2,1,0:T(8,128)(2,1)S(1)}, u32[]{:S(2)}, u32[]{:S(2)}) %collective-permute-start.4) | collective-permute-done | bytes 327712 | tf_op jit(solution)/shard_map/ppermute | solution.py:423
  12.6 0.6 %shard_map.42 = (bf16[6,2,32,128]{3,2,1,0:T(8,128)(2,1)S(1)}, bf16[6,2,32,128]{3,2,1,0:T(8,128)(2,1)S(1)}, bf16[6,2,32,128]{3,2,1,0:T(8,128)(2,1)S(1)}, bf16[6,2,32,128]{3,2,1,0:T(8,128)(2,1)S(1)}) custom-call(bf16[2,3,2,128,128]{4,3,2,1,0:T(8,128)(2,1)S(1)} %get-tuple-element.60.w_ref, f32[2,3,128,256]{3,2,1,0:T(8,128)S(1)} %get-tuple-element.36.sum_ref, ...), custom_call_target="tpu_custom_call" | custom-call | flops 268435456 | bytes 2883584 | tf_op jit(solution)/shard_map/pallas_call | solution.py:388
  13.2 1.7 %collective-permute-start.6 = (bf16[6,2,32,128]{3,2,1,0:T(8,128)(2,1)S(1)}, bf16[6,2,32,128]{3,2,1,0:T(8,128)(2,1)S(1)}, u32[]{:S(2)}, u32[]{:S(2)}) collective-permute-start(bf16[6,2,32,128]{3,2,1,0:T(8,128)(2,1)S(1)} %get-tuple-element.42), channel_id=1, source_target_pairs={{0,8},{4,12},{8,0},{12,4},{16,24},{20,28},{24,16},{28,20},{1,9},{5... | collective-permute-start | bytes 294920 | tf_op jit(solution)/shard_map/ppermute | solution.py:430
  15.0 1.5 %collective-permute-start.7 = (bf16[6,2,32,128]{3,2,1,0:T(8,128)(2,1)S(1)}, bf16[6,2,32,128]{3,2,1,0:T(8,128)(2,1)S(1)}, u32[]{:S(2)}, u32[]{:S(2)}) collective-permute-start(bf16[6,2,32,128]{3,2,1,0:T(8,128)(2,1)S(1)} %get-tuple-element.43), channel_id=1, source_target_pairs={{0,16},{4,20},{8,24},{12,28},{16,0},{20,4},{24,8},{28,12},{1,17},{... | collective-permute-start | bytes 294920 | tf_op jit(solution)/shard_map/ppermute | solution.py:430
  16.5 0.3 collective-permute-start.8
  16.8 0.1 collective-permute-start.3
  16.9 1.5 %collective-permute-done.6.refs_1_ = bf16[6,2,32,128]{3,2,1,0:T(8,128)(2,1)S(1)} collective-permute-done((bf16[6,2,32,128]{3,2,1,0:T(8,128)(2,1)S(1)}, bf16[6,2,32,128]{3,2,1,0:T(8,128)(2,1)S(1)}, u32[]{:S(2)}, u32[]{:S(2)}) %collective-permute-start.6) | collective-permute-done | bytes 98336 | tf_op jit(solution)/shard_map/ppermute | solution.py:430
  18.4 2.2 %collective-permute-done.7.refs_2_ = bf16[6,2,32,128]{3,2,1,0:T(8,128)(2,1)S(1)} collective-permute-done((bf16[6,2,32,128]{3,2,1,0:T(8,128)(2,1)S(1)}, bf16[6,2,32,128]{3,2,1,0:T(8,128)(2,1)S(1)}, u32[]{:S(2)}, u32[]{:S(2)}) %collective-permute-start.7) | collective-permute-done | bytes 98336 | tf_op jit(solution)/shard_map/ppermute | solution.py:430
  20.6 1.4 %collective-permute-done.8.refs_3_ = bf16[6,2,32,128]{3,2,1,0:T(8,128)(2,1)S(1)} collective-permute-done((bf16[6,2,32,128]{3,2,1,0:T(8,128)(2,1)S(1)}, bf16[6,2,32,128]{3,2,1,0:T(8,128)(2,1)S(1)}, u32[]{:S(2)}, u32[]{:S(2)}) %collective-permute-start.8) | collective-permute-done | bytes 98336 | tf_op jit(solution)/shard_map/ppermute | solution.py:430
  22.0 0.1 collective-permute-start.9
  22.1 0.1 shard_map.39.g_ref
  22.2 1.6 %collective-permute-done.9.other_ref = bf16[4,6,2,32,128]{4,3,2,1,0:T(8,128)(2,1)S(1)} collective-permute-done((bf16[4,6,2,32,128]{4,3,2,1,0:T(8,128)(2,1)S(1)}, bf16[4,6,2,32,128]{4,3,2,1,0:T(8,128)(2,1)S(1)}, u32[]{:S(2)}, u32[]{:S(2)}) %collective-permute-start.9) | collective-permute-done | bytes 393248 | tf_op jit(solution)/shard_map/ppermute | solution.py:426
  23.8 0.4 %shard_map.44 = (bf16[6,2,32,128]{3,2,1,0:T(8,128)(2,1)S(1)}, bf16[6,2,32,128]{3,2,1,0:T(8,128)(2,1)S(1)}, bf16[6,2,32,128]{3,2,1,0:T(8,128)(2,1)S(1)}, bf16[6,2...) custom-call(bf16[9,6,2,32,128]{4,3,2,1,0:T(8,128)(2,1)S(1)} %shard_map., ...), custom_call_target="tpu_custom_call" | custom-call | bytes 2162688 | tf_op jit(solution)/shard_map/pallas_call | solution.py:388
  24.3 0.6 %collective-permute-start.10 = (bf16[6,2,32,128]{3,2,1,0:T(8,128)(2,1)S(1)}, bf16[6,2,32,128]{3,2,1,0:T(8,128)(2,1)S(1)}, u32[]{:S(2)}, u32[]{:S(2)}) collective-permute-start(bf16[6,2,32,128]{3,2,1,0:T(8,128)(2,1)S(1)} %get-tuple-element.46), channel_id=1, source_target_pairs={{0,8},{4,12},{8,0},{12,4},{16,24},{20,28},{24,16},{28,20},{1,9},{5... | collective-permute-start | bytes 294920 | tf_op jit(solution)/shard_map/ppermute | solution.py:430
  24.9 0.5 %collective-permute-start.11 = (bf16[6,2,32,128]{3,2,1,0:T(8,128)(2,1)S(1)}, bf16[6,2,32,128]{3,2,1,0:T(8,128)(2,1)S(1)}, u32[]{:S(2)}, u32[]{:S(2)}) collective-permute-start(bf16[6,2,32,128]{3,2,1,0:T(8,128)(2,1)S(1)} %get-tuple-element.47), channel_id=1, source_target_pairs={{0,16},{4,20},{8,24},{12,28},{16,0},{20,4},{24,8},{28,12},{1,17},{... | collective-permute-start | bytes 294920 | tf_op jit(solution)/shard_map/ppermute | solution.py:430
  25.3 2.5 %collective-permute-start.12 = (bf16[6,2,32,128]{3,2,1,0:T(8,128)(2,1)S(1)}, bf16[6,2,32,128]{3,2,1,0:T(8,128)(2,1)S(1)}, u32[]{:S(2)}, u32[]{:S(2)}) collective-permute-start(bf16[6,2,32,128]{3,2,1,0:T(8,128)(2,1)S(1)} %get-tuple-element.48), channel_id=1, source_target_pairs={{0,24},{4,28},{8,16},{12,20},{16,8},{20,12},{24,0},{28,4},{1,25},{... | collective-permute-start | bytes 294920 | tf_op jit(solution)/shard_map/ppermute | solution.py:430
  27.8 2.7 %collective-permute-start.13 = (bf16[3,2,128,128]{3,2,1,0:T(8,128)(2,1)S(1)}, bf16[3,2,128,128]{3,2,1,0:T(8,128)(2,1)S(1)}, u32[]{:S(2)}, u32[]{:S(2)}) collective-permute-start(bf16[3,2,128,128]{3,2,1,0:T(8,128)(2,1)S(1)} %get-tuple-element.51), channel_id=1, source_target_pairs={{0,1},{1,0},{2,3},{3,2},{4,5},{5,4},{6,7},{7,6},{8,9},{9,8},{10,11... | collective-permute-start | bytes 589832 | tf_op jit(solution)/shard_map/ppermute | solution.py:423
  30.5 1.1 %collective-permute-done.11.refs_3_.refs_1_ = bf16[6,2,32,128]{3,2,1,0:T(8,128)(2,1)S(1)} collective-permute-done((bf16[6,2,32,128]{3,2,1,0:T(8,128)(2,1)S(1)}, bf16[6,2,32,128]{3,2,1,0:T(8,128)(2,1)S(1)}, u32[]{:S(2)}, u32[]{:S(2)}) %collective-permute-start.11) | collective-permute-done | bytes 98336 | tf_op jit(solution)/shard_map/ppermute | solution.py:430
  31.6 2.8 %collective-permute-start.16 = (bf16[3,3,2,32,128]{4,3,2,1,0:T(8,128)(2,1)S(1)}, bf16[3,3,2,32,128]{4,3,2,1,0:T(8,128)(2,1)S(1)}, u32[]{:S(2)}, u32[]{:S(2)}) collective-permute-start(bf16[3,3,2,32,128]{4,3,2,1,0:T(8,128)(2,1)S(1)} %get-tuple-element.56), channel_id=1, source_target_pairs={{0,1},{1,0},{2,3},{3,2},{4,5},{5,4},{6,7},{7,6},{8,9},{9,8},{10,11... | collective-permute-start | bytes 442376 | tf_op jit(solution)/shard_map/ppermute | solution.py:423
  34.4 2.0 %collective-permute-start.15 = (bf16[1,3,2,32,128]{4,3,2,1,0:T(8,128)(2,1)S(1)}, bf16[1,3,2,32,128]{4,3,2,1,0:T(8,128)(2,1)S(1)}, u32[]{:S(2)}, u32[]{:S(2)}) collective-permute-start(bf16[1,3,2,32,128]{4,3,2,1,0:T(8,128)(2,1)S(1)} %get-tuple-element.55), channel_id=1, source_target_pairs={{0,1},{1,0},{2,3},{3,2},{4,5},{5,4},{6,7},{7,6},{8,9},{9,8},{10,11... | collective-permute-start | bytes 147464 | tf_op jit(solution)/shard_map/ppermute | solution.py:423
  36.4 0.4 shard_map.46
  36.8 0.7 %shard_map.45 = (f32[2,3,128,256]{3,2,1,0:T(8,128)S(1)}, bf16[2,2,128,256]{3,2,1,0:T(8,128)(2,1)S(1)}) custom-call(bf16[2,3,2,128,128]{4,3,2,1,0:T(8,128)(2,1)S(1)} %bitcast.8, bf16[6,2,32,128]{3,2,1,0:T(8,128)(2,1)S(1)} %get-tuple-element.45.refs_1_, bf16[6,2,32,128]{3,2,1,0:T(8,128)(2,1)S(1)} %collective-permute-done.10.refs_2_.refs_0_, ...), custom_call_target="tpu_custom_call" | custom-call | flops 402653184 | bytes 1441792 | tf_op jit(solution)/shard_map/pallas_call | solution.py:388
  37.5 1.6 %collective-permute-done.15.rest_0_ = bf16[1,3,2,32,128]{4,3,2,1,0:T(8,128)(2,1)S(1)} collective-permute-done((bf16[1,3,2,32,128]{4,3,2,1,0:T(8,128)(2,1)S(1)}, bf16[1,3,2,32,128]{4,3,2,1,0:T(8,128)(2,1)S(1)}, u32[]{:S(2)}, u32[]{:S(2)}) %collective-permute-start.15) | collective-permute-done | bytes 49184 | tf_op jit(solution)/shard_map/ppermute | solution.py:423
  39.1 1.4 %shard_map.48 = bf16[2,3,2,128,128]{4,3,2,1,0:T(8,128)(2,1)} custom-call(bf16[2,3,2,128,128]{4,3,2,1,0:T(8,128)(2,1)S(1)} %bitcast.9, f32[2,3,128,256]{3,2,1,0:T(8,128)S(1)} %get-tuple-element.49.sum_ref, bf16[2,2,128,256]{3,2,1,0:T(8,128)(2,1)S(1)} %get-tuple-element.50.edge_ref, bf16[2,3,256,256]{3,2,1,0:T(8,128)(2,1)S(1)} %get-tuple-element.53.own_ref, ...), custom_call_target="tpu_custom_call" | custom-call | flops 301989888 | bytes 3407872 | tf_op jit(solution)/shard_map/pallas_call | solution.py:388
  (23 shorter events, 0.2 us)
Async XLA Ops:
  1.3 3.6 %copy-start = (bf16[1,2,3,2,128,128]{5,4,3,2,1,0:T(8,128)(2,1)S(1)}, bf16[1,2,3,2,128,128]{5,4,3,2,1,0:T(8,128)(2,1)}, u32[]{:S(2)}) copy-start(bf16[1,2,3,2,128,128]{5,4,3,2,1,0:T(8,128)(2,1)} %param.5) | copy-start | bytes 1179652
  1.8 10.8 %collective-permute-start.4 = (bf16[5,2,128,128]{3,2,1,0:T(8,128)(2,1)S(1)}, bf16[5,2,128,128]{3,2,1,0:T(8,128)(2,1)S(1)}, u32[]{:S(2)}, u32[]{:S(2)}) collective-permute-start(bf16[5,2,128,128]{3,2,1,0:T(8,128)(2,1)S(1)} %get-tuple-element.39), channel_id=1, source_target_pairs={{0,1},{1,0},{2,3},{3,2},{4,5},{5,4},{6,7},{7,6},{8,9},{9,8},{10,11... | collective-permute-start | bytes 983048 | tf_op jit(solution)/shard_map/ppermute | solution.py:423
  4.9 7.7 %collective-permute-start.5 = (bf16[5,2,128,128]{3,2,1,0:T(8,128)(2,1)S(1)}, bf16[5,2,128,128]{3,2,1,0:T(8,128)(2,1)S(1)}, u32[]{:S(2)}, u32[]{:S(2)}) collective-permute-start(bf16[5,2,128,128]{3,2,1,0:T(8,128)(2,1)S(1)} %get-tuple-element.40), channel_id=1, source_target_pairs={{0,4},{1,2},{2,1},{3,7},{4,0},{5,6},{6,5},{7,3},{8,12},{9,10},{10,... | collective-permute-start | bytes 983048 | tf_op jit(solution)/shard_map/ppermute | solution.py:423
  5.0 11.5 %collective-permute-start = (bf16[6,2,32,128]{3,2,1,0:T(8,128)(2,1)S(1)}, bf16[6,2,32,128]{3,2,1,0:T(8,128)(2,1)S(1)}, u32[]{:S(2)}, u32[]{:S(2)}) collective-permute-start(bf16[6,2,32,128]{3,2,1,0:T(8,128)(2,1)S(1)} %get-tuple-element.33), channel_id=1, source_target_pairs={{0,8},{4,12},{8,0},{12,4},{16,24},{20,28},{24,16},{28,20},{1,9},{5... | collective-permute-start | bytes 294920 | tf_op jit(solution)/shard_map/ppermute | solution.py:430
  6.5 10.3 %collective-permute-start.1 = (bf16[6,2,32,128]{3,2,1,0:T(8,128)(2,1)S(1)}, bf16[6,2,32,128]{3,2,1,0:T(8,128)(2,1)S(1)}, u32[]{:S(2)}, u32[]{:S(2)}) collective-permute-start(bf16[6,2,32,128]{3,2,1,0:T(8,128)(2,1)S(1)} %get-tuple-element.34), channel_id=1, source_target_pairs={{0,16},{4,20},{8,24},{12,28},{16,0},{20,4},{24,8},{28,12},{1,17},{... | collective-permute-start | bytes 294920 | tf_op jit(solution)/shard_map/ppermute | solution.py:430
  8.0 8.8 %collective-permute-start.2 = (bf16[6,2,32,128]{3,2,1,0:T(8,128)(2,1)S(1)}, bf16[6,2,32,128]{3,2,1,0:T(8,128)(2,1)S(1)}, u32[]{:S(2)}, u32[]{:S(2)}) collective-permute-start(bf16[6,2,32,128]{3,2,1,0:T(8,128)(2,1)S(1)} %get-tuple-element.35), channel_id=1, source_target_pairs={{0,24},{4,28},{8,16},{12,20},{16,8},{20,12},{24,0},{28,4},{1,25},{... | collective-permute-start | bytes 294920 | tf_op jit(solution)/shard_map/ppermute | solution.py:430
  13.2 5.2 %collective-permute-start.6 = (bf16[6,2,32,128]{3,2,1,0:T(8,128)(2,1)S(1)}, bf16[6,2,32,128]{3,2,1,0:T(8,128)(2,1)S(1)}, u32[]{:S(2)}, u32[]{:S(2)}) collective-permute-start(bf16[6,2,32,128]{3,2,1,0:T(8,128)(2,1)S(1)} %get-tuple-element.42), channel_id=1, source_target_pairs={{0,8},{4,12},{8,0},{12,4},{16,24},{20,28},{24,16},{28,20},{1,9},{5... | collective-permute-start | bytes 294920 | tf_op jit(solution)/shard_map/ppermute | solution.py:430
  15.0 5.6 %collective-permute-start.7 = (bf16[6,2,32,128]{3,2,1,0:T(8,128)(2,1)S(1)}, bf16[6,2,32,128]{3,2,1,0:T(8,128)(2,1)S(1)}, u32[]{:S(2)}, u32[]{:S(2)}) collective-permute-start(bf16[6,2,32,128]{3,2,1,0:T(8,128)(2,1)S(1)} %get-tuple-element.43), channel_id=1, source_target_pairs={{0,16},{4,20},{8,24},{12,28},{16,0},{20,4},{24,8},{28,12},{1,17},{... | collective-permute-start | bytes 294920 | tf_op jit(solution)/shard_map/ppermute | solution.py:430
  16.5 5.5 %collective-permute-start.8 = (bf16[6,2,32,128]{3,2,1,0:T(8,128)(2,1)S(1)}, bf16[6,2,32,128]{3,2,1,0:T(8,128)(2,1)S(1)}, u32[]{:S(2)}, u32[]{:S(2)}) collective-permute-start(bf16[6,2,32,128]{3,2,1,0:T(8,128)(2,1)S(1)} %get-tuple-element.44), channel_id=1, source_target_pairs={{0,24},{4,28},{8,16},{12,20},{16,8},{20,12},{24,0},{28,4},{1,25},{... | collective-permute-start | bytes 294920 | tf_op jit(solution)/shard_map/ppermute | solution.py:430
  16.8 5.3 %collective-permute-start.3 = (bf16[4,6,2,32,128]{4,3,2,1,0:T(8,128)(2,1)S(1)}, bf16[4,6,2,32,128]{4,3,2,1,0:T(8,128)(2,1)S(1)}, u32[]{:S(2)}, u32[]{:S(2)}) collective-permute-start(bf16[4,6,2,32,128]{4,3,2,1,0:T(8,128)(2,1)S(1)} %shard_map.38.own_ref), channel_id=1, source_target_pairs={{0,4},{4,0},{8,12},{12,8},{16,20},{20,16},{24,28},{28,24},{1,5},{5... | collective-permute-start | bytes 1179656 | tf_op jit(solution)/shard_map/ppermute | solution.py:426
  22.0 1.8 %collective-permute-start.9 = (bf16[4,6,2,32,128]{4,3,2,1,0:T(8,128)(2,1)S(1)}, bf16[4,6,2,32,128]{4,3,2,1,0:T(8,128)(2,1)S(1)}, u32[]{:S(2)}, u32[]{:S(2)}) collective-permute-start(bf16[4,6,2,32,128]{4,3,2,1,0:T(8,128)(2,1)S(1)} %shard_map.43.own_ref), channel_id=1, source_target_pairs={{0,4},{4,0},{8,12},{12,8},{16,20},{20,16},{24,28},{28,24},{1,5},{5... | collective-permute-start | bytes 1179656 | tf_op jit(solution)/shard_map/ppermute | solution.py:426
  24.3 6.3 %collective-permute-start.10 = (bf16[6,2,32,128]{3,2,1,0:T(8,128)(2,1)S(1)}, bf16[6,2,32,128]{3,2,1,0:T(8,128)(2,1)S(1)}, u32[]{:S(2)}, u32[]{:S(2)}) collective-permute-start(bf16[6,2,32,128]{3,2,1,0:T(8,128)(2,1)S(1)} %get-tuple-element.46), channel_id=1, source_target_pairs={{0,8},{4,12},{8,0},{12,4},{16,24},{20,28},{24,16},{28,20},{1,9},{5... | collective-permute-start | bytes 294920 | tf_op jit(solution)/shard_map/ppermute | solution.py:430
  24.9 6.7 %collective-permute-start.11 = (bf16[6,2,32,128]{3,2,1,0:T(8,128)(2,1)S(1)}, bf16[6,2,32,128]{3,2,1,0:T(8,128)(2,1)S(1)}, u32[]{:S(2)}, u32[]{:S(2)}) collective-permute-start(bf16[6,2,32,128]{3,2,1,0:T(8,128)(2,1)S(1)} %get-tuple-element.47), channel_id=1, source_target_pairs={{0,16},{4,20},{8,24},{12,28},{16,0},{20,4},{24,8},{28,12},{1,17},{... | collective-permute-start | bytes 294920 | tf_op jit(solution)/shard_map/ppermute | solution.py:430
  25.3 6.2 %collective-permute-start.12 = (bf16[6,2,32,128]{3,2,1,0:T(8,128)(2,1)S(1)}, bf16[6,2,32,128]{3,2,1,0:T(8,128)(2,1)S(1)}, u32[]{:S(2)}, u32[]{:S(2)}) collective-permute-start(bf16[6,2,32,128]{3,2,1,0:T(8,128)(2,1)S(1)} %get-tuple-element.48), channel_id=1, source_target_pairs={{0,24},{4,28},{8,16},{12,20},{16,8},{20,12},{24,0},{28,4},{1,25},{... | collective-permute-start | bytes 294920 | tf_op jit(solution)/shard_map/ppermute | solution.py:430
  27.8 8.6 %collective-permute-start.13 = (bf16[3,2,128,128]{3,2,1,0:T(8,128)(2,1)S(1)}, bf16[3,2,128,128]{3,2,1,0:T(8,128)(2,1)S(1)}, u32[]{:S(2)}, u32[]{:S(2)}) collective-permute-start(bf16[3,2,128,128]{3,2,1,0:T(8,128)(2,1)S(1)} %get-tuple-element.51), channel_id=1, source_target_pairs={{0,1},{1,0},{2,3},{3,2},{4,5},{5,4},{6,7},{7,6},{8,9},{9,8},{10,11... | collective-permute-start | bytes 589832 | tf_op jit(solution)/shard_map/ppermute | solution.py:423
  30.5 5.9 %collective-permute-start.14 = (bf16[3,2,128,128]{3,2,1,0:T(8,128)(2,1)S(1)}, bf16[3,2,128,128]{3,2,1,0:T(8,128)(2,1)S(1)}, u32[]{:S(2)}, u32[]{:S(2)}) collective-permute-start(bf16[3,2,128,128]{3,2,1,0:T(8,128)(2,1)S(1)} %get-tuple-element.52), channel_id=1, source_target_pairs={{0,4},{1,2},{2,1},{3,7},{4,0},{5,6},{6,5},{7,3},{8,12},{9,10},{10,... | collective-permute-start | bytes 589832 | tf_op jit(solution)/shard_map/ppermute | solution.py:423
  31.6 7.5 %collective-permute-start.16 = (bf16[3,3,2,32,128]{4,3,2,1,0:T(8,128)(2,1)S(1)}, bf16[3,3,2,32,128]{4,3,2,1,0:T(8,128)(2,1)S(1)}, u32[]{:S(2)}, u32[]{:S(2)}) collective-permute-start(bf16[3,3,2,32,128]{4,3,2,1,0:T(8,128)(2,1)S(1)} %get-tuple-element.56), channel_id=1, source_target_pairs={{0,1},{1,0},{2,3},{3,2},{4,5},{5,4},{6,7},{7,6},{8,9},{9,8},{10,11... | collective-permute-start | bytes 442376 | tf_op jit(solution)/shard_map/ppermute | solution.py:423
  34.4 4.7 %collective-permute-start.18 = (bf16[3,3,2,32,128]{4,3,2,1,0:T(8,128)(2,1)S(1)}, bf16[3,3,2,32,128]{4,3,2,1,0:T(8,128)(2,1)S(1)}, u32[]{:S(2)}, u32[]{:S(2)}) collective-permute-start(bf16[3,3,2,32,128]{4,3,2,1,0:T(8,128)(2,1)S(1)} %get-tuple-element.58), channel_id=1, source_target_pairs={{0,4},{1,2},{2,1},{3,7},{4,0},{5,6},{6,5},{7,3},{8,12},{9,10},{10,... | collective-permute-start | bytes 442376 | tf_op jit(solution)/shard_map/ppermute | solution.py:423
  34.4 4.7 %collective-permute-start.15 = (bf16[1,3,2,32,128]{4,3,2,1,0:T(8,128)(2,1)S(1)}, bf16[1,3,2,32,128]{4,3,2,1,0:T(8,128)(2,1)S(1)}, u32[]{:S(2)}, u32[]{:S(2)}) collective-permute-start(bf16[1,3,2,32,128]{4,3,2,1,0:T(8,128)(2,1)S(1)} %get-tuple-element.55), channel_id=1, source_target_pairs={{0,1},{1,0},{2,3},{3,2},{4,5},{5,4},{6,7},{7,6},{8,9},{9,8},{10,11... | collective-permute-start | bytes 147464 | tf_op jit(solution)/shard_map/ppermute | solution.py:423
  36.4 2.7 %collective-permute-start.17 = (bf16[1,3,2,32,128]{4,3,2,1,0:T(8,128)(2,1)S(1)}, bf16[1,3,2,32,128]{4,3,2,1,0:T(8,128)(2,1)S(1)}, u32[]{:S(2)}, u32[]{:S(2)}) collective-permute-start(bf16[1,3,2,32,128]{4,3,2,1,0:T(8,128)(2,1)S(1)} %get-tuple-element.57), channel_id=1, source_target_pairs={{0,4},{1,2},{2,1},{3,7},{4,0},{5,6},{6,5},{7,3},{8,12},{9,10},{10,... | collective-permute-start | bytes 147464 | tf_op jit(solution)/shard_map/ppermute | solution.py:423

commit v4 on v3

--- a/solution.py
+++ b/solution.py
@@ -297,13 +297,18 @@
         out_ref[2 * x + (1 - place) + 1] = other_ref[x]
 
 
-def convolve_kernel(factor, early, g_ref, own_ref, other_ref, *refs):
-    *outs, s_ref, o_ref = refs
+def convolve_kernel(factor, early, chips, g_ref, *refs):
     chip, place = owner()
-    chips, groups = own_ref.shape[0], own_ref.shape[1]
-    for x in range(chips):
-        s_ref[2 * x + place] = own_ref[x]
-        s_ref[2 * x + (1 - place)] = other_ref[x]
+    sources = chips if early else 1
+    pieces, (*outs, s_ref, o_ref) = refs[: 2 * sources], refs[2 * sources :]
+    groups = s_ref.shape[1]
+    for n, ref in enumerate(pieces):
+        shift = place if n < sources else 1 - place
+        if early:
+            s_ref[2 * (chip ^ (n % sources)) + shift] = ref[...]
+        else:
+            for x in range(chips):
+                s_ref[2 * x + shift] = ref[x]
 
     def load(ref, e, a, c, span):
         return ref[e, a, c, span].astype(F32)
@@ -348,10 +353,8 @@
     if not early:
         outs[0][...] = o_ref[...]
         return
-    *outs, first_ref, second_ref = outs
     for s, ref in enumerate(outs):
         ref[...] = o_ref[chip ^ s]
-    end_rows([outs[0]], first_ref, second_ref)
 
 
 def end_rows(pieces, first_ref, second_ref):
@@ -365,7 +368,7 @@
     by_turn(lambda: case(second_ref, first_ref), lambda: case(first_ref, second_ref))
 
 
-def late_kernel(*refs):
+def ends_kernel(*refs):
     *pieces, first_ref, second_ref = refs
     end_rows(pieces, first_ref, second_ref)
 
@@ -469,23 +472,29 @@
         screened_kernel, cut_up, w, w_sums, w_edge, w_weights, *near_w, flops=16 * product,
         scratch=[pltpu.VMEM((blocks,) + square, BF16)],
     )
-    s_own = to_owners(screened if inside else [screened])
+    if inside:
+        s_own = to_chips(screened)
+        s_other = [to_partner(x) for x in s_own]
+    else:
+        s_own = [to_owners([screened])]
+        s_other = [to_partner(s_own[0])]
     factor = (3.0 * order / count) ** 0.5
-    part, ends = (blocks, parts, piece, order), (bands, parts, piece, order)
+    part = (blocks, parts, piece, order)
     sigma = call(
-        functools.partial(convolve_kernel, factor, inside),
-        [part] * chips + [(1,) + ends] * 2 if inside else [(chips,) + part],
-        g_all, s_own, to_partner(s_own),
+        functools.partial(convolve_kernel, factor, inside, chips),
+        [part] * chips if inside else [(chips,) + part],
+        g_all, *s_own, *s_other,
         scratch=[pltpu.VMEM((size,) + part, BF16) for size in (count, chips)],
     )
-    early = []
-    if inside:
-        *sigma, first, second = sigma
-        early = trade((first, second))
     sigma = from_owners(sigma if inside else [sigma])
-    rest = sigma[len(early) // 2 :]
-    late = trade(call(late_kernel, [(len(rest), bands) + rest[0].shape[1:]] * 2, *rest))
-    near_s = [x for turn in zip(*(pair for pair in (early, late) if pair)) for x in turn]
+
+    def trade_ends(pieces):
+        return trade(call(ends_kernel, [(len(pieces), bands) + pieces[0].shape[1:]] * 2, *pieces))
+
+    half = len(sigma) // 2
+    waves = [trade_ends(sigma[:half])] if half else []
+    waves.append(trade_ends(sigma[half:]))
+    near_s = [x for turn in zip(*waves) for x in turn]
     g_sums, g_edge = call(join_kernel, sums, g, *sigma, flops=24 * product, scratch=[pltpu.VMEM(whole, BF16)])
     out = call(
         functools.partial(dressed_kernel, len(near_s) // 2), [whole],

time: 40.7 us -> 42.8 us (1.052)
  waiting for transfers between devices: 12.9 us -> 16.8 us
  starting transfers between devices: 21.4 us -> 19.6 us
    ppermute x9, waiting for transfers between devices: 6.14 us -> 14.1 us  [to_chips(): lax.ppermute(x, 'energy', [(i, i ^ 2 * s) for i in range(count)])]
    ppermute x8, waiting for transfers between devices: 5.12 us -> 2.67 us  [trade(): lax.ppermute(x, ('energy', 'space'), pairs)]
    ppermute x8, starting transfers between devices: 10.6 us -> 8.84 us  [trade(): lax.ppermute(x, ('energy', 'space'), pairs)]
    ppermute x2 -> x5, waiting for transfers between devices: 1.62 us -> 0.01 us  [to_partner(): return lax.ppermute(x, 'energy', [(i, i ^ 1) for i in range(count)])]
  transfers between devices with their start and end apart: 19 -> 22, of which waited for: 7 -> 10; matrix products, arithmetic and copies ran while one was open for 0% -> 0% of each run, Pallas kernels for 6% -> 7%
where the time goes in v4:
time: 42.8 us; the launch traced here: 42.6 us
  starting transfers between devices  19.6 us (46%)
  waiting for transfers between devices  16.8 us (39%)
  Pallas kernels  4.78 us (11%)
  other arithmetic  1.32 us (3%)
    ppermute x9, waiting for transfers between devices, to_chips(): lax.ppermute(x, 'energy', [(i, i ^ 2 * s) for i in range(count)])  14.1 us
    ppermute x9, starting transfers between devices, to_chips(): lax.ppermute(x, 'energy', [(i, i ^ 2 * s) for i in range(count)])  10.7 us
    ppermute x8, starting transfers between devices, trade(): lax.ppermute(x, ('energy', 'space'), pairs)  8.84 us
    pallas_call x12, Pallas kernels, call(): pl.pallas_call(kernel, out_shape=outs[0] if single else outs, in_specs=[V...  4.78 us
    ppermute x8, waiting for transfers between devices, trade(): lax.ppermute(x, ('energy', 'space'), pairs)  2.67 us
    select_n x1, other arithmetic, zero_where(): return jnp.where(condition, jnp.zeros_like(value), value)  1.24 us
  transfers between devices with their start and end apart: 22, of which 10 were waited for; matrix products, arithmetic and copies ran while one was open for 0% of the time, Pallas kernels for 7%

profile of v4, /device:TPU:0, one launch (start us, length us, event | category | flops | bytes accessed | tf_op | source)
XLA Modules:
  0.0 42.6 jit_solution(15284611912410866868)
XLA Ops:
  0.1 1.2 %bitcast_select_fusion = (bf16[2,3,2,128,128]{4,3,2,1,0:T(8,128)(2,1)S(1)}, bf16[2,3,2,128,128]{4,3,2,1,0:T(8,128)(2,1)S(1)}) fusion(bf16[1,2,3,2,128,128]{5,4,3,2,1,0:T(8,128)(2,1)} %param.4, pred[2,3]{1,0:T(4,128)(4,1)S(1)} %compare_or_fusion, bf16[1,2,3,2,128,128]{5,4,3,2,1,0:T(8,128)(2,1)} %param.3), kind=kLoop, calls=%fused_computation | loop fusion | flops 393216 | bytes 1572870 | tf_op jit(solution)/shard_map/jit(_where)/select_n | solution.py:35
  1.3 0.4 %shard_map.41 = (bf16[5,2,128,128]{3,2,1,0:T(8,128)(2,1)S(1)}, bf16[5,2,128,128]{3,2,1,0:T(8,128)(2,1)S(1)}) custom-call(bf16[2,3,2,128,128]{4,3,2,1,0:T(8,128)(2,1)S(1)} %get-tuple-element.60.w_ref, bf16[2,3,2,128,128]{4,3,2,1,0:T(8,128)(2,1)S(1)} %get-tuple-element.59.p_ref), custom_call_target="tpu_custom_call" | custom-call | flops 100663296 | bytes 1441792 | tf_op jit(solution)/shard_map/pallas_call | solution.py:391
  1.8 3.1 %collective-permute-start.4 = (bf16[5,2,128,128]{3,2,1,0:T(8,128)(2,1)S(1)}, bf16[5,2,128,128]{3,2,1,0:T(8,128)(2,1)S(1)}, u32[]{:S(2)}, u32[]{:S(2)}) collective-permute-start(bf16[5,2,128,128]{3,2,1,0:T(8,128)(2,1)S(1)} %get-tuple-element.39), channel_id=1, source_target_pairs={{0,1},{1,0},{2,3},{3,2},{4,5},{5,4},{6,7},{7,6},{8,9},{9,8},{10,11... | collective-permute-start | bytes 983048 | tf_op jit(solution)/shard_map/ppermute | solution.py:426
  5.0 1.6 %collective-permute-start = (bf16[6,2,32,128]{3,2,1,0:T(8,128)(2,1)S(1)}, bf16[6,2,32,128]{3,2,1,0:T(8,128)(2,1)S(1)}, u32[]{:S(2)}, u32[]{:S(2)}) collective-permute-start(bf16[6,2,32,128]{3,2,1,0:T(8,128)(2,1)S(1)} %get-tuple-element.33), channel_id=1, source_target_pairs={{0,8},{4,12},{8,0},{12,4},{16,24},{20,28},{24,16},{28,20},{1,9},{5... | collective-permute-start | bytes 294920 | tf_op jit(solution)/shard_map/ppermute | solution.py:433
  6.5 1.5 %collective-permute-start.1 = (bf16[6,2,32,128]{3,2,1,0:T(8,128)(2,1)S(1)}, bf16[6,2,32,128]{3,2,1,0:T(8,128)(2,1)S(1)}, u32[]{:S(2)}, u32[]{:S(2)}) collective-permute-start(bf16[6,2,32,128]{3,2,1,0:T(8,128)(2,1)S(1)} %get-tuple-element.34), channel_id=1, source_target_pairs={{0,16},{4,20},{8,24},{12,28},{16,0},{20,4},{24,8},{28,12},{1,17},{... | collective-permute-start | bytes 294920 | tf_op jit(solution)/shard_map/ppermute | solution.py:433
  8.0 0.5 %collective-permute-start.2 = (bf16[6,2,32,128]{3,2,1,0:T(8,128)(2,1)S(1)}, bf16[6,2,32,128]{3,2,1,0:T(8,128)(2,1)S(1)}, u32[]{:S(2)}, u32[]{:S(2)}) collective-permute-start(bf16[6,2,32,128]{3,2,1,0:T(8,128)(2,1)S(1)} %get-tuple-element.35), channel_id=1, source_target_pairs={{0,24},{4,28},{8,16},{12,20},{16,8},{20,12},{24,0},{28,4},{1,25},{... | collective-permute-start | bytes 294920 | tf_op jit(solution)/shard_map/ppermute | solution.py:433
  8.5 1.7 %collective-permute-done.refs_1_ = bf16[6,2,32,128]{3,2,1,0:T(8,128)(2,1)S(1)} collective-permute-done((bf16[6,2,32,128]{3,2,1,0:T(8,128)(2,1)S(1)}, bf16[6,2,32,128]{3,2,1,0:T(8,128)(2,1)S(1)}, u32[]{:S(2)}, u32[]{:S(2)}) %collective-permute-start) | collective-permute-done | bytes 98336 | tf_op jit(solution)/shard_map/ppermute | solution.py:433
  10.2 2.4 %collective-permute-done.1.refs_2_ = bf16[6,2,32,128]{3,2,1,0:T(8,128)(2,1)S(1)} collective-permute-done((bf16[6,2,32,128]{3,2,1,0:T(8,128)(2,1)S(1)}, bf16[6,2,32,128]{3,2,1,0:T(8,128)(2,1)S(1)}, u32[]{:S(2)}, u32[]{:S(2)}) %collective-permute-start.1) | collective-permute-done | bytes 98336 | tf_op jit(solution)/shard_map/ppermute | solution.py:433
  12.6 1.0 %collective-permute-done.2.refs_3_ = bf16[6,2,32,128]{3,2,1,0:T(8,128)(2,1)S(1)} collective-permute-done((bf16[6,2,32,128]{3,2,1,0:T(8,128)(2,1)S(1)}, bf16[6,2,32,128]{3,2,1,0:T(8,128)(2,1)S(1)}, u32[]{:S(2)}, u32[]{:S(2)}) %collective-permute-start.2) | collective-permute-done | bytes 98336 | tf_op jit(solution)/shard_map/ppermute | solution.py:433
  13.7 0.6 %shard_map.40 = (f32[2,3,128,256]{3,2,1,0:T(8,128)S(1)}, bf16[2,2,128,256]{3,2,1,0:T(8,128)(2,1)S(1)}, bf16[2,3,256,256]{3,2,1,0:T(8,128)(2,1)S(1)}) custom-call(bf16[2,3,2,128,128]{4,3,2,1,0:T(8,128)(2,1)S(1)} %get-tuple-element.60.w_ref, bf16[2,3,2,128,128]{4,3,2,1,0:T(8,128)(2,1)S(1)} %get-tuple-element.59.p_ref), custom_call_target="tpu_custom_call" | custom-call | flops 402653184 | bytes 2228224 | tf_op jit(solution)/shard_map/pallas_call | solution.py:391
  14.4 0.6 %shard_map.42 = (bf16[6,2,32,128]{3,2,1,0:T(8,128)(2,1)S(1)}, bf16[6,2,32,128]{3,2,1,0:T(8,128)(2,1)S(1)}, bf16[6,2,32,128]{3,2,1,0:T(8,128)(2,1)S(1)}, bf16[6,2,32,128]{3,2,1,0:T(8,128)(2,1)S(1)}) custom-call(bf16[2,3,2,128,128]{4,3,2,1,0:T(8,128)(2,1)S(1)} %get-tuple-element.60.w_ref, f32[2,3,128,256]{3,2,1,0:T(8,128)S(1)} %get-tuple-element.36.sum_ref, ...), custom_call_target="tpu_custom_call" | custom-call | flops 268435456 | bytes 2883584 | tf_op jit(solution)/shard_map/pallas_call | solution.py:391
  15.0 1.3 %collective-permute-start.6 = (bf16[6,2,32,128]{3,2,1,0:T(8,128)(2,1)S(1)}, bf16[6,2,32,128]{3,2,1,0:T(8,128)(2,1)S(1)}, u32[]{:S(2)}, u32[]{:S(2)}) collective-permute-start(bf16[6,2,32,128]{3,2,1,0:T(8,128)(2,1)S(1)} %get-tuple-element.42), channel_id=1, source_target_pairs={{0,8},{4,12},{8,0},{12,4},{16,24},{20,28},{24,16},{28,20},{1,9},{5... | collective-permute-start | bytes 294920 | tf_op jit(solution)/shard_map/ppermute | solution.py:433
  16.3 0.8 %collective-permute-start.7 = (bf16[6,2,32,128]{3,2,1,0:T(8,128)(2,1)S(1)}, bf16[6,2,32,128]{3,2,1,0:T(8,128)(2,1)S(1)}, u32[]{:S(2)}, u32[]{:S(2)}) collective-permute-start(bf16[6,2,32,128]{3,2,1,0:T(8,128)(2,1)S(1)} %get-tuple-element.43), channel_id=1, source_target_pairs={{0,16},{4,20},{8,24},{12,28},{16,0},{20,4},{24,8},{28,12},{1,17},{... | collective-permute-start | bytes 294920 | tf_op jit(solution)/shard_map/ppermute | solution.py:433
  17.1 1.5 %collective-permute-start.8 = (bf16[6,2,32,128]{3,2,1,0:T(8,128)(2,1)S(1)}, bf16[6,2,32,128]{3,2,1,0:T(8,128)(2,1)S(1)}, u32[]{:S(2)}, u32[]{:S(2)}) collective-permute-start(bf16[6,2,32,128]{3,2,1,0:T(8,128)(2,1)S(1)} %get-tuple-element.44), channel_id=1, source_target_pairs={{0,24},{4,28},{8,16},{12,20},{16,8},{20,12},{24,0},{28,4},{1,25},{... | collective-permute-start | bytes 294920 | tf_op jit(solution)/shard_map/ppermute | solution.py:433
  18.6 1.7 %collective-permute-done.6.refs_1_ = bf16[6,2,32,128]{3,2,1,0:T(8,128)(2,1)S(1)} collective-permute-done((bf16[6,2,32,128]{3,2,1,0:T(8,128)(2,1)S(1)}, bf16[6,2,32,128]{3,2,1,0:T(8,128)(2,1)S(1)}, u32[]{:S(2)}, u32[]{:S(2)}) %collective-permute-start.6) | collective-permute-done | bytes 98336 | tf_op jit(solution)/shard_map/ppermute | solution.py:433
  20.3 1.4 %collective-permute-done.7.refs_2_ = bf16[6,2,32,128]{3,2,1,0:T(8,128)(2,1)S(1)} collective-permute-done((bf16[6,2,32,128]{3,2,1,0:T(8,128)(2,1)S(1)}, bf16[6,2,32,128]{3,2,1,0:T(8,128)(2,1)S(1)}, u32[]{:S(2)}, u32[]{:S(2)}) %collective-permute-start.7) | collective-permute-done | bytes 98336 | tf_op jit(solution)/shard_map/ppermute | solution.py:433
  21.7 1.6 %collective-permute-done.8.refs_3_ = bf16[6,2,32,128]{3,2,1,0:T(8,128)(2,1)S(1)} collective-permute-done((bf16[6,2,32,128]{3,2,1,0:T(8,128)(2,1)S(1)}, bf16[6,2,32,128]{3,2,1,0:T(8,128)(2,1)S(1)}, u32[]{:S(2)}, u32[]{:S(2)}) %collective-permute-start.8) | collective-permute-done | bytes 98336 | tf_op jit(solution)/shard_map/ppermute | solution.py:433
  23.3 2.4 %collective-permute-start.16 = (bf16[3,2,128,128]{3,2,1,0:T(8,128)(2,1)S(1)}, bf16[3,2,128,128]{3,2,1,0:T(8,128)(2,1)S(1)}, u32[]{:S(2)}, u32[]{:S(2)}) collective-permute-start(bf16[3,2,128,128]{3,2,1,0:T(8,128)(2,1)S(1)} %get-tuple-element.51), channel_id=1, source_target_pairs={{0,1},{1,0},{2,3},{3,2},{4,5},{5,4},{6,7},{7,6},{8,9},{9,8},{10,11... | collective-permute-start | bytes 589832 | tf_op jit(solution)/shard_map/ppermute | solution.py:426
  25.7 0.2 collective-permute-start.17
  26.1 0.5 %shard_map.43 = (bf16[6,2,32,128]{3,2,1,0:T(8,128)(2,1)S(1)}, bf16[6,2,32,128]{3,2,1,0:T(8,128)(2,1)S(1)}, bf16[6,2,32,128]{3,2,1,0:T(8,128)(2,1)S(1)}, bf16[6,2,32,128]{3,2,1,0:T(8,128)(2,1)S(1)}) custom-call(bf16[9,6,2,32,128]{4,3,2,1,0:T(8,128)(2,1)S(1)} %shard_map.39.g_ref, bf16[6,2,32,128]{3,2,1,0:T(8,128)(2,1)S(1)} %get-tuple-element.41.refs_0_, ...), custom_call_target="tpu_custom_call" | custom-call | bytes 2064384 | tf_op jit(solution)/shard_map/pallas_call | solution.py:391
  26.5 1.3 %collective-permute-start.14 = (bf16[6,2,32,128]{3,2,1,0:T(8,128)(2,1)S(1)}, bf16[6,2,32,128]{3,2,1,0:T(8,128)(2,1)S(1)}, u32[]{:S(2)}, u32[]{:S(2)}) collective-permute-start(bf16[6,2,32,128]{3,2,1,0:T(8,128)(2,1)S(1)} %get-tuple-element.47), channel_id=1, source_target_pairs={{0,16},{4,20},{8,24},{12,28},{16,0},{20,4},{24,8},{28,12},{1,17},{... | collective-permute-start | bytes 294920 | tf_op jit(solution)/shard_map/ppermute | solution.py:433
  27.8 2.0 %collective-permute-start.15 = (bf16[6,2,32,128]{3,2,1,0:T(8,128)(2,1)S(1)}, bf16[6,2,32,128]{3,2,1,0:T(8,128)(2,1)S(1)}, u32[]{:S(2)}, u32[]{:S(2)}) collective-permute-start(bf16[6,2,32,128]{3,2,1,0:T(8,128)(2,1)S(1)} %get-tuple-element.48), channel_id=1, source_target_pairs={{0,24},{4,28},{8,16},{12,20},{16,8},{20,12},{24,0},{28,4},{1,25},{... | collective-permute-start | bytes 294920 | tf_op jit(solution)/shard_map/ppermute | solution.py:433
  29.9 0.2 collective-permute-start.13
  30.1 2.9 %collective-permute-done.14.refs_3_.refs_0_ = bf16[6,2,32,128]{3,2,1,0:T(8,128)(2,1)S(1)} collective-permute-done((bf16[6,2,32,128]{3,2,1,0:T(8,128)(2,1)S(1)}, bf16[6,2,32,128]{3,2,1,0:T(8,128)(2,1)S(1)}, u32[]{:S(2)}, u32[]{:S(2)}) %collective-permute-start.14) | collective-permute-done | bytes 98336 | tf_op jit(solution)/shard_map/ppermute | solution.py:433
  33.0 1.4 %collective-permute-done.15.refs_4_.refs_1_ = bf16[6,2,32,128]{3,2,1,0:T(8,128)(2,1)S(1)} collective-permute-done((bf16[6,2,32,128]{3,2,1,0:T(8,128)(2,1)S(1)}, bf16[6,2,32,128]{3,2,1,0:T(8,128)(2,1)S(1)}, u32[]{:S(2)}, u32[]{:S(2)}) %collective-permute-start.15) | collective-permute-done | bytes 98336 | tf_op jit(solution)/shard_map/ppermute | solution.py:433
  34.4 1.0 %collective-permute-start.19 = (bf16[2,3,2,32,128]{4,3,2,1,0:T(8,128)(2,1)S(1)}, bf16[2,3,2,32,128]{4,3,2,1,0:T(8,128)(2,1)S(1)}, u32[]{:S(2)}, u32[]{:S(2)}) collective-permute-start(bf16[2,3,2,32,128]{4,3,2,1,0:T(8,128)(2,1)S(1)} %get-tuple-element.56), channel_id=1, source_target_pairs={{0,1},{1,0},{2,3},{3,2},{4,5},{5,4},{6,7},{7,6},{8,9},{9,8},{10,11... | collective-permute-start | bytes 294920 | tf_op jit(solution)/shard_map/ppermute | solution.py:426
  35.5 2.1 %collective-permute-start.18 = (bf16[2,3,2,32,128]{4,3,2,1,0:T(8,128)(2,1)S(1)}, bf16[2,3,2,32,128]{4,3,2,1,0:T(8,128)(2,1)S(1)}, u32[]{:S(2)}, u32[]{:S(2)}) collective-permute-start(bf16[2,3,2,32,128]{4,3,2,1,0:T(8,128)(2,1)S(1)} %get-tuple-element.55), channel_id=1, source_target_pairs={{0,1},{1,0},{2,3},{3,2},{4,5},{5,4},{6,7},{7,6},{8,9},{9,8},{10,11... | collective-permute-start | bytes 294920 | tf_op jit(solution)/shard_map/ppermute | solution.py:426
  37.5 0.4 shard_map.45
  37.9 0.7 %shard_map.44 = (f32[2,3,128,256]{3,2,1,0:T(8,128)S(1)}, bf16[2,2,128,256]{3,2,1,0:T(8,128)(2,1)S(1)}) custom-call(bf16[2,3,2,128,128]{4,3,2,1,0:T(8,128)(2,1)S(1)} %bitcast.8, bf16[6,2,32,128]{3,2,1,0:T(8,128)(2,1)S(1)} %get-tuple-element.45.refs_1_.refs_0_, bf16[6,2,32,128]{3,2,1,0:T(8,128)(2,1)S(1)} %collective-permute-done.13.refs_2_.refs_1_, ...), custom_call_target="tpu_custom_call" | custom-call | flops 402653184 | bytes 1441792 | tf_op jit(solution)/shard_map/pallas_call | solution.py:391
  38.5 1.0 %collective-permute-done.19.rest_1_ = bf16[2,3,2,32,128]{4,3,2,1,0:T(8,128)(2,1)S(1)} collective-permute-done((bf16[2,3,2,32,128]{4,3,2,1,0:T(8,128)(2,1)S(1)}, bf16[2,3,2,32,128]{4,3,2,1,0:T(8,128)(2,1)S(1)}, u32[]{:S(2)}, u32[]{:S(2)}) %collective-permute-start.19) | collective-permute-done | bytes 98336 | tf_op jit(solution)/shard_map/ppermute | solution.py:426
  39.6 1.6 %collective-permute-done.18.rest_0_ = bf16[2,3,2,32,128]{4,3,2,1,0:T(8,128)(2,1)S(1)} collective-permute-done((bf16[2,3,2,32,128]{4,3,2,1,0:T(8,128)(2,1)S(1)}, bf16[2,3,2,32,128]{4,3,2,1,0:T(8,128)(2,1)S(1)}, u32[]{:S(2)}, u32[]{:S(2)}) %collective-permute-start.18) | collective-permute-done | bytes 98336 | tf_op jit(solution)/shard_map/ppermute | solution.py:426
  41.2 1.4 %shard_map.48 = bf16[2,3,2,128,128]{4,3,2,1,0:T(8,128)(2,1)} custom-call(bf16[2,3,2,128,128]{4,3,2,1,0:T(8,128)(2,1)S(1)} %bitcast.9, f32[2,3,128,256]{3,2,1,0:T(8,128)S(1)} %get-tuple-element.49.sum_ref, bf16[2,2,128,256]{3,2,1,0:T(8,128)(2,1)S(1)} %get-tuple-element.50.edge_ref, bf16[2,3,256,256]{3,2,1,0:T(8,128)(2,1)S(1)} %get-tuple-element.53.own_ref, ...), custom_call_target="tpu_custom_call" | custom-call | flops 301989888 | bytes 3407872 | tf_op jit(solution)/shard_map/pallas_call | solution.py:391
  (29 shorter events, 0.4 us)
Async XLA Ops:
  1.3 3.6 %copy-start = (bf16[1,2,3,2,128,128]{5,4,3,2,1,0:T(8,128)(2,1)S(1)}, bf16[1,2,3,2,128,128]{5,4,3,2,1,0:T(8,128)(2,1)}, u32[]{:S(2)}) copy-start(bf16[1,2,3,2,128,128]{5,4,3,2,1,0:T(8,128)(2,1)} %param.5) | copy-start | bytes 1179652
  1.8 12.6 %collective-permute-start.4 = (bf16[5,2,128,128]{3,2,1,0:T(8,128)(2,1)S(1)}, bf16[5,2,128,128]{3,2,1,0:T(8,128)(2,1)S(1)}, u32[]{:S(2)}, u32[]{:S(2)}) collective-permute-start(bf16[5,2,128,128]{3,2,1,0:T(8,128)(2,1)S(1)} %get-tuple-element.39), channel_id=1, source_target_pairs={{0,1},{1,0},{2,3},{3,2},{4,5},{5,4},{6,7},{7,6},{8,9},{9,8},{10,11... | collective-permute-start | bytes 983048 | tf_op jit(solution)/shard_map/ppermute | solution.py:426
  4.9 9.5 %collective-permute-start.5 = (bf16[5,2,128,128]{3,2,1,0:T(8,128)(2,1)S(1)}, bf16[5,2,128,128]{3,2,1,0:T(8,128)(2,1)S(1)}, u32[]{:S(2)}, u32[]{:S(2)}) collective-permute-start(bf16[5,2,128,128]{3,2,1,0:T(8,128)(2,1)S(1)} %get-tuple-element.40), channel_id=1, source_target_pairs={{0,4},{1,2},{2,1},{3,7},{4,0},{5,6},{6,5},{7,3},{8,12},{9,10},{10,... | collective-permute-start | bytes 983048 | tf_op jit(solution)/shard_map/ppermute | solution.py:426
  5.0 5.3 %collective-permute-start = (bf16[6,2,32,128]{3,2,1,0:T(8,128)(2,1)S(1)}, bf16[6,2,32,128]{3,2,1,0:T(8,128)(2,1)S(1)}, u32[]{:S(2)}, u32[]{:S(2)}) collective-permute-start(bf16[6,2,32,128]{3,2,1,0:T(8,128)(2,1)S(1)} %get-tuple-element.33), channel_id=1, source_target_pairs={{0,8},{4,12},{8,0},{12,4},{16,24},{20,28},{24,16},{28,20},{1,9},{5... | collective-permute-start | bytes 294920 | tf_op jit(solution)/shard_map/ppermute | solution.py:433
  6.5 6.1 %collective-permute-start.1 = (bf16[6,2,32,128]{3,2,1,0:T(8,128)(2,1)S(1)}, bf16[6,2,32,128]{3,2,1,0:T(8,128)(2,1)S(1)}, u32[]{:S(2)}, u32[]{:S(2)}) collective-permute-start(bf16[6,2,32,128]{3,2,1,0:T(8,128)(2,1)S(1)} %get-tuple-element.34), channel_id=1, source_target_pairs={{0,16},{4,20},{8,24},{12,28},{16,0},{20,4},{24,8},{28,12},{1,17},{... | collective-permute-start | bytes 294920 | tf_op jit(solution)/shard_map/ppermute | solution.py:433
  8.0 5.5 %collective-permute-start.2 = (bf16[6,2,32,128]{3,2,1,0:T(8,128)(2,1)S(1)}, bf16[6,2,32,128]{3,2,1,0:T(8,128)(2,1)S(1)}, u32[]{:S(2)}, u32[]{:S(2)}) collective-permute-start(bf16[6,2,32,128]{3,2,1,0:T(8,128)(2,1)S(1)} %get-tuple-element.35), channel_id=1, source_target_pairs={{0,24},{4,28},{8,16},{12,20},{16,8},{20,12},{24,0},{28,4},{1,25},{... | collective-permute-start | bytes 294920 | tf_op jit(solution)/shard_map/ppermute | solution.py:433
  13.6 12.1 %collective-permute-start.3 = (bf16[4,6,2,32,128]{4,3,2,1,0:T(8,128)(2,1)S(1)}, bf16[4,6,2,32,128]{4,3,2,1,0:T(8,128)(2,1)S(1)}, u32[]{:S(2)}, u32[]{:S(2)}) collective-permute-start(bf16[4,6,2,32,128]{4,3,2,1,0:T(8,128)(2,1)S(1)} %shard_map.38.own_ref), channel_id=1, source_target_pairs={{0,4},{4,0},{8,12},{12,8},{16,20},{20,16},{24,28},{28,24},{1,5},{5... | collective-permute-start | bytes 1179656 | tf_op jit(solution)/shard_map/ppermute | solution.py:429
  15.0 5.3 %collective-permute-start.6 = (bf16[6,2,32,128]{3,2,1,0:T(8,128)(2,1)S(1)}, bf16[6,2,32,128]{3,2,1,0:T(8,128)(2,1)S(1)}, u32[]{:S(2)}, u32[]{:S(2)}) collective-permute-start(bf16[6,2,32,128]{3,2,1,0:T(8,128)(2,1)S(1)} %get-tuple-element.42), channel_id=1, source_target_pairs={{0,8},{4,12},{8,0},{12,4},{16,24},{20,28},{24,16},{28,20},{1,9},{5... | collective-permute-start | bytes 294920 | tf_op jit(solution)/shard_map/ppermute | solution.py:433
  16.3 5.4 %collective-permute-start.7 = (bf16[6,2,32,128]{3,2,1,0:T(8,128)(2,1)S(1)}, bf16[6,2,32,128]{3,2,1,0:T(8,128)(2,1)S(1)}, u32[]{:S(2)}, u32[]{:S(2)}) collective-permute-start(bf16[6,2,32,128]{3,2,1,0:T(8,128)(2,1)S(1)} %get-tuple-element.43), channel_id=1, source_target_pairs={{0,16},{4,20},{8,24},{12,28},{16,0},{20,4},{24,8},{28,12},{1,17},{... | collective-permute-start | bytes 294920 | tf_op jit(solution)/shard_map/ppermute | solution.py:433
  17.1 6.2 %collective-permute-start.8 = (bf16[6,2,32,128]{3,2,1,0:T(8,128)(2,1)S(1)}, bf16[6,2,32,128]{3,2,1,0:T(8,128)(2,1)S(1)}, u32[]{:S(2)}, u32[]{:S(2)}) collective-permute-start(bf16[6,2,32,128]{3,2,1,0:T(8,128)(2,1)S(1)} %get-tuple-element.44), channel_id=1, source_target_pairs={{0,24},{4,28},{8,16},{12,20},{16,8},{20,12},{24,0},{28,4},{1,25},{... | collective-permute-start | bytes 294920 | tf_op jit(solution)/shard_map/ppermute | solution.py:433
  18.6 4.7 %collective-permute-start.9 = (bf16[6,2,32,128]{3,2,1,0:T(8,128)(2,1)S(1)}, bf16[6,2,32,128]{3,2,1,0:T(8,128)(2,1)S(1)}, u32[]{:S(2)}, u32[]{:S(2)}) collective-permute-start(bf16[6,2,32,128]{3,2,1,0:T(8,128)(2,1)S(1)} %get-tuple-element.41.refs_0_), channel_id=1, source_target_pairs={{0,4},{4,0},{8,12},{12,8},{16,20},{20,16},{24,28},{28,24},{1,5},{5... | collective-permute-start | bytes 294920 | tf_op jit(solution)/shard_map/ppermute | solution.py:429
  20.3 5.8 %collective-permute-start.10 = (bf16[6,2,32,128]{3,2,1,0:T(8,128)(2,1)S(1)}, bf16[6,2,32,128]{3,2,1,0:T(8,128)(2,1)S(1)}, u32[]{:S(2)}, u32[]{:S(2)}) collective-permute-start(bf16[6,2,32,128]{3,2,1,0:T(8,128)(2,1)S(1)} %collective-permute-done.6.refs_1_), channel_id=1, source_target_pairs={{0,4},{4,0},{8,12},{12,8},{16,20},{20,16},{24,28},{28,24},{1,5},{5... | collective-permute-start | bytes 294920 | tf_op jit(solution)/shard_map/ppermute | solution.py:429
  21.7 4.4 %collective-permute-start.11 = (bf16[6,2,32,128]{3,2,1,0:T(8,128)(2,1)S(1)}, bf16[6,2,32,128]{3,2,1,0:T(8,128)(2,1)S(1)}, u32[]{:S(2)}, u32[]{:S(2)}) collective-permute-start(bf16[6,2,32,128]{3,2,1,0:T(8,128)(2,1)S(1)} %collective-permute-done.7.refs_2_), channel_id=1, source_target_pairs={{0,4},{4,0},{8,12},{12,8},{16,20},{20,16},{24,28},{28,24},{1,5},{5... | collective-permute-start | bytes 294920 | tf_op jit(solution)/shard_map/ppermute | solution.py:429
  23.3 2.8 %collective-permute-start.12 = (bf16[6,2,32,128]{3,2,1,0:T(8,128)(2,1)S(1)}, bf16[6,2,32,128]{3,2,1,0:T(8,128)(2,1)S(1)}, u32[]{:S(2)}, u32[]{:S(2)}) collective-permute-start(bf16[6,2,32,128]{3,2,1,0:T(8,128)(2,1)S(1)} %collective-permute-done.8.refs_3_), channel_id=1, source_target_pairs={{0,4},{4,0},{8,12},{12,8},{16,20},{20,16},{24,28},{28,24},{1,5},{5... | collective-permute-start | bytes 294920 | tf_op jit(solution)/shard_map/ppermute | solution.py:429
  23.3 14.2 %collective-permute-start.16 = (bf16[3,2,128,128]{3,2,1,0:T(8,128)(2,1)S(1)}, bf16[3,2,128,128]{3,2,1,0:T(8,128)(2,1)S(1)}, u32[]{:S(2)}, u32[]{:S(2)}) collective-permute-start(bf16[3,2,128,128]{3,2,1,0:T(8,128)(2,1)S(1)} %get-tuple-element.51), channel_id=1, source_target_pairs={{0,1},{1,0},{2,3},{3,2},{4,5},{5,4},{6,7},{7,6},{8,9},{9,8},{10,11... | collective-permute-start | bytes 589832 | tf_op jit(solution)/shard_map/ppermute | solution.py:426
  25.7 11.8 %collective-permute-start.17 = (bf16[3,2,128,128]{3,2,1,0:T(8,128)(2,1)S(1)}, bf16[3,2,128,128]{3,2,1,0:T(8,128)(2,1)S(1)}, u32[]{:S(2)}, u32[]{:S(2)}) collective-permute-start(bf16[3,2,128,128]{3,2,1,0:T(8,128)(2,1)S(1)} %get-tuple-element.52), channel_id=1, source_target_pairs={{0,4},{1,2},{2,1},{3,7},{4,0},{5,6},{6,5},{7,3},{8,12},{9,10},{10,... | collective-permute-start | bytes 589832 | tf_op jit(solution)/shard_map/ppermute | solution.py:426
  26.5 6.4 %collective-permute-start.14 = (bf16[6,2,32,128]{3,2,1,0:T(8,128)(2,1)S(1)}, bf16[6,2,32,128]{3,2,1,0:T(8,128)(2,1)S(1)}, u32[]{:S(2)}, u32[]{:S(2)}) collective-permute-start(bf16[6,2,32,128]{3,2,1,0:T(8,128)(2,1)S(1)} %get-tuple-element.47), channel_id=1, source_target_pairs={{0,16},{4,20},{8,24},{12,28},{16,0},{20,4},{24,8},{28,12},{1,17},{... | collective-permute-start | bytes 294920 | tf_op jit(solution)/shard_map/ppermute | solution.py:433
  27.8 6.6 %collective-permute-start.15 = (bf16[6,2,32,128]{3,2,1,0:T(8,128)(2,1)S(1)}, bf16[6,2,32,128]{3,2,1,0:T(8,128)(2,1)S(1)}, u32[]{:S(2)}, u32[]{:S(2)}) collective-permute-start(bf16[6,2,32,128]{3,2,1,0:T(8,128)(2,1)S(1)} %get-tuple-element.48), channel_id=1, source_target_pairs={{0,24},{4,28},{8,16},{12,20},{16,8},{20,12},{24,0},{28,4},{1,25},{... | collective-permute-start | bytes 294920 | tf_op jit(solution)/shard_map/ppermute | solution.py:433
  29.9 5.6 %collective-permute-start.13 = (bf16[6,2,32,128]{3,2,1,0:T(8,128)(2,1)S(1)}, bf16[6,2,32,128]{3,2,1,0:T(8,128)(2,1)S(1)}, u32[]{:S(2)}, u32[]{:S(2)}) collective-permute-start(bf16[6,2,32,128]{3,2,1,0:T(8,128)(2,1)S(1)} %get-tuple-element.46), channel_id=1, source_target_pairs={{0,8},{4,12},{8,0},{12,4},{16,24},{20,28},{24,16},{28,20},{1,9},{5... | collective-permute-start | bytes 294920 | tf_op jit(solution)/shard_map/ppermute | solution.py:433
  34.4 5.2 %collective-permute-start.19 = (bf16[2,3,2,32,128]{4,3,2,1,0:T(8,128)(2,1)S(1)}, bf16[2,3,2,32,128]{4,3,2,1,0:T(8,128)(2,1)S(1)}, u32[]{:S(2)}, u32[]{:S(2)}) collective-permute-start(bf16[2,3,2,32,128]{4,3,2,1,0:T(8,128)(2,1)S(1)} %get-tuple-element.56), channel_id=1, source_target_pairs={{0,1},{1,0},{2,3},{3,2},{4,5},{5,4},{6,7},{7,6},{8,9},{9,8},{10,11... | collective-permute-start | bytes 294920 | tf_op jit(solution)/shard_map/ppermute | solution.py:426
  35.4 4.2 %collective-permute-start.21 = (bf16[2,3,2,32,128]{4,3,2,1,0:T(8,128)(2,1)S(1)}, bf16[2,3,2,32,128]{4,3,2,1,0:T(8,128)(2,1)S(1)}, u32[]{:S(2)}, u32[]{:S(2)}) collective-permute-start(bf16[2,3,2,32,128]{4,3,2,1,0:T(8,128)(2,1)S(1)} %get-tuple-element.58), channel_id=1, source_target_pairs={{0,4},{1,2},{2,1},{3,7},{4,0},{5,6},{6,5},{7,3},{8,12},{9,10},{10,... | collective-permute-start | bytes 294920 | tf_op jit(solution)/shard_map/ppermute | solution.py:426
  35.5 5.8 %collective-permute-start.18 = (bf16[2,3,2,32,128]{4,3,2,1,0:T(8,128)(2,1)S(1)}, bf16[2,3,2,32,128]{4,3,2,1,0:T(8,128)(2,1)S(1)}, u32[]{:S(2)}, u32[]{:S(2)}) collective-permute-start(bf16[2,3,2,32,128]{4,3,2,1,0:T(8,128)(2,1)S(1)} %get-tuple-element.55), channel_id=1, source_target_pairs={{0,1},{1,0},{2,3},{3,2},{4,5},{5,4},{6,7},{7,6},{8,9},{9,8},{10,11... | collective-permute-start | bytes 294920 | tf_op jit(solution)/shard_map/ppermute | solution.py:426
  37.5 3.7 %collective-permute-start.20 = (bf16[2,3,2,32,128]{4,3,2,1,0:T(8,128)(2,1)S(1)}, bf16[2,3,2,32,128]{4,3,2,1,0:T(8,128)(2,1)S(1)}, u32[]{:S(2)}, u32[]{:S(2)}) collective-permute-start(bf16[2,3,2,32,128]{4,3,2,1,0:T(8,128)(2,1)S(1)} %get-tuple-element.57), channel_id=1, source_target_pairs={{0,4},{1,2},{2,1},{3,7},{4,0},{5,6},{6,5},{7,3},{8,12},{9,10},{10,... | collective-permute-start | bytes 294920 | tf_op jit(solution)/shard_map/ppermute | solution.py:426

commit v5 on v4

--- a/solution.py
+++ b/solution.py
@@ -89,6 +89,12 @@
     pl.when(jnp.logical_not(even))(odd_case)
 
 
+def by_place(first_case, second_case):
+    _, place = owner()
+    pl.when(place == 0)(first_case)
+    pl.when(place != 0)(second_case)
+
+
 def missing_sides():
     place = lax.axis_index("space")
     return place == 0, place == lax.axis_size("space") - 1
@@ -99,14 +105,14 @@
     return lax.shift_right_logical(index, 1), lax.bitwise_and(index, 1)
 
 
-def fill(first_ref, second_ref, band, write):
+def fill(first_ref, second_ref, band, write, choose=by_turn):
     below, above = band.ends()
 
     def case(below_ref, above_ref):
         write(below_ref, *below)
         write(above_ref, *above)
 
-    by_turn(lambda: case(second_ref, first_ref), lambda: case(first_ref, second_ref))
+    choose(lambda: case(second_ref, first_ref), lambda: case(first_ref, second_ref))
 
 
 def send_kernel(w_ref, p_ref, first_ref, second_ref):
@@ -118,7 +124,7 @@
             store_pair(ref, at + 1, band.pair(row, past))
         store_row(ref, 4, own_adjoint(outer, inner, row))
 
-    fill(first_ref, second_ref, outer, write)
+    fill(first_ref, second_ref, outer, write, by_place)
 
 
 def own_weights(outer, weight_ref):
@@ -216,7 +222,7 @@
                 total += times_adjoint(edge_ref[side, n], load_square(refs[side], 2 + n))
             store(row, past - row + 1, zero_where(gone, total).astype(BF16))
 
-    by_turn(lambda: run(second_ref, first_ref), lambda: run(first_ref, second_ref))
+    by_place(lambda: run(first_ref, second_ref), lambda: run(second_ref, first_ref))
     cut(whole_ref, out_refs)
 
 
@@ -409,11 +415,22 @@
     ]
 
 
+def shifts(turn, peers, count):
+    pairs = []
+    for e in range(count):
+        step = 1 if e % 2 == turn else -1
+        for z in range(peers):
+            target = (e, z + step) if 0 <= z + step < peers else (e ^ 1, z)
+            pairs.append((e * peers + z, target[0] * peers + target[1]))
+    return pairs
+
+
 def local(screening, polarization, propagator):
     w, p, g = screening[0], polarization[0], propagator[0]
     rows, bands, parts, order = w.shape[0], w.shape[1], w.shape[2], w.shape[3]
     peers, count = lax.axis_size("space"), lax.axis_size("energy")
     turns = [trades(start, peers, count) for start in range(2)]
+    rounds = [shifts(start, peers, count) for start in range(2)]
     chips = count // 2
     piece = order // chips
     inside = piece % PACK == 0
@@ -422,7 +439,7 @@
     whole, square = (rows, bands, parts, order, order), (parts, order, order)
     blocks = rows * bands
 
-    def trade(buffers):
+    def trade(buffers, turns=turns):
         return [lax.ppermute(x, ("energy", "space"), pairs) for x, pairs in zip(buffers, turns)]
 
     def to_partner(x):
@@ -457,7 +474,7 @@
     past = (row[:, None] + band[None, :] == 0) | (row[:, None] + band[None, :] == peers * rows + 1)
     w, p = (zero_where(past[:, :, None, None, None], x) for x in (w, p))
 
-    near_w = trade(call(send_kernel, [(5,) + square] * 2, w, p, flops=6 * product))
+    near_w = trade(call(send_kernel, [(5,) + square] * 2, w, p, flops=6 * product), rounds)
     near_g = [(bands,) + square] * 2
     g_first, g_second, *g_pieces = call(split_kernel, near_g + (cut_up if inside else []), g)
     g_own = to_owners(g_pieces or [g.reshape((blocks,) + square)])

time: 42.8 us -> 42.9 us (level)
  starting transfers between devices: 19.6 us -> 20.2 us
  waiting for transfers between devices: 16.8 us -> 16.3 us
    ppermute x9, waiting for transfers between devices: 14.1 us -> 13.5 us  [to_chips(): lax.ppermute(x, 'energy', [(i, i ^ 2 * s) for i in range(count)])]
    ppermute x5, starting transfers between devices: 0.08 us -> 0.59 us  [to_partner(): return lax.ppermute(x, 'energy', [(i, i ^ 1) for i in range(count)])]
  transfers between devices with their start and end apart: 22 -> 22, of which waited for: 10 -> 9; matrix products, arithmetic and copies ran while one was open for 0% -> 0% of each run, Pallas kernels for 7% -> 7%
where the time goes in v5:
time: 42.9 us; the launch traced here: 42.7 us
  starting transfers between devices  20.2 us (47%)
  waiting for transfers between devices  16.3 us (38%)
  Pallas kernels  4.77 us (11%)
  other arithmetic  1.32 us (3%)
    ppermute x9, waiting for transfers between devices, to_chips(): lax.ppermute(x, 'energy', [(i, i ^ 2 * s) for i in range(count)])  13.5 us
    ppermute x9, starting transfers between devices, to_chips(): lax.ppermute(x, 'energy', [(i, i ^ 2 * s) for i in range(count)])  10.7 us
    ppermute x8, starting transfers between devices, trade(): lax.ppermute(x, ('energy', 'space'), pairs)  8.95 us
    pallas_call x12, Pallas kernels, call(): pl.pallas_call(kernel, out_shape=outs[0] if single else outs, in_specs=[V...  4.77 us
    ppermute x8, waiting for transfers between devices, trade(): lax.ppermute(x, ('energy', 'space'), pairs)  2.81 us
    select_n x1, other arithmetic, zero_where(): return jnp.where(condition, jnp.zeros_like(value), value)  1.24 us
  transfers between devices with their start and end apart: 22, of which 9 were waited for; matrix products, arithmetic and copies ran while one was open for 0% of the time, Pallas kernels for 7%

profile of v5, /device:TPU:0, one launch (start us, length us, event | category | flops | bytes accessed | tf_op | source)
XLA Modules:
  0.0 42.7 jit_solution(17954687827135360421)
XLA Ops:
  0.1 1.2 %bitcast_select_fusion = (bf16[2,3,2,128,128]{4,3,2,1,0:T(8,128)(2,1)S(1)}, bf16[2,3,2,128,128]{4,3,2,1,0:T(8,128)(2,1)S(1)}) fusion(bf16[1,2,3,2,128,128]{5,4,3,2,1,0:T(8,128)(2,1)} %param.4, pred[2,3]{1,0:T(4,128)(4,1)S(1)} %compare_or_fusion, bf16[1,2,3,2,128,128]{5,4,3,2,1,0:T(8,128)(2,1)} %param.3), kind=kLoop, calls=%fused_computation | loop fusion | flops 393216 | bytes 1572870 | tf_op jit(solution)/shard_map/jit(_where)/select_n | solution.py:35
  1.3 0.4 %shard_map.41 = (bf16[5,2,128,128]{3,2,1,0:T(8,128)(2,1)S(1)}, bf16[5,2,128,128]{3,2,1,0:T(8,128)(2,1)S(1)}) custom-call(bf16[2,3,2,128,128]{4,3,2,1,0:T(8,128)(2,1)S(1)} %get-tuple-element.60.w_ref, bf16[2,3,2,128,128]{4,3,2,1,0:T(8,128)(2,1)S(1)} %get-tuple-element.59.p_ref), custom_call_target="tpu_custom_call" | custom-call | flops 100663296 | bytes 1441792 | tf_op jit(solution)/shard_map/pallas_call | solution.py:397
  1.8 3.1 %collective-permute-start.4 = (bf16[5,2,128,128]{3,2,1,0:T(8,128)(2,1)S(1)}, bf16[5,2,128,128]{3,2,1,0:T(8,128)(2,1)S(1)}, u32[]{:S(2)}, u32[]{:S(2)}) collective-permute-start(bf16[5,2,128,128]{3,2,1,0:T(8,128)(2,1)S(1)} %get-tuple-element.39), channel_id=1, source_target_pairs={{0,1},{1,2},{2,3},{3,7},{4,0},{5,4},{6,5},{7,6},{8,9},{9,10},{10,1... | collective-permute-start | bytes 983048 | tf_op jit(solution)/shard_map/ppermute | solution.py:443
  4.9 1.6 %collective-permute-start = (bf16[6,2,32,128]{3,2,1,0:T(8,128)(2,1)S(1)}, bf16[6,2,32,128]{3,2,1,0:T(8,128)(2,1)S(1)}, u32[]{:S(2)}, u32[]{:S(2)}) collective-permute-start(bf16[6,2,32,128]{3,2,1,0:T(8,128)(2,1)S(1)} %get-tuple-element.33), channel_id=1, source_target_pairs={{0,8},{4,12},{8,0},{12,4},{16,24},{20,28},{24,16},{28,20},{1,9},{5... | collective-permute-start | bytes 294920 | tf_op jit(solution)/shard_map/ppermute | solution.py:450
  6.5 1.5 %collective-permute-start.1 = (bf16[6,2,32,128]{3,2,1,0:T(8,128)(2,1)S(1)}, bf16[6,2,32,128]{3,2,1,0:T(8,128)(2,1)S(1)}, u32[]{:S(2)}, u32[]{:S(2)}) collective-permute-start(bf16[6,2,32,128]{3,2,1,0:T(8,128)(2,1)S(1)} %get-tuple-element.34), channel_id=1, source_target_pairs={{0,16},{4,20},{8,24},{12,28},{16,0},{20,4},{24,8},{28,12},{1,17},{... | collective-permute-start | bytes 294920 | tf_op jit(solution)/shard_map/ppermute | solution.py:450
  8.0 0.5 %collective-permute-start.2 = (bf16[6,2,32,128]{3,2,1,0:T(8,128)(2,1)S(1)}, bf16[6,2,32,128]{3,2,1,0:T(8,128)(2,1)S(1)}, u32[]{:S(2)}, u32[]{:S(2)}) collective-permute-start(bf16[6,2,32,128]{3,2,1,0:T(8,128)(2,1)S(1)} %get-tuple-element.35), channel_id=1, source_target_pairs={{0,24},{4,28},{8,16},{12,20},{16,8},{20,12},{24,0},{28,4},{1,25},{... | collective-permute-start | bytes 294920 | tf_op jit(solution)/shard_map/ppermute | solution.py:450
  8.5 1.1 %collective-permute-done.refs_1_ = bf16[6,2,32,128]{3,2,1,0:T(8,128)(2,1)S(1)} collective-permute-done((bf16[6,2,32,128]{3,2,1,0:T(8,128)(2,1)S(1)}, bf16[6,2,32,128]{3,2,1,0:T(8,128)(2,1)S(1)}, u32[]{:S(2)}, u32[]{:S(2)}) %collective-permute-start) | collective-permute-done | bytes 98336 | tf_op jit(solution)/shard_map/ppermute | solution.py:450
  9.6 2.5 %collective-permute-done.1.refs_2_ = bf16[6,2,32,128]{3,2,1,0:T(8,128)(2,1)S(1)} collective-permute-done((bf16[6,2,32,128]{3,2,1,0:T(8,128)(2,1)S(1)}, bf16[6,2,32,128]{3,2,1,0:T(8,128)(2,1)S(1)}, u32[]{:S(2)}, u32[]{:S(2)}) %collective-permute-start.1) | collective-permute-done | bytes 98336 | tf_op jit(solution)/shard_map/ppermute | solution.py:450
  12.1 1.4 %collective-permute-done.2.refs_3_ = bf16[6,2,32,128]{3,2,1,0:T(8,128)(2,1)S(1)} collective-permute-done((bf16[6,2,32,128]{3,2,1,0:T(8,128)(2,1)S(1)}, bf16[6,2,32,128]{3,2,1,0:T(8,128)(2,1)S(1)}, u32[]{:S(2)}, u32[]{:S(2)}) %collective-permute-start.2) | collective-permute-done | bytes 98336 | tf_op jit(solution)/shard_map/ppermute | solution.py:450
  13.6 0.6 %shard_map.40 = (f32[2,3,128,256]{3,2,1,0:T(8,128)S(1)}, bf16[2,2,128,256]{3,2,1,0:T(8,128)(2,1)S(1)}, bf16[2,3,256,256]{3,2,1,0:T(8,128)(2,1)S(1)}) custom-call(bf16[2,3,2,128,128]{4,3,2,1,0:T(8,128)(2,1)S(1)} %get-tuple-element.60.w_ref, bf16[2,3,2,128,128]{4,3,2,1,0:T(8,128)(2,1)S(1)} %get-tuple-element.59.p_ref), custom_call_target="tpu_custom_call" | custom-call | flops 402653184 | bytes 2228224 | tf_op jit(solution)/shard_map/pallas_call | solution.py:397
  14.3 0.6 %shard_map.42 = (bf16[6,2,32,128]{3,2,1,0:T(8,128)(2,1)S(1)}, bf16[6,2,32,128]{3,2,1,0:T(8,128)(2,1)S(1)}, bf16[6,2,32,128]{3,2,1,0:T(8,128)(2,1)S(1)}, bf16[6,2,32,128]{3,2,1,0:T(8,128)(2,1)S(1)}) custom-call(bf16[2,3,2,128,128]{4,3,2,1,0:T(8,128)(2,1)S(1)} %get-tuple-element.60.w_ref, f32[2,3,128,256]{3,2,1,0:T(8,128)S(1)} %get-tuple-element.36.sum_ref, ...), custom_call_target="tpu_custom_call" | custom-call | flops 268435456 | bytes 2883584 | tf_op jit(solution)/shard_map/pallas_call | solution.py:397
  14.9 0.7 %collective-permute-start.6 = (bf16[6,2,32,128]{3,2,1,0:T(8,128)(2,1)S(1)}, bf16[6,2,32,128]{3,2,1,0:T(8,128)(2,1)S(1)}, u32[]{:S(2)}, u32[]{:S(2)}) collective-permute-start(bf16[6,2,32,128]{3,2,1,0:T(8,128)(2,1)S(1)} %get-tuple-element.42), channel_id=1, source_target_pairs={{0,8},{4,12},{8,0},{12,4},{16,24},{20,28},{24,16},{28,20},{1,9},{5... | collective-permute-start | bytes 294920 | tf_op jit(solution)/shard_map/ppermute | solution.py:450
  15.6 0.8 %collective-permute-start.7 = (bf16[6,2,32,128]{3,2,1,0:T(8,128)(2,1)S(1)}, bf16[6,2,32,128]{3,2,1,0:T(8,128)(2,1)S(1)}, u32[]{:S(2)}, u32[]{:S(2)}) collective-permute-start(bf16[6,2,32,128]{3,2,1,0:T(8,128)(2,1)S(1)} %get-tuple-element.43), channel_id=1, source_target_pairs={{0,16},{4,20},{8,24},{12,28},{16,0},{20,4},{24,8},{28,12},{1,17},{... | collective-permute-start | bytes 294920 | tf_op jit(solution)/shard_map/ppermute | solution.py:450
  16.5 2.0 %collective-permute-start.8 = (bf16[6,2,32,128]{3,2,1,0:T(8,128)(2,1)S(1)}, bf16[6,2,32,128]{3,2,1,0:T(8,128)(2,1)S(1)}, u32[]{:S(2)}, u32[]{:S(2)}) collective-permute-start(bf16[6,2,32,128]{3,2,1,0:T(8,128)(2,1)S(1)} %get-tuple-element.44), channel_id=1, source_target_pairs={{0,24},{4,28},{8,16},{12,20},{16,8},{20,12},{24,0},{28,4},{1,25},{... | collective-permute-start | bytes 294920 | tf_op jit(solution)/shard_map/ppermute | solution.py:450
  18.5 2.2 %collective-permute-done.6.refs_1_ = bf16[6,2,32,128]{3,2,1,0:T(8,128)(2,1)S(1)} collective-permute-done((bf16[6,2,32,128]{3,2,1,0:T(8,128)(2,1)S(1)}, bf16[6,2,32,128]{3,2,1,0:T(8,128)(2,1)S(1)}, u32[]{:S(2)}, u32[]{:S(2)}) %collective-permute-start.6) | collective-permute-done | bytes 98336 | tf_op jit(solution)/shard_map/ppermute | solution.py:450
  20.7 2.0 %collective-permute-done.7.refs_2_ = bf16[6,2,32,128]{3,2,1,0:T(8,128)(2,1)S(1)} collective-permute-done((bf16[6,2,32,128]{3,2,1,0:T(8,128)(2,1)S(1)}, bf16[6,2,32,128]{3,2,1,0:T(8,128)(2,1)S(1)}, u32[]{:S(2)}, u32[]{:S(2)}) %collective-permute-start.7) | collective-permute-done | bytes 98336 | tf_op jit(solution)/shard_map/ppermute | solution.py:450
  22.7 0.5 %collective-permute-start.12 = (bf16[6,2,32,128]{3,2,1,0:T(8,128)(2,1)S(1)}, bf16[6,2,32,128]{3,2,1,0:T(8,128)(2,1)S(1)}, u32[]{:S(2)}, u32[]{:S(2)}) collective-permute-start(bf16[6,2,32,128]{3,2,1,0:T(8,128)(2,1)S(1)} %collective-permute-done.8.refs_3_), channel_id=1, source_target_pairs={{0,4},{4,0},{8,12},{12,8},{16,20},{20,16},{24,28},{28,24},{1,5},{5... | collective-permute-start | bytes 294920 | tf_op jit(solution)/shard_map/ppermute | solution.py:446
  23.2 1.4 %collective-permute-start.16 = (bf16[3,2,128,128]{3,2,1,0:T(8,128)(2,1)S(1)}, bf16[3,2,128,128]{3,2,1,0:T(8,128)(2,1)S(1)}, u32[]{:S(2)}, u32[]{:S(2)}) collective-permute-start(bf16[3,2,128,128]{3,2,1,0:T(8,128)(2,1)S(1)} %get-tuple-element.51), channel_id=1, source_target_pairs={{0,1},{1,0},{2,3},{3,2},{4,5},{5,4},{6,7},{7,6},{8,9},{9,8},{10,11... | collective-permute-start | bytes 589832 | tf_op jit(solution)/shard_map/ppermute | solution.py:443
  24.6 0.2 collective-permute-start.17
  24.9 0.5 %shard_map.43 = (bf16[6,2,32,128]{3,2,1,0:T(8,128)(2,1)S(1)}, bf16[6,2,32,128]{3,2,1,0:T(8,128)(2,1)S(1)}, bf16[6,2,32,128]{3,2,1,0:T(8,128)(2,1)S(1)}, bf16[6,2,32,128]{3,2,1,0:T(8,128)(2,1)S(1)}) custom-call(bf16[9,6,2,32,128]{4,3,2,1,0:T(8,128)(2,1)S(1)} %shard_map.39.g_ref, bf16[6,2,32,128]{3,2,1,0:T(8,128)(2,1)S(1)} %get-tuple-element.41.refs_0_, ...), custom_call_target="tpu_custom_call" | custom-call | bytes 2064384 | tf_op jit(solution)/shard_map/pallas_call | solution.py:397
  25.4 1.3 %collective-permute-start.14 = (bf16[6,2,32,128]{3,2,1,0:T(8,128)(2,1)S(1)}, bf16[6,2,32,128]{3,2,1,0:T(8,128)(2,1)S(1)}, u32[]{:S(2)}, u32[]{:S(2)}) collective-permute-start(bf16[6,2,32,128]{3,2,1,0:T(8,128)(2,1)S(1)} %get-tuple-element.47), channel_id=1, source_target_pairs={{0,16},{4,20},{8,24},{12,28},{16,0},{20,4},{24,8},{28,12},{1,17},{... | collective-permute-start | bytes 294920 | tf_op jit(solution)/shard_map/ppermute | solution.py:450
  26.6 2.0 %collective-permute-start.15 = (bf16[6,2,32,128]{3,2,1,0:T(8,128)(2,1)S(1)}, bf16[6,2,32,128]{3,2,1,0:T(8,128)(2,1)S(1)}, u32[]{:S(2)}, u32[]{:S(2)}) collective-permute-start(bf16[6,2,32,128]{3,2,1,0:T(8,128)(2,1)S(1)} %get-tuple-element.48), channel_id=1, source_target_pairs={{0,24},{4,28},{8,16},{12,20},{16,8},{20,12},{24,0},{28,4},{1,25},{... | collective-permute-start | bytes 294920 | tf_op jit(solution)/shard_map/ppermute | solution.py:450
  28.7 0.3 collective-permute-start.13
  28.9 2.9 %collective-permute-done.14.refs_3_.refs_0_ = bf16[6,2,32,128]{3,2,1,0:T(8,128)(2,1)S(1)} collective-permute-done((bf16[6,2,32,128]{3,2,1,0:T(8,128)(2,1)S(1)}, bf16[6,2,32,128]{3,2,1,0:T(8,128)(2,1)S(1)}, u32[]{:S(2)}, u32[]{:S(2)}) %collective-permute-start.14) | collective-permute-done | bytes 98336 | tf_op jit(solution)/shard_map/ppermute | solution.py:450
  31.9 1.3 %collective-permute-done.15.refs_4_.refs_1_ = bf16[6,2,32,128]{3,2,1,0:T(8,128)(2,1)S(1)} collective-permute-done((bf16[6,2,32,128]{3,2,1,0:T(8,128)(2,1)S(1)}, bf16[6,2,32,128]{3,2,1,0:T(8,128)(2,1)S(1)}, u32[]{:S(2)}, u32[]{:S(2)}) %collective-permute-start.15) | collective-permute-done | bytes 98336 | tf_op jit(solution)/shard_map/ppermute | solution.py:450
  33.2 2.8 %collective-permute-start.19 = (bf16[2,3,2,32,128]{4,3,2,1,0:T(8,128)(2,1)S(1)}, bf16[2,3,2,32,128]{4,3,2,1,0:T(8,128)(2,1)S(1)}, u32[]{:S(2)}, u32[]{:S(2)}) collective-permute-start(bf16[2,3,2,32,128]{4,3,2,1,0:T(8,128)(2,1)S(1)} %get-tuple-element.56), channel_id=1, source_target_pairs={{0,1},{1,0},{2,3},{3,2},{4,5},{5,4},{6,7},{7,6},{8,9},{9,8},{10,11... | collective-permute-start | bytes 294920 | tf_op jit(solution)/shard_map/ppermute | solution.py:443
  36.1 1.4 %collective-permute-start.18 = (bf16[2,3,2,32,128]{4,3,2,1,0:T(8,128)(2,1)S(1)}, bf16[2,3,2,32,128]{4,3,2,1,0:T(8,128)(2,1)S(1)}, u32[]{:S(2)}, u32[]{:S(2)}) collective-permute-start(bf16[2,3,2,32,128]{4,3,2,1,0:T(8,128)(2,1)S(1)} %get-tuple-element.55), channel_id=1, source_target_pairs={{0,1},{1,0},{2,3},{3,2},{4,5},{5,4},{6,7},{7,6},{8,9},{9,8},{10,11... | collective-permute-start | bytes 294920 | tf_op jit(solution)/shard_map/ppermute | solution.py:443
  37.5 0.4 shard_map.45
  37.9 0.7 %shard_map.44 = (f32[2,3,128,256]{3,2,1,0:T(8,128)S(1)}, bf16[2,2,128,256]{3,2,1,0:T(8,128)(2,1)S(1)}) custom-call(bf16[2,3,2,128,128]{4,3,2,1,0:T(8,128)(2,1)S(1)} %bitcast.8, bf16[6,2,32,128]{3,2,1,0:T(8,128)(2,1)S(1)} %get-tuple-element.45.refs_1_.refs_0_, bf16[6,2,32,128]{3,2,1,0:T(8,128)(2,1)S(1)} %collective-permute-done.13.refs_2_.refs_1_, ...), custom_call_target="tpu_custom_call" | custom-call | flops 402653184 | bytes 1441792 | tf_op jit(solution)/shard_map/pallas_call | solution.py:397
  38.5 0.6 %collective-permute-done.19.rest_1_ = bf16[2,3,2,32,128]{4,3,2,1,0:T(8,128)(2,1)S(1)} collective-permute-done((bf16[2,3,2,32,128]{4,3,2,1,0:T(8,128)(2,1)S(1)}, bf16[2,3,2,32,128]{4,3,2,1,0:T(8,128)(2,1)S(1)}, u32[]{:S(2)}, u32[]{:S(2)}) %collective-permute-start.19) | collective-permute-done | bytes 98336 | tf_op jit(solution)/shard_map/ppermute | solution.py:443
  39.1 2.2 %collective-permute-done.18.rest_0_ = bf16[2,3,2,32,128]{4,3,2,1,0:T(8,128)(2,1)S(1)} collective-permute-done((bf16[2,3,2,32,128]{4,3,2,1,0:T(8,128)(2,1)S(1)}, bf16[2,3,2,32,128]{4,3,2,1,0:T(8,128)(2,1)S(1)}, u32[]{:S(2)}, u32[]{:S(2)}) %collective-permute-start.18) | collective-permute-done | bytes 98336 | tf_op jit(solution)/shard_map/ppermute | solution.py:443
  41.3 1.4 %shard_map.48 = bf16[2,3,2,128,128]{4,3,2,1,0:T(8,128)(2,1)} custom-call(bf16[2,3,2,128,128]{4,3,2,1,0:T(8,128)(2,1)S(1)} %bitcast.9, f32[2,3,128,256]{3,2,1,0:T(8,128)S(1)} %get-tuple-element.49.sum_ref, bf16[2,2,128,256]{3,2,1,0:T(8,128)(2,1)S(1)} %get-tuple-element.50.edge_ref, bf16[2,3,256,256]{3,2,1,0:T(8,128)(2,1)S(1)} %get-tuple-element.53.own_ref, ...), custom_call_target="tpu_custom_call" | custom-call | flops 301989888 | bytes 3407872 | tf_op jit(solution)/shard_map/pallas_call | solution.py:397
  (29 shorter events, 0.4 us)
Async XLA Ops:
  1.3 3.5 %copy-start = (bf16[1,2,3,2,128,128]{5,4,3,2,1,0:T(8,128)(2,1)S(1)}, bf16[1,2,3,2,128,128]{5,4,3,2,1,0:T(8,128)(2,1)}, u32[]{:S(2)}) copy-start(bf16[1,2,3,2,128,128]{5,4,3,2,1,0:T(8,128)(2,1)} %param.5) | copy-start | bytes 1179652
  1.8 12.5 %collective-permute-start.4 = (bf16[5,2,128,128]{3,2,1,0:T(8,128)(2,1)S(1)}, bf16[5,2,128,128]{3,2,1,0:T(8,128)(2,1)S(1)}, u32[]{:S(2)}, u32[]{:S(2)}) collective-permute-start(bf16[5,2,128,128]{3,2,1,0:T(8,128)(2,1)S(1)} %get-tuple-element.39), channel_id=1, source_target_pairs={{0,1},{1,2},{2,3},{3,7},{4,0},{5,4},{6,5},{7,6},{8,9},{9,10},{10,1... | collective-permute-start | bytes 983048 | tf_op jit(solution)/shard_map/ppermute | solution.py:443
  4.8 9.4 %collective-permute-start.5 = (bf16[5,2,128,128]{3,2,1,0:T(8,128)(2,1)S(1)}, bf16[5,2,128,128]{3,2,1,0:T(8,128)(2,1)S(1)}, u32[]{:S(2)}, u32[]{:S(2)}) collective-permute-start(bf16[5,2,128,128]{3,2,1,0:T(8,128)(2,1)S(1)} %get-tuple-element.40), channel_id=1, source_target_pairs={{0,4},{1,0},{2,1},{3,2},{4,5},{5,6},{6,7},{7,3},{8,12},{9,8},{10,9... | collective-permute-start | bytes 983048 | tf_op jit(solution)/shard_map/ppermute | solution.py:443
  4.9 4.7 %collective-permute-start = (bf16[6,2,32,128]{3,2,1,0:T(8,128)(2,1)S(1)}, bf16[6,2,32,128]{3,2,1,0:T(8,128)(2,1)S(1)}, u32[]{:S(2)}, u32[]{:S(2)}) collective-permute-start(bf16[6,2,32,128]{3,2,1,0:T(8,128)(2,1)S(1)} %get-tuple-element.33), channel_id=1, source_target_pairs={{0,8},{4,12},{8,0},{12,4},{16,24},{20,28},{24,16},{28,20},{1,9},{5... | collective-permute-start | bytes 294920 | tf_op jit(solution)/shard_map/ppermute | solution.py:450
  6.5 5.7 %collective-permute-start.1 = (bf16[6,2,32,128]{3,2,1,0:T(8,128)(2,1)S(1)}, bf16[6,2,32,128]{3,2,1,0:T(8,128)(2,1)S(1)}, u32[]{:S(2)}, u32[]{:S(2)}) collective-permute-start(bf16[6,2,32,128]{3,2,1,0:T(8,128)(2,1)S(1)} %get-tuple-element.34), channel_id=1, source_target_pairs={{0,16},{4,20},{8,24},{12,28},{16,0},{20,4},{24,8},{28,12},{1,17},{... | collective-permute-start | bytes 294920 | tf_op jit(solution)/shard_map/ppermute | solution.py:450
  8.0 5.5 %collective-permute-start.2 = (bf16[6,2,32,128]{3,2,1,0:T(8,128)(2,1)S(1)}, bf16[6,2,32,128]{3,2,1,0:T(8,128)(2,1)S(1)}, u32[]{:S(2)}, u32[]{:S(2)}) collective-permute-start(bf16[6,2,32,128]{3,2,1,0:T(8,128)(2,1)S(1)} %get-tuple-element.35), channel_id=1, source_target_pairs={{0,24},{4,28},{8,16},{12,20},{16,8},{20,12},{24,0},{28,4},{1,25},{... | collective-permute-start | bytes 294920 | tf_op jit(solution)/shard_map/ppermute | solution.py:450
  13.5 11.0 %collective-permute-start.3 = (bf16[4,6,2,32,128]{4,3,2,1,0:T(8,128)(2,1)S(1)}, bf16[4,6,2,32,128]{4,3,2,1,0:T(8,128)(2,1)S(1)}, u32[]{:S(2)}, u32[]{:S(2)}) collective-permute-start(bf16[4,6,2,32,128]{4,3,2,1,0:T(8,128)(2,1)S(1)} %shard_map.38.own_ref), channel_id=1, source_target_pairs={{0,4},{4,0},{8,12},{12,8},{16,20},{20,16},{24,28},{28,24},{1,5},{5... | collective-permute-start | bytes 1179656 | tf_op jit(solution)/shard_map/ppermute | solution.py:446
  14.9 5.7 %collective-permute-start.6 = (bf16[6,2,32,128]{3,2,1,0:T(8,128)(2,1)S(1)}, bf16[6,2,32,128]{3,2,1,0:T(8,128)(2,1)S(1)}, u32[]{:S(2)}, u32[]{:S(2)}) collective-permute-start(bf16[6,2,32,128]{3,2,1,0:T(8,128)(2,1)S(1)} %get-tuple-element.42), channel_id=1, source_target_pairs={{0,8},{4,12},{8,0},{12,4},{16,24},{20,28},{24,16},{28,20},{1,9},{5... | collective-permute-start | bytes 294920 | tf_op jit(solution)/shard_map/ppermute | solution.py:450
  15.6 7.0 %collective-permute-start.7 = (bf16[6,2,32,128]{3,2,1,0:T(8,128)(2,1)S(1)}, bf16[6,2,32,128]{3,2,1,0:T(8,128)(2,1)S(1)}, u32[]{:S(2)}, u32[]{:S(2)}) collective-permute-start(bf16[6,2,32,128]{3,2,1,0:T(8,128)(2,1)S(1)} %get-tuple-element.43), channel_id=1, source_target_pairs={{0,16},{4,20},{8,24},{12,28},{16,0},{20,4},{24,8},{28,12},{1,17},{... | collective-permute-start | bytes 294920 | tf_op jit(solution)/shard_map/ppermute | solution.py:450
  16.5 6.2 %collective-permute-start.8 = (bf16[6,2,32,128]{3,2,1,0:T(8,128)(2,1)S(1)}, bf16[6,2,32,128]{3,2,1,0:T(8,128)(2,1)S(1)}, u32[]{:S(2)}, u32[]{:S(2)}) collective-permute-start(bf16[6,2,32,128]{3,2,1,0:T(8,128)(2,1)S(1)} %get-tuple-element.44), channel_id=1, source_target_pairs={{0,24},{4,28},{8,16},{12,20},{16,8},{20,12},{24,0},{28,4},{1,25},{... | collective-permute-start | bytes 294920 | tf_op jit(solution)/shard_map/ppermute | solution.py:450
  18.5 4.7 %collective-permute-start.9 = (bf16[6,2,32,128]{3,2,1,0:T(8,128)(2,1)S(1)}, bf16[6,2,32,128]{3,2,1,0:T(8,128)(2,1)S(1)}, u32[]{:S(2)}, u32[]{:S(2)}) collective-permute-start(bf16[6,2,32,128]{3,2,1,0:T(8,128)(2,1)S(1)} %get-tuple-element.41.refs_0_), channel_id=1, source_target_pairs={{0,4},{4,0},{8,12},{12,8},{16,20},{20,16},{24,28},{28,24},{1,5},{5... | collective-permute-start | bytes 294920 | tf_op jit(solution)/shard_map/ppermute | solution.py:446
  20.7 4.2 %collective-permute-start.10 = (bf16[6,2,32,128]{3,2,1,0:T(8,128)(2,1)S(1)}, bf16[6,2,32,128]{3,2,1,0:T(8,128)(2,1)S(1)}, u32[]{:S(2)}, u32[]{:S(2)}) collective-permute-start(bf16[6,2,32,128]{3,2,1,0:T(8,128)(2,1)S(1)} %collective-permute-done.6.refs_1_), channel_id=1, source_target_pairs={{0,4},{4,0},{8,12},{12,8},{16,20},{20,16},{24,28},{28,24},{1,5},{5... | collective-permute-start | bytes 294920 | tf_op jit(solution)/shard_map/ppermute | solution.py:446
  22.7 2.2 %collective-permute-start.11 = (bf16[6,2,32,128]{3,2,1,0:T(8,128)(2,1)S(1)}, bf16[6,2,32,128]{3,2,1,0:T(8,128)(2,1)S(1)}, u32[]{:S(2)}, u32[]{:S(2)}) collective-permute-start(bf16[6,2,32,128]{3,2,1,0:T(8,128)(2,1)S(1)} %collective-permute-done.7.refs_2_), channel_id=1, source_target_pairs={{0,4},{4,0},{8,12},{12,8},{16,20},{20,16},{24,28},{28,24},{1,5},{5... | collective-permute-start | bytes 294920 | tf_op jit(solution)/shard_map/ppermute | solution.py:446
  22.7 2.2 %collective-permute-start.12 = (bf16[6,2,32,128]{3,2,1,0:T(8,128)(2,1)S(1)}, bf16[6,2,32,128]{3,2,1,0:T(8,128)(2,1)S(1)}, u32[]{:S(2)}, u32[]{:S(2)}) collective-permute-start(bf16[6,2,32,128]{3,2,1,0:T(8,128)(2,1)S(1)} %collective-permute-done.8.refs_3_), channel_id=1, source_target_pairs={{0,4},{4,0},{8,12},{12,8},{16,20},{20,16},{24,28},{28,24},{1,5},{5... | collective-permute-start | bytes 294920 | tf_op jit(solution)/shard_map/ppermute | solution.py:446
  23.2 14.3 %collective-permute-start.16 = (bf16[3,2,128,128]{3,2,1,0:T(8,128)(2,1)S(1)}, bf16[3,2,128,128]{3,2,1,0:T(8,128)(2,1)S(1)}, u32[]{:S(2)}, u32[]{:S(2)}) collective-permute-start(bf16[3,2,128,128]{3,2,1,0:T(8,128)(2,1)S(1)} %get-tuple-element.51), channel_id=1, source_target_pairs={{0,1},{1,0},{2,3},{3,2},{4,5},{5,4},{6,7},{7,6},{8,9},{9,8},{10,11... | collective-permute-start | bytes 589832 | tf_op jit(solution)/shard_map/ppermute | solution.py:443
  24.6 12.9 %collective-permute-start.17 = (bf16[3,2,128,128]{3,2,1,0:T(8,128)(2,1)S(1)}, bf16[3,2,128,128]{3,2,1,0:T(8,128)(2,1)S(1)}, u32[]{:S(2)}, u32[]{:S(2)}) collective-permute-start(bf16[3,2,128,128]{3,2,1,0:T(8,128)(2,1)S(1)} %get-tuple-element.52), channel_id=1, source_target_pairs={{0,4},{1,2},{2,1},{3,7},{4,0},{5,6},{6,5},{7,3},{8,12},{9,10},{10,... | collective-permute-start | bytes 589832 | tf_op jit(solution)/shard_map/ppermute | solution.py:443
  25.4 6.5 %collective-permute-start.14 = (bf16[6,2,32,128]{3,2,1,0:T(8,128)(2,1)S(1)}, bf16[6,2,32,128]{3,2,1,0:T(8,128)(2,1)S(1)}, u32[]{:S(2)}, u32[]{:S(2)}) collective-permute-start(bf16[6,2,32,128]{3,2,1,0:T(8,128)(2,1)S(1)} %get-tuple-element.47), channel_id=1, source_target_pairs={{0,16},{4,20},{8,24},{12,28},{16,0},{20,4},{24,8},{28,12},{1,17},{... | collective-permute-start | bytes 294920 | tf_op jit(solution)/shard_map/ppermute | solution.py:450
  26.6 6.6 %collective-permute-start.15 = (bf16[6,2,32,128]{3,2,1,0:T(8,128)(2,1)S(1)}, bf16[6,2,32,128]{3,2,1,0:T(8,128)(2,1)S(1)}, u32[]{:S(2)}, u32[]{:S(2)}) collective-permute-start(bf16[6,2,32,128]{3,2,1,0:T(8,128)(2,1)S(1)} %get-tuple-element.48), channel_id=1, source_target_pairs={{0,24},{4,28},{8,16},{12,20},{16,8},{20,12},{24,0},{28,4},{1,25},{... | collective-permute-start | bytes 294920 | tf_op jit(solution)/shard_map/ppermute | solution.py:450
  28.7 7.4 %collective-permute-start.13 = (bf16[6,2,32,128]{3,2,1,0:T(8,128)(2,1)S(1)}, bf16[6,2,32,128]{3,2,1,0:T(8,128)(2,1)S(1)}, u32[]{:S(2)}, u32[]{:S(2)}) collective-permute-start(bf16[6,2,32,128]{3,2,1,0:T(8,128)(2,1)S(1)} %get-tuple-element.46), channel_id=1, source_target_pairs={{0,8},{4,12},{8,0},{12,4},{16,24},{20,28},{24,16},{28,20},{1,9},{5... | collective-permute-start | bytes 294920 | tf_op jit(solution)/shard_map/ppermute | solution.py:450
  33.2 5.9 %collective-permute-start.19 = (bf16[2,3,2,32,128]{4,3,2,1,0:T(8,128)(2,1)S(1)}, bf16[2,3,2,32,128]{4,3,2,1,0:T(8,128)(2,1)S(1)}, u32[]{:S(2)}, u32[]{:S(2)}) collective-permute-start(bf16[2,3,2,32,128]{4,3,2,1,0:T(8,128)(2,1)S(1)} %get-tuple-element.56), channel_id=1, source_target_pairs={{0,1},{1,0},{2,3},{3,2},{4,5},{5,4},{6,7},{7,6},{8,9},{9,8},{10,11... | collective-permute-start | bytes 294920 | tf_op jit(solution)/shard_map/ppermute | solution.py:443
  36.0 3.1 %collective-permute-start.21 = (bf16[2,3,2,32,128]{4,3,2,1,0:T(8,128)(2,1)S(1)}, bf16[2,3,2,32,128]{4,3,2,1,0:T(8,128)(2,1)S(1)}, u32[]{:S(2)}, u32[]{:S(2)}) collective-permute-start(bf16[2,3,2,32,128]{4,3,2,1,0:T(8,128)(2,1)S(1)} %get-tuple-element.58), channel_id=1, source_target_pairs={{0,4},{1,2},{2,1},{3,7},{4,0},{5,6},{6,5},{7,3},{8,12},{9,10},{10,... | collective-permute-start | bytes 294920 | tf_op jit(solution)/shard_map/ppermute | solution.py:443
  36.1 5.3 %collective-permute-start.18 = (bf16[2,3,2,32,128]{4,3,2,1,0:T(8,128)(2,1)S(1)}, bf16[2,3,2,32,128]{4,3,2,1,0:T(8,128)(2,1)S(1)}, u32[]{:S(2)}, u32[]{:S(2)}) collective-permute-start(bf16[2,3,2,32,128]{4,3,2,1,0:T(8,128)(2,1)S(1)} %get-tuple-element.55), channel_id=1, source_target_pairs={{0,1},{1,0},{2,3},{3,2},{4,5},{5,4},{6,7},{7,6},{8,9},{9,8},{10,11... | collective-permute-start | bytes 294920 | tf_op jit(solution)/shard_map/ppermute | solution.py:443
  37.5 3.8 %collective-permute-start.20 = (bf16[2,3,2,32,128]{4,3,2,1,0:T(8,128)(2,1)S(1)}, bf16[2,3,2,32,128]{4,3,2,1,0:T(8,128)(2,1)S(1)}, u32[]{:S(2)}, u32[]{:S(2)}) collective-permute-start(bf16[2,3,2,32,128]{4,3,2,1,0:T(8,128)(2,1)S(1)} %get-tuple-element.57), channel_id=1, source_target_pairs={{0,4},{1,2},{2,1},{3,7},{4,0},{5,6},{6,5},{7,3},{8,12},{9,10},{10,... | collective-permute-start | bytes 294920 | tf_op jit(solution)/shard_map/ppermute | solution.py:443

commit v6 on v5

--- a/solution.py
+++ b/solution.py
@@ -140,9 +140,13 @@
 
 def weights_kernel(g_ref, first_ref, second_ref, own_ref, near_ref):
     own_weights(Band(g_ref), own_ref)
-    for turn, ref in enumerate((first_ref, second_ref)):
-        for t in range(ref.shape[0]):
-            near_ref[turn, t] = load_square(ref, t).T
+
+    def case(*refs):
+        for side, ref in enumerate(refs):
+            for t in range(ref.shape[0]):
+                near_ref[side, t] = load_square(ref, t).T
+
+    by_place(lambda: case(first_ref, second_ref), lambda: case(second_ref, first_ref))
 
 
 def local_kernel(w_ref, p_ref, sum_ref, edge_ref):
@@ -257,21 +261,20 @@
         order = ((1, 2, 0), (1, 0, 2))
         passed = [
             [times(link, load_square(ref, t)) for t in places]
-            for link, (ref, _), places in zip(links(outer), (below, above), order)
+            for link, ref, places in zip(links(outer), (below, above), order)
         ]
         for side, (gone, (row, past)) in enumerate(zip(missing_sides(), outer.ends())):
             total = None
             for n, t in enumerate(order[side]):
                 lhs = passed[side][n] + (edge_ref[side, n].astype(F32) if n < 2 else 0.0)
-                term = times(lhs.astype(BF16), near_ref[(below, above)[side][1], t])
+                term = times(lhs.astype(BF16), near_ref[side, t])
                 total = term if total is None else total + term
             store(row, past - row + 1, zero_where(gone, total).astype(BF16))
         passed = [[value.astype(BF16) for value in values[:2]] for values in passed]
         inside_terms(outer, sum_ref, own_ref, passed, store)
         copy(*stored[-1]).start()
 
-    first, second = (first_ref, 0), (second_ref, 1)
-    by_turn(lambda: run(second, first), lambda: run(first, second))
+    by_turn(lambda: run(second_ref, first_ref), lambda: run(first_ref, second_ref))
     for i in range(rows):
         for t in range(3):
             copy(i, t).wait()
@@ -281,7 +284,7 @@
     def write(ref, row, past):
         ref[...] = g_ref[row]
 
-    fill(first_ref, second_ref, Band(g_ref), write)
+    fill(first_ref, second_ref, Band(g_ref), write, by_place)
     if out_refs:
         chip, _ = owner()
         size = out_refs[0].shape[-2]
@@ -472,14 +475,14 @@
     row = lax.axis_index("space") * rows + jnp.arange(rows, dtype=jnp.int32)
     band = jnp.arange(bands, dtype=jnp.int32)
     past = (row[:, None] + band[None, :] == 0) | (row[:, None] + band[None, :] == peers * rows + 1)
-    w, p = (zero_where(past[:, :, None, None, None], x) for x in (w, p))
+    p = zero_where(past[:, :, None, None, None], p)
 
     near_w = trade(call(send_kernel, [(5,) + square] * 2, w, p, flops=6 * product), rounds)
     near_g = [(bands,) + square] * 2
     g_first, g_second, *g_pieces = call(split_kernel, near_g + (cut_up if inside else []), g)
     g_own = to_owners(g_pieces or [g.reshape((blocks,) + square)])
     g_all = call(order_kernel, [(count + 1,) + g_own.shape[1:]], g_own, to_partner(g_own))
-    g_weights = call(weights_kernel, [(2, 3, 2 * order, 2 * order)] * 2, g, *trade((g_first, g_second)))
+    g_weights = call(weights_kernel, [(2, 3, 2 * order, 2 * order)] * 2, g, *trade((g_first, g_second), rounds))
 
     sums = [((rows, bands, order, 2 * order), F32), ((2, 2, order, 2 * order), BF16)]
     weights = (2, 3, 2 * order, 2 * order)

time: 42.9 us -> 41.7 us (0.972)
  waiting for transfers between devices: 16.3 us -> 14.7 us
    ppermute x8, waiting for transfers between devices: 2.81 us -> 1.67 us  [trade(): lax.ppermute(x, ('energy', 'space'), pairs)]
    ppermute x9, waiting for transfers between devices: 13.5 us -> 13 us  [to_chips(): lax.ppermute(x, 'energy', [(i, i ^ 2 * s) for i in range(count)])]
    ppermute x8, starting transfers between devices: 8.95 us -> 9.38 us  [trade(): lax.ppermute(x, ('energy', 'space'), pairs)]
  transfers between devices with their start and end apart: 22 -> 22, of which waited for: 9 -> 8; matrix products, arithmetic and copies ran while one was open for 0% -> 0% of each run, Pallas kernels for 7% -> 7%
where the time goes in v6:
time: 41.7 us; the launch traced here: 41.5 us
  starting transfers between devices  20.6 us (49%)
  waiting for transfers between devices  14.7 us (35%)
  Pallas kernels  4.82 us (12%)
  other arithmetic  1.22 us (3%)
    ppermute x9, waiting for transfers between devices, to_chips(): lax.ppermute(x, 'energy', [(i, i ^ 2 * s) for i in range(count)])  13 us
    ppermute x9, starting transfers between devices, to_chips(): lax.ppermute(x, 'energy', [(i, i ^ 2 * s) for i in range(count)])  10.7 us
    ppermute x8, starting transfers between devices, trade(): lax.ppermute(x, ('energy', 'space'), pairs)  9.38 us
    pallas_call x12, Pallas kernels, call(): pl.pallas_call(kernel, out_shape=outs[0] if single else outs, in_specs=[V...  4.82 us
    ppermute x8, waiting for transfers between devices, trade(): lax.ppermute(x, ('energy', 'space'), pairs)  1.67 us
    select_n x1, other arithmetic, zero_where(): return jnp.where(condition, jnp.zeros_like(value), value)  1.14 us
  transfers between devices with their start and end apart: 22, of which 8 were waited for; matrix products, arithmetic and copies ran while one was open for 0% of the time, Pallas kernels for 7%

profile of v6, /device:TPU:0, one launch (start us, length us, event | category | flops | bytes accessed | tf_op | source)
XLA Modules:
  0.0 41.5 jit_solution(1907897258706049603)
XLA Ops:
  0.0 0.1 compare_or_fusion
  0.1 1.1 %bitcast_select_fusion.p_ref = bf16[2,3,2,128,128]{4,3,2,1,0:T(8,128)(2,1)S(1)} fusion(bf16[1,2,3,2,128,128]{5,4,3,2,1,0:T(8,128)(2,1)} %param.4, pred[2,3]{1,0:T(4,128)(4,1)S(1)} %compare_or_fusion), kind=kLoop, calls=%fused_computation | loop fusion | flops 196608 | bytes 786438 | tf_op jit(solution)/shard_map/jit(_where)/select_n | solution.py:35
  1.3 0.4 %shard_map.41 = (bf16[5,2,128,128]{3,2,1,0:T(8,128)(2,1)S(1)}, bf16[5,2,128,128]{3,2,1,0:T(8,128)(2,1)S(1)}) custom-call(bf16[2,3,2,128,128]{4,3,2,1,0:T(8,128)(2,1)S(1)} %bitcast.9, bf16[2,3,2,128,128]{4,3,2,1,0:T(8,128)(2,1)S(1)} %bitcast_select_fusion.p_ref), custom_call_target="tpu_custom_call" | custom-call | flops 100663296 | bytes 1441792 | tf_op jit(solution)/shard_map/pallas_call | solution.py:400
  1.7 3.1 %collective-permute-start.4 = (bf16[5,2,128,128]{3,2,1,0:T(8,128)(2,1)S(1)}, bf16[5,2,128,128]{3,2,1,0:T(8,128)(2,1)S(1)}, u32[]{:S(2)}, u32[]{:S(2)}) collective-permute-start(bf16[5,2,128,128]{3,2,1,0:T(8,128)(2,1)S(1)} %get-tuple-element.39), channel_id=1, source_target_pairs={{0,1},{1,2},{2,3},{3,7},{4,0},{5,4},{6,5},{7,6},{8,9},{9,10},{10,1... | collective-permute-start | bytes 983048 | tf_op jit(solution)/shard_map/ppermute | solution.py:446
  4.8 1.6 %collective-permute-start = (bf16[6,2,32,128]{3,2,1,0:T(8,128)(2,1)S(1)}, bf16[6,2,32,128]{3,2,1,0:T(8,128)(2,1)S(1)}, u32[]{:S(2)}, u32[]{:S(2)}) collective-permute-start(bf16[6,2,32,128]{3,2,1,0:T(8,128)(2,1)S(1)} %get-tuple-element.33), channel_id=1, source_target_pairs={{0,8},{4,12},{8,0},{12,4},{16,24},{20,28},{24,16},{28,20},{1,9},{5... | collective-permute-start | bytes 294920 | tf_op jit(solution)/shard_map/ppermute | solution.py:453
  6.4 1.5 %collective-permute-start.1 = (bf16[6,2,32,128]{3,2,1,0:T(8,128)(2,1)S(1)}, bf16[6,2,32,128]{3,2,1,0:T(8,128)(2,1)S(1)}, u32[]{:S(2)}, u32[]{:S(2)}) collective-permute-start(bf16[6,2,32,128]{3,2,1,0:T(8,128)(2,1)S(1)} %get-tuple-element.34), channel_id=1, source_target_pairs={{0,16},{4,20},{8,24},{12,28},{16,0},{20,4},{24,8},{28,12},{1,17},{... | collective-permute-start | bytes 294920 | tf_op jit(solution)/shard_map/ppermute | solution.py:453
  7.9 0.5 %collective-permute-start.2 = (bf16[6,2,32,128]{3,2,1,0:T(8,128)(2,1)S(1)}, bf16[6,2,32,128]{3,2,1,0:T(8,128)(2,1)S(1)}, u32[]{:S(2)}, u32[]{:S(2)}) collective-permute-start(bf16[6,2,32,128]{3,2,1,0:T(8,128)(2,1)S(1)} %get-tuple-element.35), channel_id=1, source_target_pairs={{0,24},{4,28},{8,16},{12,20},{16,8},{20,12},{24,0},{28,4},{1,25},{... | collective-permute-start | bytes 294920 | tf_op jit(solution)/shard_map/ppermute | solution.py:453
  8.4 1.2 %collective-permute-done.refs_1_ = bf16[6,2,32,128]{3,2,1,0:T(8,128)(2,1)S(1)} collective-permute-done((bf16[6,2,32,128]{3,2,1,0:T(8,128)(2,1)S(1)}, bf16[6,2,32,128]{3,2,1,0:T(8,128)(2,1)S(1)}, u32[]{:S(2)}, u32[]{:S(2)}) %collective-permute-start) | collective-permute-done | bytes 98336 | tf_op jit(solution)/shard_map/ppermute | solution.py:453
  9.5 2.5 %collective-permute-done.1.refs_2_ = bf16[6,2,32,128]{3,2,1,0:T(8,128)(2,1)S(1)} collective-permute-done((bf16[6,2,32,128]{3,2,1,0:T(8,128)(2,1)S(1)}, bf16[6,2,32,128]{3,2,1,0:T(8,128)(2,1)S(1)}, u32[]{:S(2)}, u32[]{:S(2)}) %collective-permute-start.1) | collective-permute-done | bytes 98336 | tf_op jit(solution)/shard_map/ppermute | solution.py:453
  12.1 1.4 %collective-permute-done.2.refs_3_ = bf16[6,2,32,128]{3,2,1,0:T(8,128)(2,1)S(1)} collective-permute-done((bf16[6,2,32,128]{3,2,1,0:T(8,128)(2,1)S(1)}, bf16[6,2,32,128]{3,2,1,0:T(8,128)(2,1)S(1)}, u32[]{:S(2)}, u32[]{:S(2)}) %collective-permute-start.2) | collective-permute-done | bytes 98336 | tf_op jit(solution)/shard_map/ppermute | solution.py:453
  13.5 0.1 collective-permute-start.3
  13.5 0.6 %shard_map.40 = (f32[2,3,128,256]{3,2,1,0:T(8,128)S(1)}, bf16[2,2,128,256]{3,2,1,0:T(8,128)(2,1)S(1)}, bf16[2,3,256,256]{3,2,1,0:T(8,128)(2,1)S(1)}) custom-call(bf16[2,3,2,128,128]{4,3,2,1,0:T(8,128)(2,1)S(1)} %bitcast.10, bf16[2,3,2,128,128]{4,3,2,1,0:T(8,128)(2,1)S(1)} %bitcast_select_fusion.p_ref), custom_call_target="tpu_custom_call" | custom-call | flops 402653184 | bytes 2228224 | tf_op jit(solution)/shard_map/pallas_call | solution.py:400
  14.2 0.6 %shard_map.42 = (bf16[6,2,32,128]{3,2,1,0:T(8,128)(2,1)S(1)}, bf16[6,2,32,128]{3,2,1,0:T(8,128)(2,1)S(1)}, bf16[6,2,32,128]{3,2,1,0:T(8,128)(2,1)S(1)}, bf16[6,2,32,128]{3,2,1,0:T(8,128)(2,1)S(1)}) custom-call(bf16[2,3,2,128,128]{4,3,2,1,0:T(8,128)(2,1)S(1)} %bitcast.11, f32[2,3,128,256]{3,2,1,0:T(8,128)S(1)} %get-tuple-element.36.sum_ref, ...), custom_call_target="tpu_custom_call" | custom-call | flops 268435456 | bytes 2883584 | tf_op jit(solution)/shard_map/pallas_call | solution.py:400
  14.8 0.7 %collective-permute-start.6 = (bf16[6,2,32,128]{3,2,1,0:T(8,128)(2,1)S(1)}, bf16[6,2,32,128]{3,2,1,0:T(8,128)(2,1)S(1)}, u32[]{:S(2)}, u32[]{:S(2)}) collective-permute-start(bf16[6,2,32,128]{3,2,1,0:T(8,128)(2,1)S(1)} %get-tuple-element.42), channel_id=1, source_target_pairs={{0,8},{4,12},{8,0},{12,4},{16,24},{20,28},{24,16},{28,20},{1,9},{5... | collective-permute-start | bytes 294920 | tf_op jit(solution)/shard_map/ppermute | solution.py:453
  15.6 0.8 %collective-permute-start.7 = (bf16[6,2,32,128]{3,2,1,0:T(8,128)(2,1)S(1)}, bf16[6,2,32,128]{3,2,1,0:T(8,128)(2,1)S(1)}, u32[]{:S(2)}, u32[]{:S(2)}) collective-permute-start(bf16[6,2,32,128]{3,2,1,0:T(8,128)(2,1)S(1)} %get-tuple-element.43), channel_id=1, source_target_pairs={{0,16},{4,20},{8,24},{12,28},{16,0},{20,4},{24,8},{28,12},{1,17},{... | collective-permute-start | bytes 294920 | tf_op jit(solution)/shard_map/ppermute | solution.py:453
  16.4 2.0 %collective-permute-start.8 = (bf16[6,2,32,128]{3,2,1,0:T(8,128)(2,1)S(1)}, bf16[6,2,32,128]{3,2,1,0:T(8,128)(2,1)S(1)}, u32[]{:S(2)}, u32[]{:S(2)}) collective-permute-start(bf16[6,2,32,128]{3,2,1,0:T(8,128)(2,1)S(1)} %get-tuple-element.44), channel_id=1, source_target_pairs={{0,24},{4,28},{8,16},{12,20},{16,8},{20,12},{24,0},{28,4},{1,25},{... | collective-permute-start | bytes 294920 | tf_op jit(solution)/shard_map/ppermute | solution.py:453
  18.4 2.2 %collective-permute-done.6.refs_1_ = bf16[6,2,32,128]{3,2,1,0:T(8,128)(2,1)S(1)} collective-permute-done((bf16[6,2,32,128]{3,2,1,0:T(8,128)(2,1)S(1)}, bf16[6,2,32,128]{3,2,1,0:T(8,128)(2,1)S(1)}, u32[]{:S(2)}, u32[]{:S(2)}) %collective-permute-start.6) | collective-permute-done | bytes 98336 | tf_op jit(solution)/shard_map/ppermute | solution.py:453
  20.6 2.0 %collective-permute-done.7.refs_2_ = bf16[6,2,32,128]{3,2,1,0:T(8,128)(2,1)S(1)} collective-permute-done((bf16[6,2,32,128]{3,2,1,0:T(8,128)(2,1)S(1)}, bf16[6,2,32,128]{3,2,1,0:T(8,128)(2,1)S(1)}, u32[]{:S(2)}, u32[]{:S(2)}) %collective-permute-start.7) | collective-permute-done | bytes 98336 | tf_op jit(solution)/shard_map/ppermute | solution.py:453
  22.6 0.5 %collective-permute-start.12 = (bf16[6,2,32,128]{3,2,1,0:T(8,128)(2,1)S(1)}, bf16[6,2,32,128]{3,2,1,0:T(8,128)(2,1)S(1)}, u32[]{:S(2)}, u32[]{:S(2)}) collective-permute-start(bf16[6,2,32,128]{3,2,1,0:T(8,128)(2,1)S(1)} %collective-permute-done.8.refs_3_), channel_id=1, source_target_pairs={{0,4},{4,0},{8,12},{12,8},{16,20},{20,16},{24,28},{28,24},{1,5},{5... | collective-permute-start | bytes 294920 | tf_op jit(solution)/shard_map/ppermute | solution.py:449
  23.1 1.9 %collective-permute-start.16 = (bf16[3,2,128,128]{3,2,1,0:T(8,128)(2,1)S(1)}, bf16[3,2,128,128]{3,2,1,0:T(8,128)(2,1)S(1)}, u32[]{:S(2)}, u32[]{:S(2)}) collective-permute-start(bf16[3,2,128,128]{3,2,1,0:T(8,128)(2,1)S(1)} %get-tuple-element.51), channel_id=1, source_target_pairs={{0,1},{1,2},{2,3},{3,7},{4,0},{5,4},{6,5},{7,6},{8,9},{9,10},{10,1... | collective-permute-start | bytes 589832 | tf_op jit(solution)/shard_map/ppermute | solution.py:446
  25.1 0.5 %shard_map.43 = (bf16[6,2,32,128]{3,2,1,0:T(8,128)(2,1)S(1)}, bf16[6,2,32,128]{3,2,1,0:T(8,128)(2,1)S(1)}, bf16[6,2,32,128]{3,2,1,0:T(8,128)(2,1)S(1)}, bf16[6,2,32,128]{3,2,1,0:T(8,128)(2,1)S(1)}) custom-call(bf16[9,6,2,32,128]{4,3,2,1,0:T(8,128)(2,1)S(1)} %shard_map.39.g_ref, bf16[6,2,32,128]{3,2,1,0:T(8,128)(2,1)S(1)} %get-tuple-element.41.refs_0_, ...), custom_call_target="tpu_custom_call" | custom-call | bytes 2064384 | tf_op jit(solution)/shard_map/pallas_call | solution.py:400
  25.6 0.8 %collective-permute-start.14 = (bf16[6,2,32,128]{3,2,1,0:T(8,128)(2,1)S(1)}, bf16[6,2,32,128]{3,2,1,0:T(8,128)(2,1)S(1)}, u32[]{:S(2)}, u32[]{:S(2)}) collective-permute-start(bf16[6,2,32,128]{3,2,1,0:T(8,128)(2,1)S(1)} %get-tuple-element.47), channel_id=1, source_target_pairs={{0,16},{4,20},{8,24},{12,28},{16,0},{20,4},{24,8},{28,12},{1,17},{... | collective-permute-start | bytes 294920 | tf_op jit(solution)/shard_map/ppermute | solution.py:453
  26.4 2.3 %collective-permute-start.15 = (bf16[6,2,32,128]{3,2,1,0:T(8,128)(2,1)S(1)}, bf16[6,2,32,128]{3,2,1,0:T(8,128)(2,1)S(1)}, u32[]{:S(2)}, u32[]{:S(2)}) collective-permute-start(bf16[6,2,32,128]{3,2,1,0:T(8,128)(2,1)S(1)} %get-tuple-element.48), channel_id=1, source_target_pairs={{0,24},{4,28},{8,16},{12,20},{16,8},{20,12},{24,0},{28,4},{1,25},{... | collective-permute-start | bytes 294920 | tf_op jit(solution)/shard_map/ppermute | solution.py:453
  28.6 0.5 %collective-permute-start.13 = (bf16[6,2,32,128]{3,2,1,0:T(8,128)(2,1)S(1)}, bf16[6,2,32,128]{3,2,1,0:T(8,128)(2,1)S(1)}, u32[]{:S(2)}, u32[]{:S(2)}) collective-permute-start(bf16[6,2,32,128]{3,2,1,0:T(8,128)(2,1)S(1)} %get-tuple-element.46), channel_id=1, source_target_pairs={{0,8},{4,12},{8,0},{12,4},{16,24},{20,28},{24,16},{28,20},{1,9},{5... | collective-permute-start | bytes 294920 | tf_op jit(solution)/shard_map/ppermute | solution.py:453
  29.1 2.7 %collective-permute-done.14.refs_3_.refs_0_ = bf16[6,2,32,128]{3,2,1,0:T(8,128)(2,1)S(1)} collective-permute-done((bf16[6,2,32,128]{3,2,1,0:T(8,128)(2,1)S(1)}, bf16[6,2,32,128]{3,2,1,0:T(8,128)(2,1)S(1)}, u32[]{:S(2)}, u32[]{:S(2)}) %collective-permute-start.14) | collective-permute-done | bytes 98336 | tf_op jit(solution)/shard_map/ppermute | solution.py:453
  31.8 1.1 %collective-permute-done.15.refs_4_.refs_1_ = bf16[6,2,32,128]{3,2,1,0:T(8,128)(2,1)S(1)} collective-permute-done((bf16[6,2,32,128]{3,2,1,0:T(8,128)(2,1)S(1)}, bf16[6,2,32,128]{3,2,1,0:T(8,128)(2,1)S(1)}, u32[]{:S(2)}, u32[]{:S(2)}) %collective-permute-start.15) | collective-permute-done | bytes 98336 | tf_op jit(solution)/shard_map/ppermute | solution.py:453
  32.9 1.9 %collective-permute-start.19 = (bf16[2,3,2,32,128]{4,3,2,1,0:T(8,128)(2,1)S(1)}, bf16[2,3,2,32,128]{4,3,2,1,0:T(8,128)(2,1)S(1)}, u32[]{:S(2)}, u32[]{:S(2)}) collective-permute-start(bf16[2,3,2,32,128]{4,3,2,1,0:T(8,128)(2,1)S(1)} %get-tuple-element.56), channel_id=1, source_target_pairs={{0,1},{1,0},{2,3},{3,2},{4,5},{5,4},{6,7},{7,6},{8,9},{9,8},{10,11... | collective-permute-start | bytes 294920 | tf_op jit(solution)/shard_map/ppermute | solution.py:446
  34.9 2.5 %collective-permute-start.18 = (bf16[2,3,2,32,128]{4,3,2,1,0:T(8,128)(2,1)S(1)}, bf16[2,3,2,32,128]{4,3,2,1,0:T(8,128)(2,1)S(1)}, u32[]{:S(2)}, u32[]{:S(2)}) collective-permute-start(bf16[2,3,2,32,128]{4,3,2,1,0:T(8,128)(2,1)S(1)} %get-tuple-element.55), channel_id=1, source_target_pairs={{0,1},{1,0},{2,3},{3,2},{4,5},{5,4},{6,7},{7,6},{8,9},{9,8},{10,11... | collective-permute-start | bytes 294920 | tf_op jit(solution)/shard_map/ppermute | solution.py:446
  37.4 0.4 shard_map.45
  37.8 0.7 %shard_map.44 = (f32[2,3,128,256]{3,2,1,0:T(8,128)S(1)}, bf16[2,2,128,256]{3,2,1,0:T(8,128)(2,1)S(1)}) custom-call(bf16[2,3,2,128,128]{4,3,2,1,0:T(8,128)(2,1)S(1)} %bitcast.7, bf16[6,2,32,128]{3,2,1,0:T(8,128)(2,1)S(1)} %get-tuple-element.45.refs_1_.refs_0_, bf16[6,2,32,128]{3,2,1,0:T(8,128)(2,1)S(1)} %collective-permute-done.13.refs_2_.refs_1_, ...), custom_call_target="tpu_custom_call" | custom-call | flops 402653184 | bytes 1441792 | tf_op jit(solution)/shard_map/pallas_call | solution.py:400
  38.5 1.7 %collective-permute-done.18.rest_0_ = bf16[2,3,2,32,128]{4,3,2,1,0:T(8,128)(2,1)S(1)} collective-permute-done((bf16[2,3,2,32,128]{4,3,2,1,0:T(8,128)(2,1)S(1)}, bf16[2,3,2,32,128]{4,3,2,1,0:T(8,128)(2,1)S(1)}, u32[]{:S(2)}, u32[]{:S(2)}) %collective-permute-start.18) | collective-permute-done | bytes 98336 | tf_op jit(solution)/shard_map/ppermute | solution.py:446
  40.1 1.4 %shard_map.48 = bf16[2,3,2,128,128]{4,3,2,1,0:T(8,128)(2,1)} custom-call(bf16[2,3,2,128,128]{4,3,2,1,0:T(8,128)(2,1)S(1)} %bitcast.8, f32[2,3,128,256]{3,2,1,0:T(8,128)S(1)} %get-tuple-element.49.sum_ref, bf16[2,2,128,256]{3,2,1,0:T(8,128)(2,1)S(1)} %get-tuple-element.50.edge_ref, bf16[2,3,256,256]{3,2,1,0:T(8,128)(2,1)S(1)} %get-tuple-element.53.own_ref, ...), custom_call_target="tpu_custom_call" | custom-call | flops 301989888 | bytes 3407872 | tf_op jit(solution)/shard_map/pallas_call | solution.py:400
  (31 shorter events, 0.3 us)
Async XLA Ops:
  0.1 1.2 %copy-start.1 = (bf16[1,2,3,2,128,128]{5,4,3,2,1,0:T(8,128)(2,1)S(1)}, bf16[1,2,3,2,128,128]{5,4,3,2,1,0:T(8,128)(2,1)}, u32[]{:S(2)}) copy-start(bf16[1,2,3,2,128,128]{5,4,3,2,1,0:T(8,128)(2,1)} %param.3) | copy-start | bytes 1179652
  1.2 3.5 %copy-start = (bf16[1,2,3,2,128,128]{5,4,3,2,1,0:T(8,128)(2,1)S(1)}, bf16[1,2,3,2,128,128]{5,4,3,2,1,0:T(8,128)(2,1)}, u32[]{:S(2)}) copy-start(bf16[1,2,3,2,128,128]{5,4,3,2,1,0:T(8,128)(2,1)} %param.5) | copy-start | bytes 1179652
  1.7 12.5 %collective-permute-start.4 = (bf16[5,2,128,128]{3,2,1,0:T(8,128)(2,1)S(1)}, bf16[5,2,128,128]{3,2,1,0:T(8,128)(2,1)S(1)}, u32[]{:S(2)}, u32[]{:S(2)}) collective-permute-start(bf16[5,2,128,128]{3,2,1,0:T(8,128)(2,1)S(1)} %get-tuple-element.39), channel_id=1, source_target_pairs={{0,1},{1,2},{2,3},{3,7},{4,0},{5,4},{6,5},{7,6},{8,9},{9,10},{10,1... | collective-permute-start | bytes 983048 | tf_op jit(solution)/shard_map/ppermute | solution.py:446
  4.8 9.4 %collective-permute-start.5 = (bf16[5,2,128,128]{3,2,1,0:T(8,128)(2,1)S(1)}, bf16[5,2,128,128]{3,2,1,0:T(8,128)(2,1)S(1)}, u32[]{:S(2)}, u32[]{:S(2)}) collective-permute-start(bf16[5,2,128,128]{3,2,1,0:T(8,128)(2,1)S(1)} %get-tuple-element.40), channel_id=1, source_target_pairs={{0,4},{1,0},{2,1},{3,2},{4,5},{5,6},{6,7},{7,3},{8,12},{9,8},{10,9... | collective-permute-start | bytes 983048 | tf_op jit(solution)/shard_map/ppermute | solution.py:446
  4.8 4.7 %collective-permute-start = (bf16[6,2,32,128]{3,2,1,0:T(8,128)(2,1)S(1)}, bf16[6,2,32,128]{3,2,1,0:T(8,128)(2,1)S(1)}, u32[]{:S(2)}, u32[]{:S(2)}) collective-permute-start(bf16[6,2,32,128]{3,2,1,0:T(8,128)(2,1)S(1)} %get-tuple-element.33), channel_id=1, source_target_pairs={{0,8},{4,12},{8,0},{12,4},{16,24},{20,28},{24,16},{28,20},{1,9},{5... | collective-permute-start | bytes 294920 | tf_op jit(solution)/shard_map/ppermute | solution.py:453
  6.4 5.7 %collective-permute-start.1 = (bf16[6,2,32,128]{3,2,1,0:T(8,128)(2,1)S(1)}, bf16[6,2,32,128]{3,2,1,0:T(8,128)(2,1)S(1)}, u32[]{:S(2)}, u32[]{:S(2)}) collective-permute-start(bf16[6,2,32,128]{3,2,1,0:T(8,128)(2,1)S(1)} %get-tuple-element.34), channel_id=1, source_target_pairs={{0,16},{4,20},{8,24},{12,28},{16,0},{20,4},{24,8},{28,12},{1,17},{... | collective-permute-start | bytes 294920 | tf_op jit(solution)/shard_map/ppermute | solution.py:453
  7.9 5.5 %collective-permute-start.2 = (bf16[6,2,32,128]{3,2,1,0:T(8,128)(2,1)S(1)}, bf16[6,2,32,128]{3,2,1,0:T(8,128)(2,1)S(1)}, u32[]{:S(2)}, u32[]{:S(2)}) collective-permute-start(bf16[6,2,32,128]{3,2,1,0:T(8,128)(2,1)S(1)} %get-tuple-element.35), channel_id=1, source_target_pairs={{0,24},{4,28},{8,16},{12,20},{16,8},{20,12},{24,0},{28,4},{1,25},{... | collective-permute-start | bytes 294920 | tf_op jit(solution)/shard_map/ppermute | solution.py:453
  13.5 11.5 %collective-permute-start.3 = (bf16[4,6,2,32,128]{4,3,2,1,0:T(8,128)(2,1)S(1)}, bf16[4,6,2,32,128]{4,3,2,1,0:T(8,128)(2,1)S(1)}, u32[]{:S(2)}, u32[]{:S(2)}) collective-permute-start(bf16[4,6,2,32,128]{4,3,2,1,0:T(8,128)(2,1)S(1)} %shard_map.38.own_ref), channel_id=1, source_target_pairs={{0,4},{4,0},{8,12},{12,8},{16,20},{20,16},{24,28},{28,24},{1,5},{5... | collective-permute-start | bytes 1179656 | tf_op jit(solution)/shard_map/ppermute | solution.py:449
  14.8 5.7 %collective-permute-start.6 = (bf16[6,2,32,128]{3,2,1,0:T(8,128)(2,1)S(1)}, bf16[6,2,32,128]{3,2,1,0:T(8,128)(2,1)S(1)}, u32[]{:S(2)}, u32[]{:S(2)}) collective-permute-start(bf16[6,2,32,128]{3,2,1,0:T(8,128)(2,1)S(1)} %get-tuple-element.42), channel_id=1, source_target_pairs={{0,8},{4,12},{8,0},{12,4},{16,24},{20,28},{24,16},{28,20},{1,9},{5... | collective-permute-start | bytes 294920 | tf_op jit(solution)/shard_map/ppermute | solution.py:453
  15.6 7.0 %collective-permute-start.7 = (bf16[6,2,32,128]{3,2,1,0:T(8,128)(2,1)S(1)}, bf16[6,2,32,128]{3,2,1,0:T(8,128)(2,1)S(1)}, u32[]{:S(2)}, u32[]{:S(2)}) collective-permute-start(bf16[6,2,32,128]{3,2,1,0:T(8,128)(2,1)S(1)} %get-tuple-element.43), channel_id=1, source_target_pairs={{0,16},{4,20},{8,24},{12,28},{16,0},{20,4},{24,8},{28,12},{1,17},{... | collective-permute-start | bytes 294920 | tf_op jit(solution)/shard_map/ppermute | solution.py:453
  16.4 6.2 %collective-permute-start.8 = (bf16[6,2,32,128]{3,2,1,0:T(8,128)(2,1)S(1)}, bf16[6,2,32,128]{3,2,1,0:T(8,128)(2,1)S(1)}, u32[]{:S(2)}, u32[]{:S(2)}) collective-permute-start(bf16[6,2,32,128]{3,2,1,0:T(8,128)(2,1)S(1)} %get-tuple-element.44), channel_id=1, source_target_pairs={{0,24},{4,28},{8,16},{12,20},{16,8},{20,12},{24,0},{28,4},{1,25},{... | collective-permute-start | bytes 294920 | tf_op jit(solution)/shard_map/ppermute | solution.py:453
  18.4 4.7 %collective-permute-start.9 = (bf16[6,2,32,128]{3,2,1,0:T(8,128)(2,1)S(1)}, bf16[6,2,32,128]{3,2,1,0:T(8,128)(2,1)S(1)}, u32[]{:S(2)}, u32[]{:S(2)}) collective-permute-start(bf16[6,2,32,128]{3,2,1,0:T(8,128)(2,1)S(1)} %get-tuple-element.41.refs_0_), channel_id=1, source_target_pairs={{0,4},{4,0},{8,12},{12,8},{16,20},{20,16},{24,28},{28,24},{1,5},{5... | collective-permute-start | bytes 294920 | tf_op jit(solution)/shard_map/ppermute | solution.py:449
  20.6 4.5 %collective-permute-start.10 = (bf16[6,2,32,128]{3,2,1,0:T(8,128)(2,1)S(1)}, bf16[6,2,32,128]{3,2,1,0:T(8,128)(2,1)S(1)}, u32[]{:S(2)}, u32[]{:S(2)}) collective-permute-start(bf16[6,2,32,128]{3,2,1,0:T(8,128)(2,1)S(1)} %collective-permute-done.6.refs_1_), channel_id=1, source_target_pairs={{0,4},{4,0},{8,12},{12,8},{16,20},{20,16},{24,28},{28,24},{1,5},{5... | collective-permute-start | bytes 294920 | tf_op jit(solution)/shard_map/ppermute | solution.py:449
  22.6 2.5 %collective-permute-start.11 = (bf16[6,2,32,128]{3,2,1,0:T(8,128)(2,1)S(1)}, bf16[6,2,32,128]{3,2,1,0:T(8,128)(2,1)S(1)}, u32[]{:S(2)}, u32[]{:S(2)}) collective-permute-start(bf16[6,2,32,128]{3,2,1,0:T(8,128)(2,1)S(1)} %collective-permute-done.7.refs_2_), channel_id=1, source_target_pairs={{0,4},{4,0},{8,12},{12,8},{16,20},{20,16},{24,28},{28,24},{1,5},{5... | collective-permute-start | bytes 294920 | tf_op jit(solution)/shard_map/ppermute | solution.py:449
  22.6 2.5 %collective-permute-start.12 = (bf16[6,2,32,128]{3,2,1,0:T(8,128)(2,1)S(1)}, bf16[6,2,32,128]{3,2,1,0:T(8,128)(2,1)S(1)}, u32[]{:S(2)}, u32[]{:S(2)}) collective-permute-start(bf16[6,2,32,128]{3,2,1,0:T(8,128)(2,1)S(1)} %collective-permute-done.8.refs_3_), channel_id=1, source_target_pairs={{0,4},{4,0},{8,12},{12,8},{16,20},{20,16},{24,28},{28,24},{1,5},{5... | collective-permute-start | bytes 294920 | tf_op jit(solution)/shard_map/ppermute | solution.py:449
  23.1 14.3 %collective-permute-start.16 = (bf16[3,2,128,128]{3,2,1,0:T(8,128)(2,1)S(1)}, bf16[3,2,128,128]{3,2,1,0:T(8,128)(2,1)S(1)}, u32[]{:S(2)}, u32[]{:S(2)}) collective-permute-start(bf16[3,2,128,128]{3,2,1,0:T(8,128)(2,1)S(1)} %get-tuple-element.51), channel_id=1, source_target_pairs={{0,1},{1,2},{2,3},{3,7},{4,0},{5,4},{6,5},{7,6},{8,9},{9,10},{10,1... | collective-permute-start | bytes 589832 | tf_op jit(solution)/shard_map/ppermute | solution.py:446
  25.0 12.4 %collective-permute-start.17 = (bf16[3,2,128,128]{3,2,1,0:T(8,128)(2,1)S(1)}, bf16[3,2,128,128]{3,2,1,0:T(8,128)(2,1)S(1)}, u32[]{:S(2)}, u32[]{:S(2)}) collective-permute-start(bf16[3,2,128,128]{3,2,1,0:T(8,128)(2,1)S(1)} %get-tuple-element.52), channel_id=1, source_target_pairs={{0,4},{1,0},{2,1},{3,2},{4,5},{5,6},{6,7},{7,3},{8,12},{9,8},{10,9... | collective-permute-start | bytes 589832 | tf_op jit(solution)/shard_map/ppermute | solution.py:446
  25.6 6.2 %collective-permute-start.14 = (bf16[6,2,32,128]{3,2,1,0:T(8,128)(2,1)S(1)}, bf16[6,2,32,128]{3,2,1,0:T(8,128)(2,1)S(1)}, u32[]{:S(2)}, u32[]{:S(2)}) collective-permute-start(bf16[6,2,32,128]{3,2,1,0:T(8,128)(2,1)S(1)} %get-tuple-element.47), channel_id=1, source_target_pairs={{0,16},{4,20},{8,24},{12,28},{16,0},{20,4},{24,8},{28,12},{1,17},{... | collective-permute-start | bytes 294920 | tf_op jit(solution)/shard_map/ppermute | solution.py:453
  26.4 6.6 %collective-permute-start.15 = (bf16[6,2,32,128]{3,2,1,0:T(8,128)(2,1)S(1)}, bf16[6,2,32,128]{3,2,1,0:T(8,128)(2,1)S(1)}, u32[]{:S(2)}, u32[]{:S(2)}) collective-permute-start(bf16[6,2,32,128]{3,2,1,0:T(8,128)(2,1)S(1)} %get-tuple-element.48), channel_id=1, source_target_pairs={{0,24},{4,28},{8,16},{12,20},{16,8},{20,12},{24,0},{28,4},{1,25},{... | collective-permute-start | bytes 294920 | tf_op jit(solution)/shard_map/ppermute | solution.py:453
  28.6 6.2 %collective-permute-start.13 = (bf16[6,2,32,128]{3,2,1,0:T(8,128)(2,1)S(1)}, bf16[6,2,32,128]{3,2,1,0:T(8,128)(2,1)S(1)}, u32[]{:S(2)}, u32[]{:S(2)}) collective-permute-start(bf16[6,2,32,128]{3,2,1,0:T(8,128)(2,1)S(1)} %get-tuple-element.46), channel_id=1, source_target_pairs={{0,8},{4,12},{8,0},{12,4},{16,24},{20,28},{24,16},{28,20},{1,9},{5... | collective-permute-start | bytes 294920 | tf_op jit(solution)/shard_map/ppermute | solution.py:453
  32.9 5.5 %collective-permute-start.19 = (bf16[2,3,2,32,128]{4,3,2,1,0:T(8,128)(2,1)S(1)}, bf16[2,3,2,32,128]{4,3,2,1,0:T(8,128)(2,1)S(1)}, u32[]{:S(2)}, u32[]{:S(2)}) collective-permute-start(bf16[2,3,2,32,128]{4,3,2,1,0:T(8,128)(2,1)S(1)} %get-tuple-element.56), channel_id=1, source_target_pairs={{0,1},{1,0},{2,3},{3,2},{4,5},{5,4},{6,7},{7,6},{8,9},{9,8},{10,11... | collective-permute-start | bytes 294920 | tf_op jit(solution)/shard_map/ppermute | solution.py:446
  34.8 3.6 %collective-permute-start.21 = (bf16[2,3,2,32,128]{4,3,2,1,0:T(8,128)(2,1)S(1)}, bf16[2,3,2,32,128]{4,3,2,1,0:T(8,128)(2,1)S(1)}, u32[]{:S(2)}, u32[]{:S(2)}) collective-permute-start(bf16[2,3,2,32,128]{4,3,2,1,0:T(8,128)(2,1)S(1)} %get-tuple-element.58), channel_id=1, source_target_pairs={{0,4},{1,2},{2,1},{3,7},{4,0},{5,6},{6,5},{7,3},{8,12},{9,10},{10,... | collective-permute-start | bytes 294920 | tf_op jit(solution)/shard_map/ppermute | solution.py:446
  34.9 5.3 %collective-permute-start.18 = (bf16[2,3,2,32,128]{4,3,2,1,0:T(8,128)(2,1)S(1)}, bf16[2,3,2,32,128]{4,3,2,1,0:T(8,128)(2,1)S(1)}, u32[]{:S(2)}, u32[]{:S(2)}) collective-permute-start(bf16[2,3,2,32,128]{4,3,2,1,0:T(8,128)(2,1)S(1)} %get-tuple-element.55), channel_id=1, source_target_pairs={{0,1},{1,0},{2,3},{3,2},{4,5},{5,4},{6,7},{7,6},{8,9},{9,8},{10,11... | collective-permute-start | bytes 294920 | tf_op jit(solution)/shard_map/ppermute | solution.py:446
  37.4 2.8 %collective-permute-start.20 = (bf16[2,3,2,32,128]{4,3,2,1,0:T(8,128)(2,1)S(1)}, bf16[2,3,2,32,128]{4,3,2,1,0:T(8,128)(2,1)S(1)}, u32[]{:S(2)}, u32[]{:S(2)}) collective-permute-start(bf16[2,3,2,32,128]{4,3,2,1,0:T(8,128)(2,1)S(1)} %get-tuple-element.57), channel_id=1, source_target_pairs={{0,4},{1,2},{2,1},{3,7},{4,0},{5,6},{6,5},{7,3},{8,12},{9,10},{10,... | collective-permute-start | bytes 294920 | tf_op jit(solution)/shard_map/ppermute | solution.py:446
